TPU v7x, 32 devices: a whole 2x2x4 slice. The times are simulated.
32 devices in a mesh: dp: 4 (over y, core), seq: 8 (over z, x).
Axes of the slice: x: 2, y: 2, z: 4, core: 2. Of those that a mesh axis runs over, the one named last changes fastest.
Arguments:
- hidden_in: bfloat16 [4, 1024, 2048], P('dp', 'seq'), may hold values from -6 to 6
- in_weight: bfloat16 [2048, 6160], P(('dp', 'seq')), may hold values from -0.125 to 0.125
- out_weight: bfloat16 [2048, 2048], P(('dp', 'seq')), may hold values from -0.125 to 0.125
- decay_up: bfloat16 [16, 1024], P(None, ('dp', 'seq')), may hold values from -1.5 to 1.5
- decay_bias: bfloat16 [1024], P(('dp', 'seq')), may hold values from 0.5 to 6
- mixer_gain: bfloat16 [2048], P(('dp', 'seq')), may hold values from 0.099609375 to 1.8984375
- head_gain: bfloat16 [512], P(('dp', 'seq')), may hold values from 0.099609375 to 1.8984375
- ffn_in: bfloat16 [2048, 11264], P(('dp', 'seq')), may hold values from -0.125 to 0.125
- ffn_out: bfloat16 [5632, 2048], P(('dp', 'seq')), may hold values from -0.078125 to 0.078125
- ffn_gain: bfloat16 [2048], P(('dp', 'seq')), may hold values from 0.099609375 to 1.8984375
- out_grad: bfloat16 [4, 1024, 2048], P('dp', 'seq'), may hold values from -6 to 6
- seg_ids: int32 [4, 1024], P('dp', 'seq'), may hold values from 0 to 7, never falling along the last dimension, each value on 1 to 512 neighbouring positions
- valid_mask: int32 [4, 1024], P('dp', 'seq'), may hold values from 0 to 1
Outputs:
- block_out: bfloat16 [4, 1024, 2048], P('dp', 'seq')
- input_grad: float32 [4, 1024, 2048], P('dp', 'seq')
- inproj_grad: float32 [2048, 6160], P(('dp', 'seq'))
- outproj_grad: float32 [2048, 2048], P(('dp', 'seq'))
- decayup_grad: float32 [16, 1024], P(None, ('dp', 'seq'))
- decaybias_grad: float32 [1024], P(('dp', 'seq'))
- mixgain_grad: float32 [2048], P(('dp', 'seq'))
- headgain_grad: float32 [512], P(('dp', 'seq'))
- ffnin_grad: float32 [2048, 11264], P(('dp', 'seq'))
- ffnout_grad: float32 [5632, 2048], P(('dp', 'seq'))
- ffngain_grad: float32 [2048], P(('dp', 'seq'))
- root_means: float32 [3], replicated
Inputs may be any that keep to these rules, and one draw needn't show every extreme that they name: `seg_ids`: a sequence's segment numbers never fall; a segment holds at most 512 tokens, and one segment of each sequence exactly that many.
All inputs are finite; a program needn't handle non-finite values.
Results may differ from a plain program's by a relative error of at most 0.012.
Values may be sent and summed in bfloat16 or wider, within the bound.
No kernel may reach another device: no remote copies, remote signals or barrier semaphores. Data moves between devices by JAX's collectives and lax.ppermute only.
A program may use at most 384 MiB of HBM per device.

v0:
```python
import jax
import jax.numpy as jnp
from jax import lax
from jax.sharding import PartitionSpec as P

HEADS = 4
KEY = 256
VAL = 512
FF = 5632
SPAN = 64


HIGHEST = lax.Precision.HIGHEST
epsilon = 1e-05
head_floor = 1.0


def entering_2(value, axis, join, neutral):
    count, mine = (lax.axis_size(axis), lax.axis_index(axis))
    pieces = jax.tree.map(lambda part: lax.all_gather(part, axis), value)
    subtotal = jax.tree.map(
        lambda part, zero: jnp.full_like(part, 0) + jnp.asarray(zero, part.dtype), value, neutral
    )

    def lap(position, subtotal):
        longer = join(subtotal, jax.tree.map(lambda part: part[position], pieces))
        return jax.tree.map(lambda new, old: jnp.where(position < mine, new, old), longer, subtotal)

    return lax.fori_loop(0, count - 1, lap, subtotal)


def entering_3(value, axis, join, neutral):
    count = lax.axis_size(axis)
    place = lax.axis_index(axis)
    ahead = count - 1 - place
    gathered = jax.tree.map(
        lambda a, kind: lax.all_gather(a.astype(kind), axis), value, (jnp.bfloat16, jnp.bfloat16)
    )
    state = jax.tree.map(lambda a, e: jnp.zeros_like(a) + jnp.asarray(e, a.dtype), value, neutral)

    def one(lap, state):
        source = count - 1 - lap
        return join(
            state,
            jax.tree.map(
                lambda a, own: lax.dynamic_index_in_dim(a, source, 0, False).astype(own.dtype),
                gathered,
                value,
            ),
        )

    return lax.fori_loop(0, ahead, one, state)


def rms_norm(values, gain_in):
    return values * lax.rsqrt(jnp.mean(values * values, axis=-1, keepdims=True) + epsilon) * gain_in


def head_norm(values, gain_in):
    return (
        values * lax.rsqrt(jnp.mean(values * values, axis=-1, keepdims=True) + head_floor) * gain_in
    )


def span_masks(segments, seg_before):
    span_len = segments.shape[-1]
    causal = jnp.arange(span_len)[:, None] >= jnp.arange(span_len)[None, :]
    same_seg = (segments[:, :, None] == segments[:, None, :]) & causal[None]
    enter_mask = segments == seg_before[:, None]
    carry_end = segments == segments[:, -1:]
    keep_all = segments[:, -1] == seg_before
    return (
        same_seg.astype(jnp.float32),
        enter_mask.astype(jnp.float32),
        carry_end.astype(jnp.float32),
        keep_all.astype(jnp.float32),
    )


def span_local(query_in, key_in, value_in, log_in, same_seg, carry_end, keep_all):
    span_len = log_in.shape[1]
    triangle = (jnp.arange(span_len)[:, None] >= jnp.arange(span_len)[None, :]).astype(jnp.float32)
    summed = jnp.einsum("ij,njhk->nihk", triangle, log_in, precision=HIGHEST)
    last_sum = summed[:, -1]
    q_decay = query_in * jnp.exp(summed)
    k_decay = key_in * jnp.exp(-summed)
    k_final = key_in * jnp.exp(last_sum[:, None] - summed) * carry_end[:, :, None, None]
    scores = jnp.einsum("nihk,njhk->nhij", q_decay, k_decay, precision=HIGHEST) * same_seg[:, None]
    inner_out = jnp.einsum("nhij,njhv->nihv", scores, value_in, precision=HIGHEST)
    delta_state = jnp.einsum("nihk,nihv->nhkv", k_final, value_in, precision=HIGHEST)
    decay_rows = keep_all[:, None, None] * jnp.exp(last_sum)
    return (q_decay, inner_out, delta_state, decay_rows)


def product(left, right):
    return jnp.dot(left, right, preferred_element_type=jnp.float32)


def product_tn(left, right):
    return lax.dot_general(
        left, right, (((0,), (0,)), ((), ())), preferred_element_type=jnp.float32
    )


def product_nt(left, right):
    return lax.dot_general(
        left, right, (((1,), (1,)), ((), ())), preferred_element_type=jnp.float32
    )


def join_states(earlier, later):
    decay_e, state_e, first_e, last_e = earlier
    decay_l, state_l, first_l, last_l = later
    joined = ((last_e == first_l) | (last_e < 0.0) | (first_l < 0.0)).astype(jnp.float32)
    factor = decay_l * joined[..., None, None]
    return (
        factor * decay_e,
        factor[..., None] * state_e + state_l,
        jnp.where(first_e >= 0.0, first_e, first_l),
        jnp.where(last_l >= 0.0, last_l, last_e),
    )


def join_grads(earlier, later):
    decay_e, grad_e = earlier
    decay_l, grad_l = later
    return (decay_l * decay_e, decay_l[..., None] * grad_e + grad_l)


def local(
    hidden_in,
    in_weight,
    out_weight,
    decay_up,
    decay_bias,
    mixer_gain,
    head_gain,
    ffn_in,
    ffn_out,
    ffn_gain,
    out_grad,
    seg_ids,
    valid_mask,
):
    seq_count, tok_count, model_width = hidden_in.shape
    blocks = tok_count // SPAN
    rows_all = seq_count * tok_count
    groups = seq_count * blocks
    qk_cols = HEADS * KEY
    v_cols = HEADS * VAL
    inputs = hidden_in.reshape(rows_all, model_width).astype(jnp.float32)
    in_full, out_full, up_full, bias_full, gain_first, head_full, ffn_gain_full = (
        lax.all_gather(in_weight, ("dp", "seq"), axis=0, tiled=True),
        lax.all_gather(out_weight, ("dp", "seq"), axis=0, tiled=True),
        lax.all_gather(decay_up, ("dp", "seq"), axis=1, tiled=True),
        lax.all_gather(decay_bias, ("dp", "seq"), axis=0, tiled=True),
        lax.all_gather(mixer_gain, ("dp", "seq"), axis=0, tiled=True),
        lax.all_gather(head_gain, ("dp", "seq"), axis=0, tiled=True),
        lax.all_gather(ffn_gain, ("dp", "seq"), axis=0, tiled=True),
    )
    gain_one = gain_first.astype(jnp.float32)
    head_scale = head_full.astype(jnp.float32)
    normed = rms_norm(inputs, gain_one).astype(jnp.bfloat16)
    projected = product(normed, in_full)
    queries = projected[:, :qk_cols].astype(jnp.bfloat16)
    key_rows = projected[:, qk_cols : 2 * qk_cols].astype(jnp.bfloat16)
    value_rows = projected[:, 2 * qk_cols : 2 * qk_cols + v_cols].astype(jnp.bfloat16)
    out_gate = projected[:, 2 * qk_cols + v_cols : 2 * qk_cols + 2 * v_cols]
    low_rank = projected[:, 2 * qk_cols + 2 * v_cols :].astype(jnp.bfloat16)
    raw_gate = product(low_rank, up_full) + bias_full.astype(jnp.float32)
    log_decay = jax.nn.log_sigmoid(raw_gate) / 16.0
    live_rows = valid_mask.reshape(rows_all, 1).astype(jnp.float32)
    grouped_k = (groups, SPAN, HEADS, KEY)
    scaled_q = (queries.astype(jnp.float32) * KEY ** (-0.5)).reshape(grouped_k)
    masked_k = (key_rows.astype(jnp.float32) * live_rows).reshape(grouped_k)
    values_grouped = value_rows.astype(jnp.float32).reshape(groups, SPAN, HEADS, VAL)
    logs_grouped = log_decay.reshape(grouped_k)
    seg_blocks = seg_ids.reshape(seq_count, blocks, SPAN)
    before = jnp.concatenate([seg_blocks[:, :1, 0], seg_blocks[:, :-1, -1]], axis=1).reshape(groups)
    same_seg, enter_mask, carry_end, keep_all = span_masks(seg_blocks.reshape(groups, SPAN), before)

    def local_part(query_in, key_in, value_in, log_in):
        return span_local(query_in, key_in, value_in, log_in, same_seg, carry_end, keep_all)

    q_decay, inner_out, delta_state, decay_rows = local_part(
        scaled_q, masked_k, values_grouped, logs_grouped
    )
    delta_blocks = delta_state.reshape(seq_count, blocks, HEADS, KEY, VAL)
    decay_blocks = decay_rows.reshape(seq_count, blocks, HEADS, KEY)
    zero_state = jnp.zeros((seq_count, HEADS, KEY, VAL), jnp.float32)
    unit_decay = jnp.ones((seq_count, HEADS, KEY), jnp.float32)
    partial_value = [zero_state]
    through = [unit_decay]
    for block_id in range(blocks):
        partial_value.append(
            decay_blocks[:, block_id, ..., None] * partial_value[-1] + delta_blocks[:, block_id]
        )
        through.append(decay_blocks[:, block_id] * through[-1])
    first_seg = seg_ids[:, 0]
    last_seg = seg_ids[:, -1]
    identity = (
        unit_decay,
        zero_state,
        jnp.full((seq_count,), -1.0, jnp.float32),
        jnp.full((seq_count,), -1.0, jnp.float32),
    )
    scanned = entering_2(
        (
            through[-1],
            partial_value[-1],
            first_seg.astype(jnp.float32),
            last_seg.astype(jnp.float32),
        ),
        "seq",
        join_states,
        identity,
    )
    incoming = scanned[1]
    link_in = ((scanned[3] == first_seg.astype(jnp.float32)) & (scanned[3] >= 0.0)).astype(
        jnp.float32
    )
    entering = link_in[:, None, None, None] * incoming
    prior_states = jnp.stack(
        [
            partial_value[block_id] + through[block_id][..., None] * entering
            for block_id in range(blocks)
        ],
        axis=1,
    ).reshape(groups, HEADS, KEY, VAL)
    outer_out = (
        jnp.einsum("nihk,nhkv->nihv", q_decay, prior_states, precision=HIGHEST)
        * enter_mask[:, :, None, None]
    )
    mixed_out = (inner_out + outer_out).reshape(rows_all, HEADS, VAL)
    gate_heads = out_gate.reshape(rows_all, HEADS, VAL)

    def head_gate(mixed_in, gate_in, gain_in):
        return (head_norm(mixed_in, gain_in) * gate_in * jax.nn.sigmoid(gate_in)).reshape(
            rows_all, v_cols
        )

    gated_out = head_gate(mixed_out, gate_heads, head_scale).astype(jnp.bfloat16)
    mix_out = product(gated_out, out_full)
    middle = inputs + mix_out
    gain_two = ffn_gain_full.astype(jnp.float32)
    normed_two = rms_norm(middle, gain_two).astype(jnp.bfloat16)
    grad_y = out_grad.reshape(rows_all, model_width)
    weight_first, weight_second = (
        lax.all_gather(ffn_in, ("dp", "seq"), axis=0, tiled=True),
        lax.all_gather(ffn_out, ("dp", "seq"), axis=0, tiled=True),
    )
    gate_up = product(normed_two, weight_first)
    gate_half = gate_up[:, :FF]
    up_half = gate_up[:, FF:]
    hidden = (jax.nn.silu(gate_half) * up_half).astype(jnp.bfloat16)
    ffn_result = product(hidden, weight_second)
    result = middle + ffn_result
    totals = lax.psum(
        (
            jnp.sum(live_rows * result * result),
            jnp.sum(live_rows * mix_out * mix_out),
            jnp.sum(live_rows * ffn_result * ffn_result),
            jnp.sum(live_rows),
        ),
        ("dp", "seq"),
    )
    live_count = jnp.maximum(totals[3], 1.0) * model_width
    root_means = jnp.sqrt(jnp.stack([totals[0], totals[1], totals[2]]) / live_count)
    upstream = out_grad.reshape(rows_all, model_width).astype(jnp.float32)
    grad_ffn_out = product_tn(hidden, grad_y)
    grad_hidden = product_nt(grad_y, weight_second)
    gate_sig = jax.nn.sigmoid(gate_half)
    grad_gate = grad_hidden * up_half * gate_sig * (1.0 + gate_half * (1.0 - gate_sig))
    grad_up = grad_hidden * gate_half * gate_sig
    grad_gu = jnp.concatenate([grad_gate, grad_up], axis=1).astype(jnp.bfloat16)
    grad_ffn_in = product_tn(normed_two, grad_gu)
    normed_grad_terms = product_nt(grad_gu, weight_first)
    ffnin_grad, ffnout_grad = (
        lax.psum_scatter(grad_ffn_in, ("dp", "seq"), scatter_dimension=0, tiled=True),
        lax.psum_scatter(grad_ffn_out, ("dp", "seq"), scatter_dimension=0, tiled=True),
    )
    _, norm_pull = jax.vjp(rms_norm, middle, gain_two)
    grad_mid_part, grad_gain_two = norm_pull(normed_grad_terms)
    grad_middle = upstream + grad_mid_part
    grad_mix = grad_middle.astype(jnp.bfloat16)
    grad_out_w = product_tn(gated_out, grad_mix)
    grad_gated = product_nt(grad_mix, out_full)
    _, gate_pull = jax.vjp(head_gate, mixed_out, gate_heads, head_scale)
    grad_mixed, grad_gate_heads, grad_head = gate_pull(grad_gated)
    grad_o = grad_mixed.reshape(groups, SPAN, HEADS, VAL)
    outer_q = (
        jnp.einsum("nihv,nhkv->nihk", grad_o, prior_states, precision=HIGHEST)
        * enter_mask[:, :, None, None]
    )
    local_grad = jnp.einsum(
        "nihk,nihv->nhkv", q_decay, grad_o * enter_mask[:, :, None, None], precision=HIGHEST
    ).reshape(seq_count, blocks, HEADS, KEY, VAL)
    back_states = [zero_state]
    after_decay = [unit_decay]
    for block_id in reversed(range(blocks)):
        back_states.insert(
            0, local_grad[:, block_id] + decay_blocks[:, block_id, ..., None] * back_states[0]
        )
        after_decay.insert(0, decay_blocks[:, block_id] * after_decay[0])
    flowed = entering_3(
        (link_in[:, None, None] * through[-1], link_in[:, None, None, None] * back_states[0]),
        "seq",
        join_grads,
        (unit_decay, zero_state),
    )
    outgoing = flowed[1]
    next_grad = jnp.stack(
        [
            back_states[block_id + 1] + after_decay[block_id + 1][..., None] * outgoing
            for block_id in range(blocks)
        ],
        axis=1,
    ).reshape(groups, HEADS, KEY, VAL)
    grad_decay = jnp.sum(prior_states * next_grad, axis=-1)
    _, span_pull = jax.vjp(local_part, scaled_q, masked_k, values_grouped, logs_grouped)
    grad_q, grad_k, grad_v, grad_logs = span_pull((outer_q, grad_o, next_grad, grad_decay))
    grad_queries = grad_q.reshape(rows_all, qk_cols) * KEY ** (-0.5)
    grad_keys = grad_k.reshape(rows_all, qk_cols) * live_rows
    grad_values = grad_v.reshape(rows_all, v_cols)
    grad_raw = grad_logs.reshape(rows_all, qk_cols) * jax.nn.sigmoid(-raw_gate) / 16.0
    grad_bias = jnp.sum(grad_raw, axis=0)
    grad_up_w = lax.dot_general(
        low_rank.astype(jnp.float32), grad_raw, (((0,), (0,)), ((), ())), precision=HIGHEST
    )
    grad_rank = lax.dot_general(
        grad_raw, up_full.astype(jnp.float32), (((1,), (1,)), ((), ())), precision=HIGHEST
    )
    grad_proj = jnp.concatenate(
        [
            grad_queries,
            grad_keys,
            grad_values,
            grad_gate_heads.reshape(rows_all, v_cols),
            grad_rank,
        ],
        axis=1,
    ).astype(jnp.bfloat16)
    grad_in_w = product_tn(normed, grad_proj)
    grad_normed = product_nt(grad_proj, in_full)
    _, first_pull = jax.vjp(rms_norm, inputs, gain_one)
    grad_input_part, grad_gain_one = first_pull(grad_normed)
    input_grad = grad_middle + grad_input_part
    mixer_grads = (
        lax.psum_scatter(grad_in_w, ("dp", "seq"), scatter_dimension=0, tiled=True),
        lax.psum_scatter(grad_out_w, ("dp", "seq"), scatter_dimension=0, tiled=True),
        lax.psum_scatter(grad_up_w, ("dp", "seq"), scatter_dimension=1, tiled=True),
        lax.psum_scatter(grad_bias, ("dp", "seq"), scatter_dimension=0, tiled=True),
        lax.psum_scatter(grad_gain_one, ("dp", "seq"), scatter_dimension=0, tiled=True),
        lax.psum_scatter(grad_head, ("dp", "seq"), scatter_dimension=0, tiled=True),
        lax.psum_scatter(grad_gain_two, ("dp", "seq"), scatter_dimension=0, tiled=True),
    )
    block_out = result.astype(jnp.bfloat16).reshape(seq_count, tok_count, model_width)
    return (
        block_out,
        input_grad.reshape(seq_count, tok_count, model_width),
        mixer_grads[0],
        mixer_grads[1],
        mixer_grads[2],
        mixer_grads[3],
        mixer_grads[4],
        mixer_grads[5],
        ffnin_grad,
        ffnout_grad,
        mixer_grads[6],
        root_means,
    )


def solution(mesh):
    placed = (
        P("dp", "seq", None),
        P(("dp", "seq"), None),
        P(("dp", "seq"), None),
        P(None, ("dp", "seq")),
        P(("dp", "seq")),
        P(("dp", "seq")),
        P(("dp", "seq")),
        P(("dp", "seq"), None),
        P(("dp", "seq"), None),
        P(("dp", "seq")),
        P("dp", "seq", None),
        P("dp", "seq"),
        P("dp", "seq"),
    )
    return jax.shard_map(
        local,
        mesh=mesh,
        in_specs=placed,
        out_specs=(
            P("dp", "seq", None),
            P("dp", "seq", None),
            P(("dp", "seq"), None),
            P(("dp", "seq"), None),
            P(None, ("dp", "seq")),
            P(("dp", "seq")),
            P(("dp", "seq")),
            P(("dp", "seq")),
            P(("dp", "seq"), None),
            P(("dp", "seq"), None),
            P(("dp", "seq")),
            P(),
        ),
        check_vma=False,
    )
```

profile of v0, /device:TPU:8, one launch (start us, length us, event | category | flops | bytes accessed | tf_op | source)
XLA Modules:
  0.0 5624.9 jit_solution(14394421057465528074)
XLA Ops:
  11.4 42.0 all-reduce.13
  53.4 65.8 %all-gather = bf16[32,32,16]{1,2,0:T(8,128)(2,1)S(1)} all-gather(bf16[1,32,16]{1,2,0:T(8,128)(2,1)} %bitcast.273), channel_id=1, replica_groups=mesh['dp'=4,'seq'=8] {'dp','seq'}, dimensions={0}, use_global_device_ids=true | all-gather | bytes 33792 | tf_op jit(solution)/shard_map/all_gather | solution.py:155
  126.8 44.2 all-gather.8.cloned.1.call-done
  171.0 16.8 fusion.100
  210.4 18.4 all-reduce.12
  229.7 31.0 all_gather.55
  262.4 168.2 %all-gather.10.cloned.1.call-done = f32[8,1,4,256,512]{4,3,2,1,0:T(8,128)} async-done(((f32[1,1,4,256,512]{4,3,2,1,0:T(8,128)}), f32[8,1,4,256,512]{4,3,2,1,0:T(8,128)}) %all-gather.10.cloned.1.call-update) | async-done | bytes 16777232 | tf_op jit(solution)/shard_map/all_gather | solution.py:20
  430.6 42.7 while.31
  487.2 23.9 all-gather.12.cloned.1.call-done
  511.1 5.6 multiply_reduce_fusion.5
  516.8 249.1 %all-gather.14.cloned.1.call-done = bf16[2048,11264]{1,0:T(8,128)(2,1)} async-done(((bf16[64,11264]{1,0:T(8,128)(2,1)}), bf16[2048,11264]{1,0:T(8,128)(2,1)}) %all-gather.14.cloned.1.call-update) | async-done | bytes 46137360 | tf_op jit(solution)/shard_map/all_gather | solution.py:249
  765.9 20.5 fusion.95
  786.4 125.2 %all-gather.16.cloned.1.call-done = bf16[5632,2048]{1,0:T(8,128)(2,1)} async-done(((bf16[176,2048]{1,0:T(8,128)(2,1)}), bf16[5632,2048]{1,0:T(8,128)(2,1)}) %all-gather.16.cloned.1.call-update) | async-done | bytes 23068688 | tf_op jit(solution)/shard_map/all_gather | solution.py:250
  911.6 15.0 multiply_convert_fusion.1
  926.6 21.4 fusion.12
  948.1 13.6 fusion.34
  979.2 4.4 copy.113
  994.8 27.0 all_gather.64
  1025.7 5.0 fusion.22
  1030.7 87.4 %all-gather.18.cloned.1.call-done = bf16[8,1,4,256,512]{4,3,2,1,0:T(8,128)(2,1)} async-done(((bf16[1,1,4,256,512]{4,3,2,1,0:T(8,128)(2,1)}), bf16[8,1,4,256,512]{4,3,2,1,0:T(8,128)(2,1)}) %all-gather.18.cloned.1.call-update) | async-done | bytes 8388624 | tf_op jit(solution)/shard_map/all_gather | solution.py:37
  1118.4 9.4 while.30
  1146.1 9.6 fusion.69
  1155.8 19.1 fusion.50
  1177.6 4.9 fusion.19
  1193.4 20.0 fusion.76
  1213.7 33.7 fusion.11
  1248.6 14.9 fusion.27
  1263.5 52.7 all-reduce.11
  1325.5 314.9 %reduce-scatter.10.cloned.1.call-done = f32[64,2048]{1,0:T(8,128)} async-done(((f32[2048,2048]{1,0:T(8,128)}), f32[64,2048]{1,0:T(8,128)}) %reduce-scatter.10.cloned.1.call-update) | async-done | bytes 524304 | tf_op jit(solution)/shard_map/reduce_scatter | solution.py:350
  1640.3 970.4 %reduce-scatter.14.cloned.1.call-done = f32[176,2048]{1,0:T(8,128)} async-done(((f32[5632,2048]{1,0:T(8,128)}), f32[176,2048]{1,0:T(8,128)}) %reduce-scatter.14.cloned.1.call-update) | async-done | bytes 1441808 | tf_op jit(solution)/shard_map/reduce_scatter | solution.py:280
  2610.7 1079.2 %reduce-scatter.8.cloned.1.call-done = f32[64,6160]{1,0:T(8,128)} async-done(((f32[2048,6160]{1,0:T(8,128)}), f32[64,6160]{1,0:T(8,128)}) %reduce-scatter.8.cloned.1.call-update) | async-done | bytes 1576976 | tf_op jit(solution)/shard_map/reduce_scatter | solution.py:349
  3689.9 1928.2 %reduce-scatter.12.cloned.1.call-done = f32[64,11264]{1,0:T(8,128)} async-done(((f32[2048,11264]{1,0:T(8,128)}), f32[64,11264]{1,0:T(8,128)}) %reduce-scatter.12.cloned.1.call-update) | async-done | bytes 2883600 | tf_op jit(solution)/shard_map/reduce_scatter | solution.py:279
  (313 shorter events, 156.7 us)
Async XLA Ops:
  7.2 163.9 %copy-start.15 = (bf16[1,128,2048]{2,1,0:T(8,128)(2,1)S(1)}, bf16[1,128,2048]{2,1,0:T(8,128)(2,1)}, u32[]{:S(2)}) copy-start(bf16[1,128,2048]{2,1,0:T(8,128)(2,1)} %param.17) | copy-start | bytes 1572868
  7.2 163.8 %all-gather.8.cloned.1.call-start = ((), (), s32[]{:S(2)}) async-start(), calls=%async_computation.5 | async-start | bytes 26492928 | tf_op jit(solution)/shard_map/all_gather | solution.py:153
  7.9 422.7 %all-gather.10.cloned.1.call-start = ((), (), s32[]{:S(2)}) async-start(), calls=%async_computation.6 | async-start | bytes 18874368 | tf_op jit(solution)/shard_map/all_gather | solution.py:20
  53.4 134.4 %copy-start.47 = (f32[2048]{0:T(1024)}, f32[2048]{0:T(1024)S(1)}, u32[]{:S(2)}) copy-start(f32[2048]{0:T(1024)S(1)} %convert_element_type.165) | copy-start | bytes 24580
  119.4 69.3 %copy-start.49 = (bf16[1024,16]{0,1:T(8,128)(2,1)}, bf16[1024,16]{0,1:T(8,128)(2,1)S(1)}, u32[]{:S(2)}) copy-start(bf16[1024,16]{0,1:T(8,128)(2,1)S(1)} %reshape.472) | copy-start | bytes 98308
  124.1 63.7 %copy-start.56 = (f32[128]{0:T(128)}, f32[128]{0:T(128)S(1)}, u32[]{:S(2)}) copy-start(f32[128]{0:T(128)S(1)} %fusion.86) | copy-start | bytes 1540
  124.8 66.9 %copy-start.62 = (f32[128]{0:T(128)}, f32[128]{0:T(128)S(1)}, u32[]{:S(2)}) copy-start(f32[128]{0:T(128)S(1)} %convert_bitcast_fusion.1) | copy-start | bytes 1540
  126.2 72.1 %copy-start.60 = (f32[2]{0:T(128)}, f32[2]{0:T(128)S(1)}, u32[]{:S(2)}) copy-start(f32[2]{0:T(128)S(1)} %get-tuple-element.321) | copy-start | bytes 28
  126.8 71.6 %copy-start.54 = (f32[2,64]{1,0:T(2,128)}, f32[2,64]{1,0:T(2,128)S(1)}, u32[]{:S(2)}) copy-start(f32[2,64]{1,0:T(2,128)S(1)} %get-tuple-element.343) | copy-start | bytes 1540
  195.9 829.2 %copy-start.11 = (f32[2,64,4,256]{3,1,2,0:T(8,128)}, f32[2,64,4,256]{3,1,2,0:T(8,128)S(1)}, u32[]{:S(2)}) copy-start(f32[2,64,4,256]{3,1,2,0:T(8,128)S(1)} %get-tuple-element.353) | copy-start | bytes 1572868
  197.1 827.9 %copy-start.13 = (f32[2,64,4,256]{3,1,2,0:T(8,128)}, f32[2,64,4,256]{3,1,2,0:T(8,128)S(1)}, u32[]{:S(2)}) copy-start(f32[2,64,4,256]{3,1,2,0:T(8,128)S(1)} %copy.102) | copy-start | bytes 1572868
  204.2 307.0 %all-gather.12.cloned.1.call-start = ((), (), s32[]{:S(2)}) async-start(), calls=%async_computation.7 | async-start | bytes 8650752 | tf_op jit(solution)/shard_map/all_gather | solution.py:154
  204.9 561.0 %all-gather.14.cloned.1.call-start = ((), (), s32[]{:S(2)}) async-start(), calls=%async_computation.8 | async-start | bytes 47579136 | tf_op jit(solution)/shard_map/all_gather | solution.py:249
  205.5 706.1 %all-gather.16.cloned.1.call-start = ((), (), s32[]{:S(2)}) async-start(), calls=%async_computation.9 | async-start | bytes 23789568 | tf_op jit(solution)/shard_map/all_gather | solution.py:250
  206.1 912.0 %all-gather.18.cloned.1.call-start = ((), (), s32[]{:S(2)}) async-start(), calls=%async_computation.10 | async-start | bytes 9437184 | tf_op jit(solution)/shard_map/all_gather | solution.py:37
  485.1 26.0 copy-start.16
  487.2 29.6 copy-start.33
  765.9 145.7 %copy-start.41 = (bf16[1,128,2048]{2,1,0:T(8,128)(2,1)S(1)}, bf16[1,128,2048]{2,1,0:T(8,128)(2,1)}, u32[]{:S(2)}) copy-start(bf16[1,128,2048]{2,1,0:T(8,128)(2,1)} %param.27) | copy-start | bytes 1572868
  926.6 21.4 copy-start.63
  948.0 15.2 slice-start
  948.1 15.2 slice-start.1
  987.6 38.0 copy-start.10
  994.7 329.4 %reduce-scatter.16.cloned.1.call-start = ((), (), s32[]{:S(2)}) async-start(), calls=%async_computation.15 | async-start | bytes 540672
  994.8 28.8 copy-start.25
  1146.0 494.3 %reduce-scatter.10.cloned.1.call-start = ((), (), s32[]{:S(2)}) async-start(), calls=%async_computation.12 | async-start | bytes 17301504 | tf_op jit(solution)/shard_map/reduce_scatter | solution.py:350
  1155.7 1455.0 %reduce-scatter.14.cloned.1.call-start = ((), (), s32[]{:S(2)}) async-start(), calls=%async_computation.14 | async-start | bytes 47579136 | tf_op jit(solution)/shard_map/reduce_scatter | solution.py:280
  1174.9 2515.0 %reduce-scatter.8.cloned.1.call-start = ((), (), s32[]{:S(2)}) async-start(), calls=%async_computation.11 | async-start | bytes 52985856 | tf_op jit(solution)/shard_map/reduce_scatter | solution.py:349
  1213.4 4404.7 %reduce-scatter.12.cloned.1.call-start = ((), (), s32[]{:S(2)}) async-start(), calls=%async_computation.13 | async-start | bytes 95158272 | tf_op jit(solution)/shard_map/reduce_scatter | solution.py:279
  1248.6 14.9 copy-start.51
  1248.6 14.9 copy-start.59
  1248.6 72.9 %copy-start.66 = (f32[128]{0:T(128)S(1)}, f32[128]{0:T(128)}, u32[]{:S(2)}) copy-start(f32[128]{0:T(128)} %copy-done.65) | copy-start | bytes 1540
  1248.6 72.9 %copy-start.19 = (f32[128,2048]{1,0:T(8,128)S(1)}, f32[128,2048]{1,0:T(8,128)}, u32[]{:S(2)}) copy-start(f32[128,2048]{1,0:T(8,128)} %copy-done.18) | copy-start | bytes 3145732
  (50 other events, 155.9 us)
Sparse Core Ops, SparseCore 0:
  10.9 160.1 all-gather.7
  204.3 226.2 all-gather.9
  433.6 77.5 all-gather.11
  513.8 252.0 all-gather.13
  768.7 142.8 all-gather.15
  994.8 123.2 all-gather.17
  1146.2 134.0 reduce-scatter.15
  1283.3 357.0 reduce-scatter.9
  1643.3 967.3 reduce-scatter.13
  2613.6 1076.2 reduce-scatter.7
  3692.9 1925.1 reduce-scatter.11
where the time goes:
time: 5630 us; the launch traced here: 5620 us
  waiting for transfers between devices  4990 us (89%)
  blocking collectives  237 us (4%)
  matrix products  232 us (4%)
  local copies, waits for them, and re-layouts  69.7 us (1%)
    reduce_scatter x1, waiting for transfers between devices, local(): lax.psum_scatter(grad_ffn_in, ('dp', 'seq'), scatter_dimension=0, tiled=T...  1930 us
    reduce_scatter x1, waiting for transfers between devices, local(): lax.psum_scatter(grad_in_w, ('dp', 'seq'), scatter_dimension=0, tiled=True)  1080 us
    reduce_scatter x1, waiting for transfers between devices, local(): lax.psum_scatter(grad_ffn_out, ('dp', 'seq'), scatter_dimension=0, tiled=...  970 us
    reduce_scatter x1, waiting for transfers between devices, local(): lax.psum_scatter(grad_out_w, ('dp', 'seq'), scatter_dimension=0, tiled=True)  315 us
    all_gather x1, waiting for transfers between devices, local(): lax.all_gather(ffn_in, ('dp', 'seq'), axis=0, tiled=True)  249 us
    all_gather x1, waiting for transfers between devices, entering_2(): pieces = jax.tree.map(lambda part: lax.all_gather(part, axis), value)  168 us
    all_gather x1, waiting for transfers between devices, local(): lax.all_gather(ffn_out, ('dp', 'seq'), axis=0, tiled=True)  125 us
    unnamed x3, blocking collectives  113 us
  transfers between devices with their start and end apart: 11, of which 10 were waited for; matrix products, arithmetic and copies ran while one was open for 4% of the time, Pallas kernels for 0%

commit v1 on v0

v1 whole, which is shorter than its diff:
```python
import jax
import jax.numpy as jnp
from jax import lax
from jax.experimental import pallas as pl
from jax.experimental.pallas import tpu as pltpu
from jax.sharding import Mesh, PartitionSpec as P

HEADS = 4
KEY = 256
VAL = 512
SPAN = 64
RANK = 16
EPS = 1e-05
FLOOR = 1.0
QSCALE = KEY**-0.5

AXES = ("y", "c", "h", "p", "q")
COPIES = ("y", "c", "h")

bf16 = jnp.bfloat16
f32 = jnp.float32


def after(value, *deps):
    return lax.optimization_barrier((value, deps))[0]


def swap(value, axis):
    return lax.ppermute(value, axis, [(0, 1), (1, 0)])


def across(value, mask):
    return lax.ppermute(value, ("p", "q"), [(i, i ^ mask) for i in range(4)])


def gather_group(value):
    return [value] + [across(value, mask) for mask in (1, 2, 3)]


def scatter_group(parts):
    received = [across(parts[mask].astype(bf16), mask) for mask in (1, 2, 3)]
    return parts[0] + received[0].astype(f32) + received[1].astype(f32) + received[2].astype(f32)


def stack_axis(value, axis):
    if lax.axis_size(axis) != 2:
        return lax.all_gather(value, axis)
    other = swap(value, axis)
    first = lax.axis_index(axis) == 0
    return jnp.where(first, jnp.stack([value, other]), jnp.stack([other, value]))


def gather_all(value):
    for axis in AXES[::-1]:
        value = stack_axis(value, axis)
    return value


def sum_all(value):
    for axis in ("q", "p", "c", "h", "y"):
        if lax.axis_size(axis) == 2:
            value = value + swap(value, axis)
        else:
            value = lax.psum(value, axis)
    return value


def binary_copies():
    return all(lax.axis_size(axis) == 2 for axis in COPIES)


def join(first, one, two):
    return jnp.where(first, jnp.concatenate([one, two]), jnp.concatenate([two, one]))


def gather_copies(block, chain):
    if not binary_copies():
        return lax.all_gather(block, COPIES, axis=0, tiled=True), chain
    block = after(block, chain) if chain is not None else block
    from_h = swap(block, "h")
    from_y = swap(block, "y")
    from_hy = swap(from_h, "y")
    mine = [block, from_h, from_y, from_hy]
    core = [swap(part, "c") for part in mine]
    h0, c0, y0 = (lax.axis_index(axis) == 0 for axis in ("h", "c", "y"))
    near = join(c0, join(h0, mine[0], mine[1]), join(h0, core[0], core[1]))
    far = join(c0, join(h0, mine[2], mine[3]), join(h0, core[2], core[3]))
    return join(y0, near, far), from_h


def pick(value, index, axis):
    return lax.dynamic_index_in_dim(value, index, axis, keepdims=False)


def scatter_copies(grad, order=("c", "y", "h")):
    sizes = [lax.axis_size(axis) for axis in COPIES]
    rows = grad.shape[0] // (sizes[0] * sizes[1] * sizes[2])
    value = grad.reshape(*sizes, rows, grad.shape[1])
    left = list(COPIES)
    for axis in order:
        dim = left.index(axis)
        if lax.axis_size(axis) == 2:
            mine = lax.axis_index(axis)
            keep = pick(value, mine, dim).astype(f32)
            value = keep + swap(pick(value, 1 - mine, dim).astype(bf16), axis).astype(f32)
        else:
            value = lax.psum_scatter(value.astype(bf16), axis, scatter_dimension=dim).astype(f32)
        left.remove(axis)
    return value


def share_columns(weight, place, columns):
    pieces = [columns(weight, t) for t in range(4)]
    got = []
    for mask in range(4):
        piece = lax.select_n(place, *[pieces[t ^ mask] for t in range(4)])
        got.append(piece if mask == 0 else across(piece, mask))
    return jnp.concatenate(
        [lax.select_n(place, *[got[t ^ spot] for t in range(4)]) for spot in range(4)]
    )


def return_columns(grad, place):
    value = grad.reshape(4, grad.shape[0] // 4, grad.shape[1])
    got = [pick(value, place, 0)]
    for mask in (1, 2, 3):
        got.append(across(pick(value, place ^ mask, 0).astype(bf16), mask).astype(f32))
    return [lax.select_n(place, *[got[t ^ spot] for t in range(4)]) for spot in range(4)]


def row_owner_moves():
    total = 1
    for axis in AXES:
        total *= lax.axis_size(axis)
    copies = total // 4
    return [(g, (g % copies) * 4 + g // copies) for g in range(total)]


def dot_nn(a, b):
    return lax.dot_general(a, b, (((1,), (0,)), ((), ())), preferred_element_type=f32)


def dot_nt(a, b):
    return lax.dot_general(a, b, (((1,), (1,)), ((), ())), preferred_element_type=f32)


def dot_tn(a, b):
    return lax.dot_general(a, b, (((0,), (0,)), ((), ())), preferred_element_type=f32)


def two_parts(value):
    high = value.astype(bf16)
    return high, (value - high.astype(f32)).astype(bf16)


def triangle(lower):
    row = lax.broadcasted_iota(jnp.int32, (SPAN, SPAN), 0)
    col = lax.broadcasted_iota(jnp.int32, (SPAN, SPAN), 1)
    return jnp.where(row >= col if lower else row <= col, 1.0, 0.0)


def running_sum(value, lower):
    ones = triangle(lower).astype(bf16)
    high, low = two_parts(value)
    return dot_nn(ones, high) + dot_nn(ones, low)


def pair_mask(meta, rows):
    return jnp.where(meta[:, 0:1] == rows[0:1, :], triangle(True), 0.0)


def states_kernel(
    place, kvr, up, bias, meta, rows, sums, raw, prior, through, end, decay, state, total
):
    @pl.when(pl.program_id(0) == 0)
    def _():
        state[...] = jnp.zeros_like(state)
        total[...] = jnp.ones_like(total)

    keys = kvr[:, :KEY].astype(f32)
    gate = dot_nn(kvr[:, KEY + VAL :], up[...]) + bias[...]
    log_decay = (jnp.minimum(gate, 0.0) - jnp.log1p(jnp.exp(-jnp.abs(gate)))) * (1.0 / 16.0)
    run = running_sum(log_decay, True)
    raw[...] = gate
    sums[...] = run
    last = run[SPAN - 1 :, :]
    info = meta[...]
    k_final = (keys * jnp.exp(last - run) * (info[:, 1:2] * info[:, 3:4])).astype(bf16)
    step = rows[0, 1:2, 0:1] * jnp.exp(last)
    prior[0] = state[...].astype(bf16)
    through[0] = total[...]
    state[...] = step * state[...] + dot_tn(kvr[:, KEY : KEY + VAL], k_final)
    total[...] = step * total[...]
    end[...] = state[...].astype(bf16)
    decay[...] = total[...]


def mixed_kernel(place, kvr, qog, sums, prior, through, entering, gain, meta, rows, gated, mixed):
    info = meta[...]
    run = sums[...]
    query = qog[:, :KEY].astype(bf16).astype(f32)
    q_decay = (query * QSCALE * jnp.exp(run)).astype(bf16)
    k_decay = (kvr[:, :KEY].astype(f32) * info[:, 1:2] * jnp.exp(-run)).astype(bf16)
    scores = (dot_nt(q_decay, k_decay) * pair_mask(info, rows[0])).astype(bf16)
    state = (prior[0].astype(f32) + through[0] * entering[...].astype(f32)).astype(bf16)
    out = dot_nn(scores, kvr[:, KEY : KEY + VAL]) + info[:, 2:3] * dot_nt(q_decay, state)
    mixed[...] = out
    gate = qog[:, KEY:]
    scale = lax.rsqrt(jnp.mean(out * out, axis=-1, keepdims=True) + FLOOR)
    gated[...] = (out * scale * gain[...] * gate * jax.nn.sigmoid(gate)).astype(bf16)


def gate_grad_kernel(
    place,
    grad_gated,
    qog,
    mixed,
    sums,
    gain,
    meta,
    rows,
    grad_out,
    grad_gate,
    later,
    beyond,
    start,
    decay,
    grad_gain,
    state,
    total,
):
    @pl.when(pl.program_id(0) == 0)
    def _():
        state[...] = jnp.zeros_like(state)
        total[...] = jnp.ones_like(total)
        grad_gain[...] = jnp.zeros_like(grad_gain)

    info = meta[...]
    run = sums[...]
    out = mixed[...]
    gate = qog[:, KEY:]
    grad = grad_gated[...]
    sig = jax.nn.sigmoid(gate)
    scale = lax.rsqrt(jnp.mean(out * out, axis=-1, keepdims=True) + FLOOR)
    scaled = out * scale
    swish = gate * sig
    weighted = grad * gain[...] * swish
    inner = jnp.mean(scaled * weighted, axis=-1, keepdims=True)
    grad_o = (scale * (weighted - scaled * inner)).astype(bf16)
    grad_out[...] = grad_o
    grad_gate[...] = (grad * scaled * gain[...] * sig * (1.0 + gate * (1.0 - sig))).astype(bf16)
    grad_gain[...] += jnp.sum(grad * scaled * swish, axis=0, keepdims=True)
    query = qog[:, :KEY].astype(bf16).astype(f32)
    q_enter = (query * QSCALE * jnp.exp(run)).astype(bf16)
    o_enter = jnp.where(info[:, 2:3] > 0.0, grad_o.astype(f32), 0.0).astype(bf16)
    step = rows[0, 1:2, 0:1] * jnp.exp(run[SPAN - 1 :, :])
    later[0] = state[...].astype(bf16)
    beyond[0] = total[...]
    state[...] = step * state[...] + dot_tn(o_enter, q_enter)
    total[...] = step * total[...]
    start[...] = state[...].astype(bf16)
    decay[...] = total[...]


def inputs_grad_kernel(
    place,
    kvr,
    qog,
    sums,
    raw,
    grad_out,
    grad_gate,
    prior,
    through,
    entering,
    later,
    beyond,
    leaving,
    up,
    meta,
    rows,
    grad_kvr,
    grad_qog,
    grad_up,
    grad_bias,
):
    @pl.when(pl.program_id(0) == 0)
    def _():
        grad_up[...] = jnp.zeros_like(grad_up)
        grad_bias[...] = jnp.zeros_like(grad_bias)

    info = meta[...]
    run = sums[...]
    last = run[SPAN - 1 :, :]
    valid, enter, carry = info[:, 1:2], info[:, 2:3], info[:, 3:4]
    grow, shrink, tail = jnp.exp(run), jnp.exp(-run), jnp.exp(last - run) * carry
    query = qog[:, :KEY].astype(bf16).astype(f32)
    keys = kvr[:, :KEY].astype(f32) * valid
    values = kvr[:, KEY : KEY + VAL]
    q_decay = (query * QSCALE * grow).astype(bf16)
    k_decay = (keys * shrink).astype(bf16)
    k_final = (keys * tail).astype(bf16)
    mask = pair_mask(info, rows[0])
    state = prior[0].astype(f32) + through[0] * entering[...].astype(f32)
    state_grad = later[0].astype(f32) + beyond[0] * leaving[...].astype(f32)
    state_b, state_grad_b = state.astype(bf16), state_grad.astype(bf16)
    grad_o = grad_out[...]
    scores = (dot_nt(q_decay, k_decay) * mask).astype(bf16)
    grad_scores = (dot_nt(grad_o, values) * mask).astype(bf16)
    grad_v = dot_tn(scores, grad_o) + dot_nt(k_final, state_grad_b)
    grad_qd = dot_nn(grad_scores, k_decay) + enter * dot_nn(grad_o, state_b)
    grad_kd = dot_tn(grad_scores, q_decay)
    grad_kf = dot_nn(values, state_grad_b)
    step = rows[0, 1:2, 0:1] * jnp.exp(last)
    through_last = step * jnp.sum(state * state_grad, axis=0, keepdims=True)
    final_part = grad_kf * k_final.astype(f32)
    grad_run = grad_qd * q_decay.astype(f32) - grad_kd * k_decay.astype(f32) - final_part
    grad_last = through_last + jnp.sum(final_part, axis=0, keepdims=True)
    grad_log = running_sum(grad_run, False) + grad_last
    grad_raw = grad_log * jax.nn.sigmoid(-raw[...]) * (1.0 / 16.0)
    high, low = two_parts(grad_raw)
    rank = kvr[:, KEY + VAL :]
    grad_up[...] += dot_tn(rank, high) + dot_tn(rank, low)
    grad_bias[...] += jnp.sum(grad_raw, axis=0, keepdims=True)
    grad_rank = dot_nt(high, up[...]) + dot_nt(low, up[...])
    grad_k = (grad_kd * shrink + grad_kf * tail) * valid
    grad_kvr[:, :KEY] = grad_k.astype(bf16)
    grad_kvr[:, KEY : KEY + VAL] = grad_v.astype(bf16)
    grad_kvr[:, KEY + VAL :] = grad_rank.astype(bf16)
    grad_qog[:, :KEY] = (grad_qd * grow * QSCALE).astype(bf16)
    grad_qog[:, KEY:] = grad_gate[...]


class Mixer:
    def __init__(self, place, blocks, per_device):
        self.place = place.reshape(1)
        self.blocks = blocks
        self.per_device = per_device

    def call(self, kernel, specs, args, outs, scratch=(), reverse=False, flops=0):
        count, per_device = self.blocks, self.per_device

        def at(step):
            return count - 1 - step if reverse else step

        def spec(kind, shape):
            if kind == "rows":
                return pl.BlockSpec(
                    (SPAN, shape[1]),
                    lambda n, place: (
                        lax.bitwise_xor(at(n) // per_device, place[0]) * per_device
                        + at(n) % per_device,
                        0,
                    ),
                )
            if kind == "tokens":
                return pl.BlockSpec((SPAN, shape[1]), lambda n, place: (at(n), 0))
            if kind == "blocks":
                return pl.BlockSpec((1,) + shape[1:], lambda n, place: (at(n), 0, 0))
            return pl.BlockSpec(shape, lambda n, place: (0,) * len(shape))

        size = sum(a.size * a.dtype.itemsize for a in args)
        return pl.pallas_call(
            kernel,
            grid_spec=pltpu.PrefetchScalarGridSpec(
                num_scalar_prefetch=1,
                grid=(count,),
                in_specs=[spec(kind, a.shape) for kind, a in zip(specs, args)],
                out_specs=[spec(kind, shape) for kind, shape, _ in outs],
                scratch_shapes=list(scratch),
            ),
            out_shape=[jax.ShapeDtypeStruct(shape, kind) for _, shape, kind in outs],
            compiler_params=pltpu.CompilerParams(
                dimension_semantics=("arbitrary",), vmem_limit_bytes=48 * 1024 * 1024
            ),
            cost_estimate=pl.CostEstimate(
                flops=flops, bytes_accessed=2 * size, transcendentals=4 * SPAN * KEY * count
            ),
        )(self.place, *args)


def normed(values, gain):
    return values * lax.rsqrt(jnp.mean(values * values, axis=-1, keepdims=True) + EPS) * gain


def normed_grad(values, gain, grad):
    scale = lax.rsqrt(jnp.mean(values * values, axis=-1, keepdims=True) + EPS)
    weighted = grad * gain
    inner = jnp.mean(weighted * values, axis=-1, keepdims=True)
    return (
        scale * weighted - scale * scale * scale * values * inner,
        jnp.sum(grad * values * scale, axis=0),
    )


def mm(left, right, out=f32):
    return jnp.dot(left, right, preferred_element_type=f32).astype(out)


def mm_tn(left, right, out=f32):
    return dot_tn(left, right).astype(out)


def kvr_columns(weight, t):
    wide = HEADS * KEY
    return jnp.concatenate(
        [
            weight[:, wide + t * KEY : wide + (t + 1) * KEY],
            weight[:, 2 * wide + t * VAL : 2 * wide + (t + 1) * VAL],
            weight[:, 2 * wide + 2 * HEADS * VAL :],
        ],
        axis=1,
    )


def qog_columns(weight, t):
    start = 2 * HEADS * KEY + HEADS * VAL
    return jnp.concatenate(
        [
            weight[:, t * KEY : (t + 1) * KEY],
            weight[:, start + t * VAL : start + (t + 1) * VAL],
        ],
        axis=1,
    )


def from_earlier(end, decay):
    count = lax.axis_size("h")
    if count == 2:
        return lax.ppermute(end, "h", [(0, 1)])
    ends, decays = lax.all_gather(end, "h"), lax.all_gather(decay, "h")
    mine = lax.axis_index("h")
    state = jnp.zeros(end.shape, f32)
    for h in range(count - 1):
        state = jnp.where(h < mine, decays[h] * state + ends[h].astype(f32), state)
    return state.astype(bf16)


def from_later(start, decay):
    count = lax.axis_size("h")
    if count == 2:
        return lax.ppermute(start, "h", [(1, 0)])
    starts, decays = lax.all_gather(start, "h"), lax.all_gather(decay, "h")
    mine = lax.axis_index("h")
    state = jnp.zeros(start.shape, f32)
    for h in range(count - 1, 0, -1):
        state = jnp.where(h > mine, decays[h] * state + starts[h].astype(f32), state)
    return state.astype(bf16)


def local(
    hidden_in,
    in_weight,
    out_weight,
    decay_up,
    decay_bias,
    mixer_gain,
    head_gain,
    ffn_in,
    ffn_out,
    ffn_gain,
    out_grad,
    seg_ids,
    valid_mask,
):
    tokens, width = hidden_in.shape[1:]
    place = 2 * lax.axis_index("p") + lax.axis_index("q")
    half = lax.axis_index("h")
    sizes = [lax.axis_size(axis) for axis in AXES]
    devices = sizes[0] * sizes[1] * sizes[2] * 4
    me = place
    stride = 4
    for axis in ("h", "c", "y"):
        me = me + stride * lax.axis_index(axis)
        stride *= lax.axis_size(axis)
    ff = ffn_in.shape[1] // 2
    quarter = ff // 4
    rows_all = 4 * tokens
    count = rows_all // SPAN
    x_own = hidden_in.reshape(tokens, width)
    dy_own = out_grad.reshape(tokens, width)

    small = [
        decay_up.reshape(-1),
        decay_bias,
        mixer_gain,
        head_gain,
        ffn_gain,
        seg_ids.reshape(-1).astype(bf16),
        valid_mask.reshape(-1).astype(bf16),
    ]
    lengths = [part.shape[0] for part in small]
    packed = jnp.concatenate(small)
    padded = -(-packed.shape[0] // 1024) * 1024
    packed = jnp.pad(packed, (0, padded - packed.shape[0])).reshape(-1, 128)
    everyone = gather_all(packed).reshape(sizes[0], sizes[1], -1, padded)
    offset = [sum(lengths[:i]) for i in range(len(lengths) + 1)]

    def small_part(i):
        return everyone[..., offset[i] : offset[i + 1]]

    up_cols = decay_up.shape[1]
    up_all = small_part(0).reshape(devices, RANK, up_cols).transpose(1, 0, 2).reshape(RANK, HEADS, KEY)
    up_head = pick(up_all, place, 1)
    bias_head = pick(small_part(1).reshape(HEADS, 1, KEY), place, 0).astype(f32)
    gain_one = small_part(2).reshape(-1).astype(f32)
    gain_head = small_part(3).reshape(1, -1).astype(f32)
    gain_two = small_part(4).reshape(-1).astype(f32)

    def of_sequence(value):
        return pick(pick(value, lax.axis_index("y"), 0), lax.axis_index("c"), 0).reshape(-1)

    seg_all = of_sequence(small_part(5)).astype(f32)
    valid_all = of_sequence(small_part(6)).astype(f32)
    valid_count = jnp.sum(small_part(6).astype(f32))
    seg_here = lax.dynamic_slice(
        jnp.concatenate([jnp.full((1,), -1.0, f32), seg_all]), (half * rows_all,), (rows_all + 1,)
    )
    valid_here = lax.dynamic_slice(valid_all, (half * rows_all,), (rows_all,))
    seg_blocks = seg_here[1:].reshape(count, SPAN)
    before = seg_here[:-1].reshape(count, SPAN)[:, :1]
    final = seg_blocks[:, -1:]
    meta = jnp.stack(
        [
            seg_here[1:],
            valid_here,
            (seg_blocks == before).astype(f32).reshape(-1),
            (seg_blocks == final).astype(f32).reshape(-1),
        ]
        + [jnp.zeros((rows_all,), f32)] * 4,
        axis=1,
    )
    keep = jnp.broadcast_to((final == before).astype(f32), (count, SPAN))
    rows = jnp.stack([seg_blocks, keep] + [jnp.zeros((count, SPAN), f32)] * 6, axis=1)

    kvr_rows = share_columns(in_weight, place, kvr_columns)
    qog_rows = share_columns(in_weight, place, qog_columns)
    w_kvr, chain = gather_copies(kvr_rows, None)
    w_qog, chain = gather_copies(qog_rows, chain)
    x_group = jnp.concatenate(gather_group(after(x_own, qog_rows)))
    moves = row_owner_moves()
    back = [(b, a) for a, b in moves]
    w_out, chain = gather_copies(lax.ppermute(out_weight, AXES, moves), chain)
    dy_group = jnp.concatenate(gather_group(after(dy_own, x_group)))
    ffn_late = after(ffn_in, x_group)
    gate_rows = share_columns(ffn_late, place, lambda w, t: w[:, t * quarter : (t + 1) * quarter])
    up_rows = share_columns(
        ffn_late, place, lambda w, t: w[:, ff + t * quarter : ff + (t + 1) * quarter]
    )
    down_rows = lax.ppermute(ffn_out, AXES, moves)
    w_down, chain = gather_copies(down_rows, chain)
    w_gate, chain = gather_copies(gate_rows, chain)
    w_up, chain = gather_copies(up_rows, chain)

    n1 = normed(x_group.astype(f32), gain_one).astype(bf16)
    kvr = mm(n1, w_kvr, bf16)
    mixer = Mixer(place, count, tokens // SPAN)
    state_shape = (VAL, KEY)
    scratch = [pltpu.VMEM(state_shape, f32), pltpu.VMEM((1, KEY), f32)]
    sums, raw, prior, through, end, decay = mixer.call(
        states_kernel,
        ["rows", "whole", "whole", "tokens", "blocks"],
        [kvr, up_head, bias_head, meta, rows],
        [
            ("rows", (rows_all, KEY), f32),
            ("rows", (rows_all, KEY), f32),
            ("blocks", (count,) + state_shape, bf16),
            ("blocks", (count, 1, KEY), f32),
            ("whole", state_shape, bf16),
            ("whole", (1, KEY), f32),
        ],
        scratch,
        flops=2 * rows_all * KEY * VAL,
    )
    entering = from_earlier(end, decay)
    qog = mm(n1, w_qog)
    gated, mixed = mixer.call(
        mixed_kernel,
        ["rows", "rows", "rows", "blocks", "blocks", "whole", "whole", "tokens", "blocks"],
        [kvr, qog, sums, prior, through, entering, gain_head, meta, rows],
        [("rows", (rows_all, VAL), bf16), ("rows", (rows_all, VAL), f32)],
        flops=2 * rows_all * (KEY * VAL + SPAN * (KEY + VAL)),
    )
    mix_parts = mm(gated, w_out).reshape(4, tokens, width)
    mix = scatter_group([mix_parts[m] for m in range(4)])
    h1 = x_own.astype(f32) + mix

    grad_hidden = mm_nt(dy_group, w_down)
    n2 = normed(h1, gain_two).astype(bf16)
    n2_group = jnp.concatenate(gather_group(n2))
    gate = mm(n2_group, w_gate)
    up = mm(n2_group, w_up)
    sig = jax.nn.sigmoid(gate)
    hidden = (gate * sig * up).astype(bf16)
    y_parts = mm(hidden, w_down).reshape(4, tokens, width)
    grad_g = (grad_hidden * up * sig * (1.0 + gate * (1.0 - sig))).astype(bf16)
    grad_u = (grad_hidden * gate * sig).astype(bf16)
    n2_grad_parts = (mm_nt(grad_g, w_gate) + mm_nt(grad_u, w_up)).reshape(4, tokens, width)
    n2_grad = scatter_group([n2_grad_parts[m] for m in range(4)])
    h1_grad_part, gain_two_grad = normed_grad(h1, gain_two, n2_grad)
    h1_grad = dy_own.astype(f32) + h1_grad_part
    mix_grad = jnp.concatenate(gather_group(h1_grad.astype(bf16)))

    down_grad = mm_tn(hidden, dy_group, bf16)
    gate_w_grad = mm_tn(n2_group, grad_g, bf16)
    up_w_grad = mm_tn(n2_group, grad_u, bf16)
    down_sum = scatter_copies(down_grad)
    gate_sum = scatter_copies(gate_w_grad)
    up_sum = scatter_copies(up_w_grad, ("c", "h", "y"))
    ffnout_grad = lax.ppermute(down_sum.astype(bf16), AXES, back).astype(f32)
    ffnin_grad = jnp.concatenate(return_columns(gate_sum, place) + return_columns(up_sum, place), axis=1)

    grad_gated = mm_nt(mix_grad, w_out)
    grad_o, grad_gate, later, beyond, start, decay_b, head_grad = mixer.call(
        gate_grad_kernel,
        ["rows", "rows", "rows", "rows", "whole", "tokens", "blocks"],
        [grad_gated, qog, mixed, sums, gain_head, meta, rows],
        [
            ("rows", (rows_all, VAL), bf16),
            ("rows", (rows_all, VAL), bf16),
            ("blocks", (count,) + state_shape, bf16),
            ("blocks", (count, 1, KEY), f32),
            ("whole", state_shape, bf16),
            ("whole", (1, KEY), f32),
            ("whole", (1, VAL), f32),
        ],
        scratch,
        reverse=True,
        flops=2 * rows_all * KEY * VAL,
    )
    leaving = from_later(start, decay_b)
    out_w_grad = mm_tn(gated, mix_grad, bf16)
    outproj_grad = lax.ppermute(scatter_copies(out_w_grad).astype(bf16), AXES, back).astype(f32)

    y = scatter_group([after(y_parts[m], mix_grad) for m in range(4)])
    result = h1 + y
    block_out = result.astype(bf16).reshape(1, tokens, width)
    live = valid_mask.reshape(tokens, 1).astype(f32)
    squares = jnp.stack(
        [jnp.sum(live * result * result), jnp.sum(live * mix * mix), jnp.sum(live * y * y)]
    )

    grad_kvr, grad_qog, up_grad, bias_grad = mixer.call(
        inputs_grad_kernel,
        ["rows"] * 6 + ["blocks", "blocks", "whole", "blocks", "blocks", "whole", "whole", "tokens", "blocks"],
        [
            kvr,
            qog,
            sums,
            raw,
            grad_o,
            grad_gate,
            prior,
            through,
            entering,
            later,
            beyond,
            leaving,
            up_head,
            meta,
            rows,
        ],
        [
            ("rows", kvr.shape, bf16),
            ("rows", qog.shape, bf16),
            ("whole", (RANK, KEY), f32),
            ("whole", (1, KEY), f32),
        ],
        flops=2 * rows_all * (3 * KEY * VAL + SPAN * (3 * KEY + 2 * VAL)),
    )
    n1_grad_parts = (mm_nt(grad_kvr, w_kvr) + mm_nt(grad_qog, w_qog)).reshape(4, tokens, width)
    n1_grad = scatter_group([n1_grad_parts[m] for m in range(4)])
    input_part, gain_one_grad = normed_grad(x_own.astype(f32), gain_one, n1_grad)
    input_grad = (h1_grad + input_part).reshape(1, tokens, width)
    kvr_sum = scatter_copies(mm_tn(n1, grad_kvr, bf16))
    qog_sum = scatter_copies(mm_tn(n1, grad_qog, bf16), ("c", "h", "y"))
    kvr_back = return_columns(kvr_sum, place)
    qog_back = return_columns(qog_sum, place)
    inproj_grad = jnp.concatenate(
        [part[:, :KEY] for part in qog_back]
        + [part[:, :KEY] for part in kvr_back]
        + [part[:, KEY : KEY + VAL] for part in kvr_back]
        + [part[:, KEY:] for part in qog_back]
        + [sum(part[:, KEY + VAL :] for part in kvr_back)],
        axis=1,
    )

    head_slot = (lax.broadcasted_iota(jnp.int32, (HEADS, 1, 1), 0) == place).astype(f32)
    decay_part = head_slot * jnp.concatenate([up_grad, bias_grad], axis=0)[None]
    early = [squares, head_grad.reshape(-1), gain_two_grad, decay_part.reshape(-1)]
    total = jnp.concatenate(early)
    short = -total.shape[0] % 1024
    total = sum_all(jnp.pad(total, (0, short)).reshape(-1, 128)).reshape(-1)
    gain_one_sum = sum_all(gain_one_grad.reshape(-1, 128)).reshape(-1)
    ends = [0]
    for part in early:
        ends.append(ends[-1] + part.shape[0])
    squares = total[: ends[1]]
    root_means = jnp.sqrt(squares / (jnp.maximum(valid_count, 1.0) * width))

    def own(value, length):
        return lax.dynamic_slice(value, (me * length,), (length,))

    headgain_grad = own(total[ends[1] : ends[2]], head_gain.shape[0])
    ffngain_grad = own(total[ends[2] : ends[3]], ffn_gain.shape[0])
    mixgain_grad = own(gain_one_sum, mixer_gain.shape[0])
    decay_all = total[ends[3] : ends[4]].reshape(HEADS, RANK + 1, KEY)
    decay_all = decay_all.transpose(1, 0, 2).reshape(RANK + 1, HEADS * KEY)
    decay_own = lax.dynamic_slice(decay_all, (0, me * up_cols), (RANK + 1, up_cols))
    return (
        block_out,
        input_grad,
        inproj_grad,
        outproj_grad,
        decay_own[:RANK],
        decay_own[RANK],
        mixgain_grad,
        headgain_grad,
        ffnin_grad,
        ffnout_grad,
        ffngain_grad,
        root_means,
    )


def mm_nt(left, right, out=f32):
    return dot_nt(left, right).astype(out)


def solution(mesh):
    dp, seq = mesh.shape["dp"], mesh.shape["seq"]
    fine = Mesh(mesh.devices.reshape(dp // 2, 2, seq // 4, 2, 2), AXES)
    batch, spread, whole = ("y", "c"), ("h", "p", "q"), AXES
    placed = (
        P(batch, spread, None),
        P(whole, None),
        P(whole, None),
        P(None, whole),
        P(whole),
        P(whole),
        P(whole),
        P(whole, None),
        P(whole, None),
        P(whole),
        P(batch, spread, None),
        P(batch, spread),
        P(batch, spread),
    )
    return jax.shard_map(
        local,
        mesh=fine,
        in_specs=placed,
        out_specs=(
            P(batch, spread, None),
            P(batch, spread, None),
            P(whole, None),
            P(whole, None),
            P(None, whole),
            P(whole),
            P(whole),
            P(whole),
            P(whole, None),
            P(whole, None),
            P(whole),
            P(),
        ),
        check_vma=False,
    )
```

time: 5630 us -> 950 us (0.17)
  waiting for transfers between devices: 4990 us -> 480 us
  blocking collectives: 237 us -> 0 us
  starting transfers between devices: 0.9 us -> 186 us
  matrix products: 232 us -> 95.9 us
    reduce_scatter x4 -> x0, waiting for transfers between devices: 4290 us -> none  [the longest x1 1930 us: local(): lax.psum_scatter(grad_ffn_in, ('dp', 'seq'), scatter_dimension=0, tiled=T...]
    all_gather x6 -> x0, waiting for transfers between devices: 698 us -> none  [the longest x1 249 us: local(): lax.all_gather(ffn_in, ('dp', 'seq'), axis=0, tiled=True)]
    ppermute x0 -> x129, waiting for transfers between devices: none -> 480 us  [the longest x75 276 us: swap(): return lax.ppermute(value, axis, [(0, 1), (1, 0)])]
    ppermute x0 -> x129, starting transfers between devices: none -> 186 us  [the longest x75 80.8 us: swap(): return lax.ppermute(value, axis, [(0, 1), (1, 0)])]
    dot_general x28 -> x18, matrix products: 231 us -> 95.9 us  [the longest x6 45.4 us: dot_nt(): lax.dot_general(a, b, (((1,), (1,)), ((), ())), preferred_element_type=f32)]
    all_gather x3 -> x0, blocking collectives: 124 us -> none  [the longest x1 65.8 us: local(): lax.all_gather(decay_up, ('dp', 'seq'), axis=1, tiled=True)]
    unnamed x3 -> x0, blocking collectives: 113 us -> none
  transfers between devices with their start and end apart: 11 -> 129, of which waited for: 10 -> 58; matrix products, arithmetic and copies ran while one was open for 4% -> 18% of each run, Pallas kernels for 0% -> 3%
where the time goes in v1:
time: 950 us; the launch traced here: 938 us
  waiting for transfers between devices  480 us (51%)
  starting transfers between devices  186 us (20%)
  matrix products  95.9 us (10%)
  other arithmetic  82.5 us (9%)
  local copies, waits for them, and re-layouts  63.4 us (7%)
  Pallas kernels  25.6 us (3%)
    ppermute x75, waiting for transfers between devices, swap(): return lax.ppermute(value, axis, [(0, 1), (1, 0)])  276 us
    ppermute x48, waiting for transfers between devices, across(): return lax.ppermute(value, ('p', 'q'), [(i, i ^ mask) for i in range(4)])  164 us
    ppermute x75, starting transfers between devices, swap(): return lax.ppermute(value, axis, [(0, 1), (1, 0)])  80.8 us
    ppermute x48, starting transfers between devices, across(): return lax.ppermute(value, ('p', 'q'), [(i, i ^ mask) for i in range(4)])  80.1 us
    dot_general x6, matrix products, dot_nt(): lax.dot_general(a, b, (((1,), (1,)), ((), ())), preferred_element_type=f32)  45.4 us
    select_n x36, other arithmetic, join(): jnp.where(first, jnp.concatenate([one, two]), jnp.concatenate([two, one]))  42.4 us
    ppermute x1, waiting for transfers between devices, from_earlier(): return lax.ppermute(end, 'h', [(0, 1)])  32.4 us
    dot_general x6, matrix products, mm(): return jnp.dot(left, right, preferred_element_type=f32).astype(out)  26.7 us
  transfers between devices with their start and end apart: 129, of which 58 were waited for; matrix products, arithmetic and copies ran while one was open for 18% of the time, Pallas kernels for 3%

profile of v1, /device:TPU:8, one launch (start us, length us, event | category | flops | bytes accessed | tf_op | source)
XLA Modules:
  0.0 937.9 jit_solution(12942130011152741724)
XLA Ops:
  20.4 10.2 %collective-permute-done.7 = bf16[2,8,128]{2,1,0:T(8,128)(2,1)S(1)} collective-permute-done((bf16[2,8,128]{2,1,0:T(8,128)(2,1)S(1)}, bf16[2,8,128]{2,1,0:T(8,128)(2,1)S(1)}, u32[]{:S(2)}, u32[]{:S(2)}) %collective-permute-start.7) | collective-permute-done | bytes 4128 | tf_op jit(solution)/shard_map/ppermute | solution.py:29
  58.7 13.7 %collective-permute-done.14 = bf16[256,784]{1,0:T(8,128)(2,1)S(1)} collective-permute-done((bf16[256,784]{1,0:T(8,128)(2,1)S(1)}, bf16[256,784]{1,0:T(8,128)(2,1)S(1)}, u32[]{:S(2)}, u32[]{:S(2)}) %collective-permute-start.14) | collective-permute-done | bytes 401440 | tf_op jit(solution)/shard_map/ppermute | solution.py:29
  100.2 13.8 %collective-permute-done.21 = bf16[256,768]{1,0:T(8,128)(2,1)S(1)} collective-permute-done((bf16[256,768]{1,0:T(8,128)(2,1)S(1)}, bf16[256,768]{1,0:T(8,128)(2,1)S(1)}, u32[]{:S(2)}, u32[]{:S(2)}) %collective-permute-start.21) | collective-permute-done | bytes 393248 | tf_op jit(solution)/shard_map/ppermute | solution.py:29
  124.2 45.2 %collective-permute-done.57 = bf16[64,1408]{1,0:T(8,128)(2,1)S(1)} collective-permute-done((bf16[64,1408]{1,0:T(8,128)(2,1)S(1)}, bf16[64,1408]{1,0:T(8,128)(2,1)S(1)}, u32[]{:S(2)}, u32[]{:S(2)}) %collective-permute-start.57) | collective-permute-done | bytes 180256 | tf_op jit(solution)/shard_map/ppermute | solution.py:33
  173.9 7.4 collective-permute-done.71
  217.9 32.4 %collective-permute-done.28.entering = bf16[512,256]{1,0:T(8,128)(2,1)S(1)} collective-permute-done((bf16[512,256]{1,0:T(8,128)(2,1)S(1)}, bf16[512,256]{1,0:T(8,128)(2,1)S(1)}, u32[]{:S(2)}, u32[]{:S(2)}) %collective-permute-start.28) | collective-permute-done | bytes 262176 | tf_op jit(solution)/shard_map/ppermute | solution.py:430
  269.4 13.7 %collective-permute-done.37 = bf16[128,2048]{1,0:T(8,128)(2,1)S(1)} collective-permute-done((bf16[128,2048]{1,0:T(8,128)(2,1)S(1)}, bf16[128,2048]{1,0:T(8,128)(2,1)S(1)}, u32[]{:S(2)}, u32[]{:S(2)}) %collective-permute-start.37) | collective-permute-done | bytes 524320 | tf_op jit(solution)/shard_map/ppermute | solution.py:33
  286.5 8.8 collective-permute-done.38
  299.7 14.5 %collective-permute-done.48 = bf16[256,1408]{1,0:T(8,128)(2,1)S(1)} collective-permute-done((bf16[256,1408]{1,0:T(8,128)(2,1)S(1)}, bf16[256,1408]{1,0:T(8,128)(2,1)S(1)}, u32[]{:S(2)}, u32[]{:S(2)}) %collective-permute-start.48) | collective-permute-done | bytes 720928 | tf_op jit(solution)/shard_map/ppermute | solution.py:29
  314.7 17.3 %collective-permute-start.51 = (bf16[256,1408]{1,0:T(8,128)(2,1)S(1)}, bf16[256,1408]{1,0:T(8,128)(2,1)S(1)}, u32[]{:S(2)}, u32[]{:S(2)}) collective-permute-start(bf16[256,1408]{1,0:T(8,128)(2,1)S(1)} %pad_maximum_fusion.2), channel_id=1, source_target_pairs={{0,16},{16,0},{1,17},{17,1},{2,18},{18,2},{3,19},{19,3},{4,20},{20... | collective-permute-start | bytes 2162696 | tf_op jit(solution)/shard_map/ppermute | solution.py:29
  339.7 12.2 %collective-permute-done.58 = bf16[256,1408]{1,0:T(8,128)(2,1)S(1)} collective-permute-done((bf16[256,1408]{1,0:T(8,128)(2,1)S(1)}, bf16[256,1408]{1,0:T(8,128)(2,1)S(1)}, u32[]{:S(2)}, u32[]{:S(2)}) %collective-permute-start.58) | collective-permute-done | bytes 720928 | tf_op jit(solution)/shard_map/ppermute | solution.py:29
  356.7 12.9 %collective-permute-done.52 = bf16[256,1408]{1,0:T(8,128)(2,1)S(1)} collective-permute-done((bf16[256,1408]{1,0:T(8,128)(2,1)S(1)}, bf16[256,1408]{1,0:T(8,128)(2,1)S(1)}, u32[]{:S(2)}, u32[]{:S(2)}) %collective-permute-start.52) | collective-permute-done | bytes 720928 | tf_op jit(solution)/shard_map/ppermute | solution.py:29
  378.4 10.9 %collective-permute-done.61 = bf16[256,1408]{1,0:T(8,128)(2,1)S(1)} collective-permute-done((bf16[256,1408]{1,0:T(8,128)(2,1)S(1)}, bf16[256,1408]{1,0:T(8,128)(2,1)S(1)}, u32[]{:S(2)}, u32[]{:S(2)}) %collective-permute-start.61) | collective-permute-done | bytes 720928 | tf_op jit(solution)/shard_map/ppermute | solution.py:29
  389.2 15.1 %collective-permute-done.62 = bf16[256,1408]{1,0:T(8,128)(2,1)S(1)} collective-permute-done((bf16[256,1408]{1,0:T(8,128)(2,1)S(1)}, bf16[256,1408]{1,0:T(8,128)(2,1)S(1)}, u32[]{:S(2)}, u32[]{:S(2)}) %collective-permute-start.62) | collective-permute-done | bytes 720928 | tf_op jit(solution)/shard_map/ppermute | solution.py:29
  438.9 13.3 %multiply_convert_fusion = (bf16[512,1408]{1,0:T(8,128)(2,1)}, bf16[512,1408]{1,0:T(8,128)(2,1)}, bf16[512,1408]{1,0:T(8,128)(2,1)}) fusion(f32[512,1408]{1,0:T(8,128)} %fusion.28, f32[512,1408]{1,0:T(8,128)} %fusion.26, bf16[512,2048]{1,0:T(8,128)(2,1)} %constant_dynamic-update-slice_fusion.14, bf16[704,2048]{1,0:T(8,128)(2,1)} %maximum_select_fusion.10, ...), kind=kOutput, calls=%fused_computation.38 | convolution fusion | flops 2990276608 | bytes 17956864 | tf_op jit(solution)/shard_map/dot_general | solution.py:144
  452.2 7.4 fusion.25
  464.7 10.2 %fusion.27 = f32[512,2048]{1,0:T(8,128)} fusion(bf16[512,1408]{1,0:T(8,128)(2,1)} %get-tuple-element.103, bf16[1024,1408]{1,0:T(8,128)(2,1)S(1)} %copy-done.24, bf16[1024,1408]{1,0:T(8,128)(2,1)S(1)} %copy-done.20, pred[]{:T(512)S(6)} %eq.75), kind=kOutput, calls=%fused_computation.122 | convolution fusion | flops 2978742272 | bytes 11403265 | tf_op jit(solution)/shard_map/dot_general | solution.py:144
  474.9 11.5 %fusion.118 = (bf16[512,2048]{1,0:T(8,128)(2,1)S(1)}, f32[512,2048]{1,0:T(8,128)}) fusion(f32[512,2048]{1,0:T(8,128)} %fusion.27, bf16[512,1408]{1,0:T(8,128)(2,1)} %get-tuple-element.102, bf16[1024,1408]{1,0:T(8,128)(2,1)} %copy-done.25, bf16[1024,1408]{1,0:T(8,128)(2,1)S(1)} %copy-done.22, pred[]{:T(512)S(6)} %eq.75), kind=kOutput, calls=%fused_computation.406 | convolution fusion | flops 2980839424 | bytes 17694720 | tf_op jit(solution)/shard_map/dot_general | solution.py:144
  523.0 7.9 collective-permute-done.79
  530.8 8.0 collective-permute-done.78
  562.9 9.2 shard_map.223
  581.4 7.2 fusion.119
  588.6 8.7 reshape.740
  618.0 14.4 %collective-permute-done.84 = bf16[128,2048]{1,0:T(8,128)(2,1)} collective-permute-done((bf16[128,2048]{1,0:T(8,128)(2,1)}, bf16[128,2048]{1,0:T(8,128)(2,1)}, u32[]{:S(2)}, u32[]{:S(2)}) %collective-permute-start.84) | collective-permute-done | bytes 524320 | tf_op jit(solution)/shard_map/ppermute | solution.py:33
  665.0 12.0 %collective-permute-done.100 = bf16[2,64,2048]{2,1,0:T(8,128)(2,1)S(1)} collective-permute-done((bf16[2,64,2048]{2,1,0:T(8,128)(2,1)S(1)}, bf16[2,64,2048]{2,1,0:T(8,128)(2,1)S(1)}, u32[]{:S(2)}, u32[]{:S(2)}) %collective-permute-start.100) | collective-permute-done | bytes 524320 | tf_op jit(solution)/shard_map/ppermute | solution.py:29
  715.8 46.3 %collective-permute-done.88 = bf16[2,256,768]{2,1,0:T(8,128)(2,1)S(1)} collective-permute-done((bf16[2,256,768]{2,1,0:T(8,128)(2,1)S(1)}, bf16[2,256,768]{2,1,0:T(8,128)(2,1)S(1)}, u32[]{:S(2)}, u32[]{:S(2)}) %collective-permute-start.88) | collective-permute-done | bytes 786464 | tf_op jit(solution)/shard_map/ppermute | solution.py:29
  782.4 27.1 %collective-permute-done.95 = bf16[256,784]{0,1:T(8,128)(2,1)S(1)} collective-permute-done((bf16[256,784]{0,1:T(8,128)(2,1)S(1)}, bf16[256,784]{0,1:T(8,128)(2,1)S(1)}, u32[]{:S(2)}, u32[]{:S(2)}) %collective-permute-start.95) | collective-permute-done | bytes 401440 | tf_op jit(solution)/shard_map/ppermute | solution.py:29
  811.2 8.7 collective-permute-done.91
  834.1 22.9 %collective-permute-done.114 = bf16[2,256,1408]{2,1,0:T(8,128)(2,1)S(1)} collective-permute-done((bf16[2,256,1408]{2,1,0:T(8,128)(2,1)}, bf16[2,256,1408]{2,1,0:T(8,128)(2,1)S(1)}, u32[]{:S(2)}, u32[]{:S(2)}) %collective-permute-start.114) | collective-permute-done | bytes 1441824 | tf_op jit(solution)/shard_map/ppermute | solution.py:29
  865.1 14.3 %collective-permute-done.127 = bf16[176,2048]{1,0:T(8,128)(2,1)S(1)} collective-permute-done((bf16[176,2048]{1,0:T(8,128)(2,1)S(1)}, bf16[176,2048]{1,0:T(8,128)(2,1)S(1)}, u32[]{:S(2)}, u32[]{:S(2)}) %collective-permute-start.127) | collective-permute-done | bytes 720928 | tf_op jit(solution)/shard_map/ppermute | solution.py:29
  879.6 8.6 collective-permute-start.128
  894.9 20.2 %collective-permute-start.117 = (bf16[64,1408]{1,0:T(8,128)(2,1)S(1)}, bf16[64,1408]{1,0:T(8,128)(2,1)S(1)}, u32[]{:S(2)}, u32[]{:S(2)}) collective-permute-start(bf16[64,1408]{1,0:T(8,128)(2,1)S(1)} %get-tuple-element.122), channel_id=1, source_target_pairs={{0,2},{1,3},{2,0},{3,1},{4,6},{5,7},{6,4},{7,5},{8,10},{9,11},{10,... | collective-permute-start | bytes 540680 | tf_op jit(solution)/shard_map/ppermute | solution.py:33
  (659 shorter events, 447.9 us)
Async XLA Ops:
  7.0 93.0 %collective-permute-start.29 = (bf16[64,2048]{1,0:T(8,128)(2,1)}, bf16[64,2048]{1,0:T(8,128)(2,1)}, u32[]{:S(2)}, u32[]{:S(2)}) collective-permute-start(bf16[64,2048]{1,0:T(8,128)(2,1)} %param.15), channel_id=1, source_target_pairs={{0,0},{1,4},{2,8},{3,12},{4,16},{5,20},{6,24},{7,28},{8,1},{9,5},{... | collective-permute-start | bytes 786440 | tf_op jit(solution)/shard_map/ppermute | solution.py:543
  72.4 46.6 %collective-permute-start.17 = (bf16[256,784]{1,0:T(8,128)(2,1)S(1)}, bf16[256,784]{1,0:T(8,128)(2,1)S(1)}, u32[]{:S(2)}, u32[]{:S(2)}) collective-permute-start(bf16[256,784]{1,0:T(8,128)(2,1)S(1)} %pad_maximum_fusion.4), channel_id=1, source_target_pairs={{0,16},{16,0},{1,17},{17,1},{2,18},{18,2},{3,19},{19,3},{4,20},{20... | collective-permute-start | bytes 1204232 | tf_op jit(solution)/shard_map/ppermute | solution.py:29
  114.0 59.8 %collective-permute-start.46 = (bf16[176,2048]{1,0:T(8,128)(2,1)S(1)}, bf16[176,2048]{1,0:T(8,128)(2,1)S(1)}, u32[]{:S(2)}, u32[]{:S(2)}) collective-permute-start(bf16[176,2048]{1,0:T(8,128)(2,1)S(1)} %copy-done.63), channel_id=1, source_target_pairs={{0,0},{1,4},{2,8},{3,12},{4,16},{5,20},{6,24},{7,28},{8,1},{9,5},{... | collective-permute-start | bytes 2162696 | tf_op jit(solution)/shard_map/ppermute | solution.py:550
  119.0 68.9 %collective-permute-start.22 = (bf16[256,768]{1,0:T(8,128)(2,1)S(1)}, bf16[256,768]{1,0:T(8,128)(2,1)S(1)}, u32[]{:S(2)}, u32[]{:S(2)}) collective-permute-start(bf16[256,768]{1,0:T(8,128)(2,1)S(1)} %pad_maximum_fusion.5), channel_id=1, source_target_pairs={{0,8},{8,0},{1,9},{9,1},{2,10},{10,2},{3,11},{11,3},{4,12},{12,4},... | collective-permute-start | bytes 1179656 | tf_op jit(solution)/shard_map/ppermute | solution.py:29
  119.1 50.3 %collective-permute-start.57 = (bf16[64,1408]{1,0:T(8,128)(2,1)S(1)}, bf16[64,1408]{1,0:T(8,128)(2,1)S(1)}, u32[]{:S(2)}, u32[]{:S(2)}) collective-permute-start(bf16[64,1408]{1,0:T(8,128)(2,1)S(1)} %get-tuple-element.130), channel_id=1, source_target_pairs={{0,3},{1,2},{2,1},{3,0},{4,7},{5,6},{6,5},{7,4},{8,11},{9,10},{10,... | collective-permute-start | bytes 540680 | tf_op jit(solution)/shard_map/ppermute | solution.py:33
  120.3 49.1 %collective-permute-start.55 = (bf16[64,1408]{1,0:T(8,128)(2,1)S(1)}, bf16[64,1408]{1,0:T(8,128)(2,1)S(1)}, u32[]{:S(2)}, u32[]{:S(2)}) collective-permute-start(bf16[64,1408]{1,0:T(8,128)(2,1)S(1)} %get-tuple-element.125), channel_id=1, source_target_pairs={{0,1},{1,0},{2,3},{3,2},{4,5},{5,4},{6,7},{7,6},{8,9},{9,8},{10,11... | collective-permute-start | bytes 540680 | tf_op jit(solution)/shard_map/ppermute | solution.py:33
  122.0 50.3 %collective-permute-start.56 = (bf16[64,1408]{1,0:T(8,128)(2,1)S(1)}, bf16[64,1408]{1,0:T(8,128)(2,1)S(1)}, u32[]{:S(2)}, u32[]{:S(2)}) collective-permute-start(bf16[64,1408]{1,0:T(8,128)(2,1)S(1)} %get-tuple-element.126), channel_id=1, source_target_pairs={{0,2},{1,3},{2,0},{3,1},{4,6},{5,7},{6,4},{7,5},{8,10},{9,11},{10,... | collective-permute-start | bytes 540680 | tf_op jit(solution)/shard_map/ppermute | solution.py:33
  186.1 77.6 %collective-permute-start.73 = (bf16[128,2048]{1,0:T(8,128)(2,1)S(1)}, bf16[128,2048]{1,0:T(8,128)(2,1)}, u32[]{:S(2)}, u32[]{:S(2)}) collective-permute-start(bf16[128,2048]{1,0:T(8,128)(2,1)S(1)} %bitcast.300), channel_id=1, source_target_pairs={{0,3},{1,2},{2,1},{3,0},{4,7},{5,6},{6,5},{7,4},{8,11},{9,10},{10,... | collective-permute-start | bytes 1572872 | tf_op jit(solution)/shard_map/ppermute | solution.py:33
  201.5 57.9 %collective-permute-start.72 = (bf16[128,2048]{1,0:T(8,128)(2,1)S(1)}, bf16[128,2048]{1,0:T(8,128)(2,1)}, u32[]{:S(2)}, u32[]{:S(2)}) collective-permute-start(bf16[128,2048]{1,0:T(8,128)(2,1)S(1)} %bitcast.301), channel_id=1, source_target_pairs={{0,2},{1,3},{2,0},{3,1},{4,6},{5,7},{6,4},{7,5},{8,10},{9,11},{10,... | collective-permute-start | bytes 1572872 | tf_op jit(solution)/shard_map/ppermute | solution.py:33
  205.3 60.4 %collective-permute-start.47 = (bf16[176,2048]{1,0:T(8,128)(2,1)}, bf16[176,2048]{1,0:T(8,128)(2,1)}, u32[]{:S(2)}, u32[]{:S(2)}) collective-permute-start(bf16[176,2048]{1,0:T(8,128)(2,1)} %copy-done.48), channel_id=1, source_target_pairs={{0,4},{4,0},{1,5},{5,1},{2,6},{6,2},{3,7},{7,3},{8,12},{12,8},{9,1... | collective-permute-start | bytes 2162696 | tf_op jit(solution)/shard_map/ppermute | solution.py:29
  265.6 70.2 %collective-permute-start.65 = (bf16[176,2048]{1,0:T(8,128)(2,1)S(1)}, bf16[176,2048]{1,0:T(8,128)(2,1)S(1)}, u32[]{:S(2)}, u32[]{:S(2)}) collective-permute-start(bf16[176,2048]{1,0:T(8,128)(2,1)S(1)} %copy-done.49), channel_id=1, source_target_pairs={{0,8},{8,0},{1,9},{9,1},{2,10},{10,2},{3,11},{11,3},{4,12},{12,4},... | collective-permute-start | bytes 2162696 | tf_op jit(solution)/shard_map/ppermute | solution.py:29
  265.7 49.1 %collective-permute-start.67 = (bf16[176,2048]{1,0:T(8,128)(2,1)S(1)}, bf16[176,2048]{1,0:T(8,128)(2,1)S(1)}, u32[]{:S(2)}, u32[]{:S(2)}) collective-permute-start(bf16[176,2048]{1,0:T(8,128)(2,1)S(1)} %copy-done.49), channel_id=1, source_target_pairs={{0,16},{16,0},{1,17},{17,1},{2,18},{18,2},{3,19},{19,3},{4,20},{20... | collective-permute-start | bytes 2162696 | tf_op jit(solution)/shard_map/ppermute | solution.py:29
  286.5 49.5 %collective-permute-start.66 = (bf16[176,2048]{1,0:T(8,128)(2,1)}, bf16[176,2048]{1,0:T(8,128)(2,1)S(1)}, u32[]{:S(2)}, u32[]{:S(2)}) collective-permute-start(bf16[176,2048]{1,0:T(8,128)(2,1)} %collective-permute-done.47), channel_id=1, source_target_pairs={{0,8},{8,0},{1,9},{9,1},{2,10},{10,2},{3,11},{11,3},{4,12},{12,4},... | collective-permute-start | bytes 2162696 | tf_op jit(solution)/shard_map/ppermute | solution.py:29
  314.2 56.0 %collective-permute-start.49 = (bf16[256,1408]{1,0:T(8,128)(2,1)S(1)}, bf16[256,1408]{1,0:T(8,128)(2,1)S(1)}, u32[]{:S(2)}, u32[]{:S(2)}) collective-permute-start(bf16[256,1408]{1,0:T(8,128)(2,1)S(1)} %pad_maximum_fusion.2), channel_id=1, source_target_pairs={{0,8},{8,0},{1,9},{9,1},{2,10},{10,2},{3,11},{11,3},{4,12},{12,4},... | collective-permute-start | bytes 2162696 | tf_op jit(solution)/shard_map/ppermute | solution.py:29
  314.7 41.5 %collective-permute-start.51 = (bf16[256,1408]{1,0:T(8,128)(2,1)S(1)}, bf16[256,1408]{1,0:T(8,128)(2,1)S(1)}, u32[]{:S(2)}, u32[]{:S(2)}) collective-permute-start(bf16[256,1408]{1,0:T(8,128)(2,1)S(1)} %pad_maximum_fusion.2), channel_id=1, source_target_pairs={{0,16},{16,0},{1,17},{17,1},{2,18},{18,2},{3,19},{19,3},{4,20},{20... | collective-permute-start | bytes 2162696 | tf_op jit(solution)/shard_map/ppermute | solution.py:29
  352.9 62.3 %collective-permute-start.42 = (bf16[128,2048]{1,0:T(8,128)(2,1)S(1)}, bf16[128,2048]{1,0:T(8,128)(2,1)}, u32[]{:S(2)}, u32[]{:S(2)}) collective-permute-start(bf16[128,2048]{1,0:T(8,128)(2,1)S(1)} %multiply_convert_fusion.3), channel_id=1, source_target_pairs={{0,3},{1,2},{2,1},{3,0},{4,7},{5,6},{6,5},{7,4},{8,11},{9,10},{10,... | collective-permute-start | bytes 1572872 | tf_op jit(solution)/shard_map/ppermute | solution.py:33
  494.1 202.3 %collective-permute-start.125 = (bf16[2,2,176,2048]{3,2,1,0:T(8,128)(2,1)}, bf16[2,2,176,2048]{3,2,1,0:T(8,128)(2,1)}, u32[]{:S(2)}, u32[]{:S(2)}) collective-permute-start(bf16[2,2,176,2048]{3,2,1,0:T(8,128)(2,1)} %dynamic-slice_bitcast_fusion), channel_id=1, source_target_pairs={{0,8},{8,0},{1,9},{9,1},{2,10},{10,2},{3,11},{11,3},{4,12},{12,4},... | collective-permute-start | bytes 8650760 | tf_op jit(solution)/shard_map/ppermute | solution.py:29
  520.4 183.3 %collective-permute-start.119 = (bf16[2,2,256,1408]{3,2,1,0:T(8,128)(2,1)}, bf16[2,2,256,1408]{3,2,1,0:T(8,128)(2,1)}, u32[]{:S(2)}, u32[]{:S(2)}) collective-permute-start(bf16[2,2,256,1408]{3,2,1,0:T(8,128)(2,1)} %dynamic-slice_bitcast_fusion.1), channel_id=1, source_target_pairs={{0,8},{8,0},{1,9},{9,1},{2,10},{10,2},{3,11},{11,3},{4,12},{12,4},... | collective-permute-start | bytes 8650760 | tf_op jit(solution)/shard_map/ppermute | solution.py:29
  547.3 61.0 %collective-permute-start.80 = (bf16[128,2048]{1,0:T(8,128)(2,1)}, bf16[128,2048]{1,0:T(8,128)(2,1)}, u32[]{:S(2)}, u32[]{:S(2)}) collective-permute-start(bf16[128,2048]{1,0:T(8,128)(2,1)} %get-tuple-element.55), channel_id=1, source_target_pairs={{0,1},{1,0},{2,3},{3,2},{4,5},{5,4},{6,7},{7,6},{8,9},{9,8},{10,11... | collective-permute-start | bytes 1572872 | tf_op jit(solution)/shard_map/ppermute | solution.py:33
  548.3 61.1 %collective-permute-start.81 = (bf16[128,2048]{1,0:T(8,128)(2,1)}, bf16[128,2048]{1,0:T(8,128)(2,1)}, u32[]{:S(2)}, u32[]{:S(2)}) collective-permute-start(bf16[128,2048]{1,0:T(8,128)(2,1)} %get-tuple-element.56), channel_id=1, source_target_pairs={{0,2},{1,3},{2,0},{3,1},{4,6},{5,7},{6,4},{7,5},{8,10},{9,11},{10,... | collective-permute-start | bytes 1572872 | tf_op jit(solution)/shard_map/ppermute | solution.py:33
  557.8 51.7 %collective-permute-start.82 = (bf16[128,2048]{1,0:T(8,128)(2,1)S(1)}, bf16[128,2048]{1,0:T(8,128)(2,1)}, u32[]{:S(2)}, u32[]{:S(2)}) collective-permute-start(bf16[128,2048]{1,0:T(8,128)(2,1)S(1)} %get-tuple-element.57), channel_id=1, source_target_pairs={{0,3},{1,2},{2,1},{3,0},{4,7},{5,6},{6,5},{7,4},{8,11},{9,10},{10,... | collective-permute-start | bytes 1572872 | tf_op jit(solution)/shard_map/ppermute | solution.py:33
  644.4 66.9 %collective-permute-start.113 = (bf16[2,2,256,1408]{3,2,1,0:T(8,128)(2,1)}, bf16[2,2,256,1408]{3,2,1,0:T(8,128)(2,1)}, u32[]{:S(2)}, u32[]{:S(2)}) collective-permute-start(bf16[2,2,256,1408]{3,2,1,0:T(8,128)(2,1)} %dynamic-slice_bitcast_fusion.2), channel_id=1, source_target_pairs={{0,8},{8,0},{1,9},{9,1},{2,10},{10,2},{3,11},{11,3},{4,12},{12,4},... | collective-permute-start | bytes 8650760 | tf_op jit(solution)/shard_map/ppermute | solution.py:29
  688.5 85.4 %collective-permute-start.102 = (bf16[64,2048]{1,0:T(8,128)(2,1)S(1)}, bf16[64,2048]{1,0:T(8,128)(2,1)S(1)}, u32[]{:S(2)}, u32[]{:S(2)}) collective-permute-start(bf16[64,2048]{1,0:T(8,128)(2,1)S(1)} %fusion.37), channel_id=1, source_target_pairs={{0,0},{4,1},{8,2},{12,3},{16,4},{20,5},{24,6},{28,7},{1,8},{5,9},{... | collective-permute-start | bytes 786440 | tf_op jit(solution)/shard_map/ppermute | solution.py:633
  696.4 65.7 %collective-permute-start.88 = (bf16[2,256,768]{2,1,0:T(8,128)(2,1)S(1)}, bf16[2,256,768]{2,1,0:T(8,128)(2,1)S(1)}, u32[]{:S(2)}, u32[]{:S(2)}) collective-permute-start(bf16[2,256,768]{2,1,0:T(8,128)(2,1)S(1)} %fusion.30), channel_id=1, source_target_pairs={{0,4},{4,0},{1,5},{5,1},{2,6},{6,2},{3,7},{7,3},{8,12},{12,8},{9,1... | collective-permute-start | bytes 2359304 | tf_op jit(solution)/shard_map/ppermute | solution.py:29
  705.2 125.4 %collective-permute-start.126 = (bf16[2,176,2048]{2,1,0:T(8,128)(2,1)}, bf16[2,176,2048]{2,1,0:T(8,128)(2,1)}, u32[]{:S(2)}, u32[]{:S(2)}) collective-permute-start(bf16[2,176,2048]{2,1,0:T(8,128)(2,1)} %fusion.5), channel_id=1, source_target_pairs={{0,16},{16,0},{1,17},{17,1},{2,18},{18,2},{3,19},{19,3},{4,20},{20... | collective-permute-start | bytes 4325384 | tf_op jit(solution)/shard_map/ppermute | solution.py:29
  708.9 152.6 %collective-permute-start.120 = (bf16[2,256,1408]{2,1,0:T(8,128)(2,1)}, bf16[2,256,1408]{2,1,0:T(8,128)(2,1)}, u32[]{:S(2)}, u32[]{:S(2)}) collective-permute-start(bf16[2,256,1408]{2,1,0:T(8,128)(2,1)} %fusion.4), channel_id=1, source_target_pairs={{0,4},{4,0},{1,5},{5,1},{2,6},{6,2},{3,7},{7,3},{8,12},{12,8},{9,1... | collective-permute-start | bytes 4325384 | tf_op jit(solution)/shard_map/ppermute | solution.py:29
  711.3 57.7 %collective-permute-start.94 = (bf16[2,256,784]{1,2,0:T(8,128)(2,1)S(1)}, bf16[2,256,784]{1,2,0:T(8,128)(2,1)S(1)}, u32[]{:S(2)}, u32[]{:S(2)}) collective-permute-start(bf16[2,256,784]{1,2,0:T(8,128)(2,1)S(1)} %fusion.29), channel_id=1, source_target_pairs={{0,16},{16,0},{1,17},{17,1},{2,18},{18,2},{3,19},{19,3},{4,20},{20... | collective-permute-start | bytes 2408456 | tf_op jit(solution)/shard_map/ppermute | solution.py:29
  769.2 40.4 %collective-permute-start.95 = (bf16[256,784]{0,1:T(8,128)(2,1)S(1)}, bf16[256,784]{0,1:T(8,128)(2,1)S(1)}, u32[]{:S(2)}, u32[]{:S(2)}) collective-permute-start(bf16[256,784]{0,1:T(8,128)(2,1)S(1)} %fusion.38), channel_id=1, source_target_pairs={{0,4},{4,0},{1,5},{5,1},{2,6},{6,2},{3,7},{7,3},{8,12},{12,8},{9,1... | collective-permute-start | bytes 1204232 | tf_op jit(solution)/shard_map/ppermute | solution.py:29
  777.4 42.5 %collective-permute-start.91 = (bf16[64,768]{1,0:T(8,128)(2,1)S(1)}, bf16[64,768]{1,0:T(8,128)(2,1)S(1)}, u32[]{:S(2)}, u32[]{:S(2)}) collective-permute-start(bf16[64,768]{1,0:T(8,128)(2,1)S(1)} %get-tuple-element.158), channel_id=1, source_target_pairs={{0,2},{1,3},{2,0},{3,1},{4,6},{5,7},{6,4},{7,5},{8,10},{9,11},{10,... | collective-permute-start | bytes 294920 | tf_op jit(solution)/shard_map/ppermute | solution.py:33
  834.1 45.3 %collective-permute-start.127 = (bf16[176,2048]{1,0:T(8,128)(2,1)S(1)}, bf16[176,2048]{1,0:T(8,128)(2,1)S(1)}, u32[]{:S(2)}, u32[]{:S(2)}) collective-permute-start(bf16[176,2048]{1,0:T(8,128)(2,1)S(1)} %fusion.33), channel_id=1, source_target_pairs={{0,4},{4,0},{1,5},{5,1},{2,6},{6,2},{3,7},{7,3},{8,12},{12,8},{9,1... | collective-permute-start | bytes 2162696 | tf_op jit(solution)/shard_map/ppermute | solution.py:29
  863.3 53.4 %collective-permute-start.121 = (bf16[256,1408]{1,0:T(8,128)(2,1)S(1)}, bf16[256,1408]{1,0:T(8,128)(2,1)S(1)}, u32[]{:S(2)}, u32[]{:S(2)}) collective-permute-start(bf16[256,1408]{1,0:T(8,128)(2,1)S(1)} %fusion.32), channel_id=1, source_target_pairs={{0,16},{16,0},{1,17},{17,1},{2,18},{18,2},{3,19},{19,3},{4,20},{20... | collective-permute-start | bytes 2162696 | tf_op jit(solution)/shard_map/ppermute | solution.py:29
  879.6 56.1 %collective-permute-start.128 = (bf16[176,2048]{1,0:T(8,128)(2,1)S(1)}, bf16[176,2048]{1,0:T(8,128)(2,1)S(1)}, u32[]{:S(2)}, u32[]{:S(2)}) collective-permute-start(bf16[176,2048]{1,0:T(8,128)(2,1)S(1)} %fusion.6), channel_id=1, source_target_pairs={{0,0},{4,1},{8,2},{12,3},{16,4},{20,5},{24,6},{28,7},{1,8},{5,9},{... | collective-permute-start | bytes 2162696 | tf_op jit(solution)/shard_map/ppermute | solution.py:610
  (175 other events, 3090.6 us)

commit v2 on v1

--- a/solution.py
+++ b/solution.py
@@ -10,9 +10,11 @@
 VAL = 512
 SPAN = 64
 RANK = 16
+LANES = 128
 EPS = 1e-05
 FLOOR = 1.0
 QSCALE = KEY**-0.5
+KEYS, VALUES, GATES, RANKS = KEY, 2 * KEY, 2 * KEY + VAL, 2 * KEY + 2 * VAL
 
 AXES = ("y", "c", "h", "p", "q")
 COPIES = ("y", "c", "h")
@@ -23,6 +25,10 @@
 
 def after(value, *deps):
     return lax.optimization_barrier((value, deps))[0]
+
+
+def together(*values):
+    return lax.optimization_barrier(values)
 
 
 def swap(value, axis):
@@ -50,14 +56,8 @@
     return jnp.where(first, jnp.stack([value, other]), jnp.stack([other, value]))
 
 
-def gather_all(value):
-    for axis in AXES[::-1]:
-        value = stack_axis(value, axis)
-    return value
-
-
 def sum_all(value):
-    for axis in ("q", "p", "c", "h", "y"):
+    for axis in ("q", "p", "c", "y", "h"):
         if lax.axis_size(axis) == 2:
             value = value + swap(value, axis)
         else:
@@ -69,44 +69,111 @@
     return all(lax.axis_size(axis) == 2 for axis in COPIES)
 
 
-def join(first, one, two):
-    return jnp.where(first, jnp.concatenate([one, two]), jnp.concatenate([two, one]))
-
-
-def gather_copies(block, chain):
+def half_swap(block):
+    return swap(block, "h") if binary_copies() else block
+
+
+def near_copies(block):
+    return (swap(block, "y"), swap(block, "c")) if binary_copies() else (block, block)
+
+
+def core_swap(block):
+    return swap(block, "c") if binary_copies() else block
+
+
+def lay_kernel(count, slots, *refs):
+    blocks, whole, sems = refs[:count], refs[count], refs[count + 1]
+    copies = [
+        pltpu.make_async_copy(blocks[i], whole.at[slots[i]], sems.at[i]) for i in range(count)
+    ]
+    for copy in copies:
+        copy.start()
+    for copy in copies:
+        copy.wait()
+
+
+def lay(blocks, slots):
+    count, (rows, cols), kind = len(blocks), blocks[0].shape, blocks[0].dtype
+    size = count * rows * cols * kind.itemsize
+    whole = pl.pallas_call(
+        lambda *refs: lay_kernel(count, *refs),
+        grid_spec=pltpu.PrefetchScalarGridSpec(
+            num_scalar_prefetch=1,
+            grid=(1,),
+            in_specs=[pl.BlockSpec(memory_space=pl.ANY)] * count,
+            out_specs=pl.BlockSpec(memory_space=pl.ANY),
+            scratch_shapes=[pltpu.SemaphoreType.DMA((count,))],
+        ),
+        out_shape=jax.ShapeDtypeStruct((count, rows, cols), kind),
+        compiler_params=pltpu.CompilerParams(vmem_limit_bytes=16 * 1024 * 1024),
+        cost_estimate=pl.CostEstimate(flops=0, bytes_accessed=2 * size, transcendentals=0),
+    )(jnp.stack(slots).astype(jnp.int32), *blocks)
+    return whole.reshape(count * rows, cols)
+
+
+def in_order(blocks):
+    return lay(blocks, [jnp.int32(i) for i in range(len(blocks))])
+
+
+def all_copies(block, parts, tall=False):
     if not binary_copies():
-        return lax.all_gather(block, COPIES, axis=0, tiled=True), chain
-    block = after(block, chain) if chain is not None else block
-    from_h = swap(block, "h")
-    from_y = swap(block, "y")
-    from_hy = swap(from_h, "y")
-    mine = [block, from_h, from_y, from_hy]
-    core = [swap(part, "c") for part in mine]
-    h0, c0, y0 = (lax.axis_index(axis) == 0 for axis in ("h", "c", "y"))
-    near = join(c0, join(h0, mine[0], mine[1]), join(h0, core[0], core[1]))
-    far = join(c0, join(h0, mine[2], mine[3]), join(h0, core[2], core[3]))
-    return join(y0, near, far), from_h
+        return lax.all_gather(block, COPIES, axis=0, tiled=True)
+    h, c, y = (lax.axis_index(axis) for axis in ("h", "c", "y"))
+    flips = [(0, 0, 0), (1, 0, 0), (0, 1, 0), (1, 1, 0), (0, 0, 1), (1, 0, 1), (0, 1, 1), (1, 1, 1)]
+    slots = []
+    for fy, fc, fh in flips:
+        ty, tc, th = y ^ fy, c ^ fc, h ^ fh
+        slots.append(th * 4 + ty * 2 + tc if tall else ty * 4 + tc * 2 + th)
+    return lay((block,) + tuple(parts), slots)
 
 
 def pick(value, index, axis):
     return lax.dynamic_index_in_dim(value, index, axis, keepdims=False)
 
 
-def scatter_copies(grad, order=("c", "y", "h")):
-    sizes = [lax.axis_size(axis) for axis in COPIES]
-    rows = grad.shape[0] // (sizes[0] * sizes[1] * sizes[2])
-    value = grad.reshape(*sizes, rows, grad.shape[1])
-    left = list(COPIES)
-    for axis in order:
-        dim = left.index(axis)
-        if lax.axis_size(axis) == 2:
-            mine = lax.axis_index(axis)
-            keep = pick(value, mine, dim).astype(f32)
-            value = keep + swap(pick(value, 1 - mine, dim).astype(bf16), axis).astype(f32)
+def copies_part(value, y, tall):
+    ys, hs = lax.axis_size("y"), lax.axis_size("h")
+    c = lax.axis_index("c")
+    rows, cols = value.shape
+    if tall and binary_copies():
+        return pick(pick(value.reshape(hs, ys, 2, -1, cols), y, 1), c, 1)
+    part = rows // (2 * ys)
+    return lax.dynamic_slice_in_dim(value, (y * 2 + c) * part, part, 0).reshape(hs, -1, cols)
+
+
+class Summing:
+    def __init__(self, grad, tall=False):
+        self.grad, self.tall = grad, tall
+        self.from_c = swap(grad, "c")
+
+    def of(self, y):
+        one = copies_part(self.grad, y, self.tall).astype(f32)
+        return one + copies_part(self.from_c, y, self.tall).astype(f32)
+
+    def send_y(self):
+        mine = lax.axis_index("y")
+        if lax.axis_size("y") == 2:
+            self.from_y = swap(self.of(1 - mine).astype(bf16), "y")
         else:
-            value = lax.psum_scatter(value.astype(bf16), axis, scatter_dimension=dim).astype(f32)
-        left.remove(axis)
-    return value
+            parts = jnp.stack([self.of(y) for y in range(lax.axis_size("y"))])
+            self.from_y = lax.psum_scatter(parts.astype(bf16), "y", scatter_dimension=0)
+
+    def near(self):
+        if lax.axis_size("y") == 2:
+            return self.of(lax.axis_index("y")) + self.from_y.astype(f32)
+        return self.from_y.astype(f32)
+
+    def send_h(self):
+        mine = lax.axis_index("h")
+        if lax.axis_size("h") == 2:
+            self.from_h = swap(pick(self.near(), 1 - mine, 0).astype(bf16), "h")
+        else:
+            self.from_h = lax.psum_scatter(self.near().astype(bf16), "h", scatter_dimension=0)
+
+    def total(self):
+        if lax.axis_size("h") == 2:
+            return pick(self.near(), lax.axis_index("h"), 0) + self.from_h.astype(f32)
+        return self.from_h.astype(f32)
 
 
 def share_columns(weight, place, columns):
@@ -122,16 +189,31 @@
 
 def return_columns(grad, place):
     value = grad.reshape(4, grad.shape[0] // 4, grad.shape[1])
-    got = [pick(value, place, 0)]
+    got = [pick(value, place, 0).astype(f32)]
     for mask in (1, 2, 3):
         got.append(across(pick(value, place ^ mask, 0).astype(bf16), mask).astype(f32))
     return [lax.select_n(place, *[got[t ^ spot] for t in range(4)]) for spot in range(4)]
+
+
+def reduce_copies(grad):
+    return lax.psum_scatter(grad, COPIES, scatter_dimension=0, tiled=True)
+
+
+def reduce_tall(grad):
+    axes = ("h", "y", "c") if binary_copies() else COPIES
+    return lax.psum_scatter(grad, axes, scatter_dimension=0, tiled=True)
 
 
 def row_owner_moves():
     total = 1
     for axis in AXES:
         total *= lax.axis_size(axis)
+    if binary_copies():
+        pairs = []
+        for g in range(total):
+            yc, h, pq = g // 8, g // 4 % 2, g % 4
+            pairs.append((g, pq * 8 + h * 4 + yc))
+        return pairs
     copies = total // 4
     return [(g, (g % copies) * 4 + g // copies) for g in range(total)]
 
@@ -170,15 +252,15 @@
 
 
 def states_kernel(
-    place, kvr, up, bias, meta, rows, sums, raw, prior, through, end, decay, state, total
+    place, proj, up, bias, meta, rows, sums, raw, prior, through, end, decay, state, total
 ):
     @pl.when(pl.program_id(0) == 0)
     def _():
         state[...] = jnp.zeros_like(state)
         total[...] = jnp.ones_like(total)
 
-    keys = kvr[:, :KEY].astype(f32)
-    gate = dot_nn(kvr[:, KEY + VAL :], up[...]) + bias[...]
+    keys = proj[:, KEYS:VALUES].astype(bf16).astype(f32)
+    gate = dot_nn(proj[:, RANKS:].astype(bf16), up[...]) + bias[...]
     log_decay = (jnp.minimum(gate, 0.0) - jnp.log1p(jnp.exp(-jnp.abs(gate)))) * (1.0 / 16.0)
     run = running_sum(log_decay, True)
     raw[...] = gate
@@ -189,23 +271,23 @@
     step = rows[0, 1:2, 0:1] * jnp.exp(last)
     prior[0] = state[...].astype(bf16)
     through[0] = total[...]
-    state[...] = step * state[...] + dot_tn(kvr[:, KEY : KEY + VAL], k_final)
+    state[...] = step * state[...] + dot_tn(proj[:, VALUES:GATES].astype(bf16), k_final)
     total[...] = step * total[...]
     end[...] = state[...].astype(bf16)
     decay[...] = total[...]
 
 
-def mixed_kernel(place, kvr, qog, sums, prior, through, entering, gain, meta, rows, gated, mixed):
+def mixed_kernel(place, proj, sums, prior, through, entering, gain, meta, rows, gated, mixed):
     info = meta[...]
     run = sums[...]
-    query = qog[:, :KEY].astype(bf16).astype(f32)
+    query = proj[:, :KEYS].astype(bf16).astype(f32)
     q_decay = (query * QSCALE * jnp.exp(run)).astype(bf16)
-    k_decay = (kvr[:, :KEY].astype(f32) * info[:, 1:2] * jnp.exp(-run)).astype(bf16)
+    k_decay = (proj[:, KEYS:VALUES].astype(bf16).astype(f32) * info[:, 1:2] * jnp.exp(-run)).astype(bf16)
     scores = (dot_nt(q_decay, k_decay) * pair_mask(info, rows[0])).astype(bf16)
     state = (prior[0].astype(f32) + through[0] * entering[...].astype(f32)).astype(bf16)
-    out = dot_nn(scores, kvr[:, KEY : KEY + VAL]) + info[:, 2:3] * dot_nt(q_decay, state)
+    out = dot_nn(scores, proj[:, VALUES:GATES].astype(bf16)) + info[:, 2:3] * dot_nt(q_decay, state)
     mixed[...] = out
-    gate = qog[:, KEY:]
+    gate = proj[:, GATES:RANKS]
     scale = lax.rsqrt(jnp.mean(out * out, axis=-1, keepdims=True) + FLOOR)
     gated[...] = (out * scale * gain[...] * gate * jax.nn.sigmoid(gate)).astype(bf16)
 
@@ -213,7 +295,7 @@
 def gate_grad_kernel(
     place,
     grad_gated,
-    qog,
+    proj,
     mixed,
     sums,
     gain,
@@ -238,7 +320,7 @@
     info = meta[...]
     run = sums[...]
     out = mixed[...]
-    gate = qog[:, KEY:]
+    gate = proj[:, GATES:RANKS]
     grad = grad_gated[...]
     sig = jax.nn.sigmoid(gate)
     scale = lax.rsqrt(jnp.mean(out * out, axis=-1, keepdims=True) + FLOOR)
@@ -250,7 +332,7 @@
     grad_out[...] = grad_o
     grad_gate[...] = (grad * scaled * gain[...] * sig * (1.0 + gate * (1.0 - sig))).astype(bf16)
     grad_gain[...] += jnp.sum(grad * scaled * swish, axis=0, keepdims=True)
-    query = qog[:, :KEY].astype(bf16).astype(f32)
+    query = proj[:, :KEYS].astype(bf16).astype(f32)
     q_enter = (query * QSCALE * jnp.exp(run)).astype(bf16)
     o_enter = jnp.where(info[:, 2:3] > 0.0, grad_o.astype(f32), 0.0).astype(bf16)
     step = rows[0, 1:2, 0:1] * jnp.exp(run[SPAN - 1 :, :])
@@ -264,8 +346,7 @@
 
 def inputs_grad_kernel(
     place,
-    kvr,
-    qog,
+    proj,
     sums,
     raw,
     grad_out,
@@ -279,8 +360,7 @@
     up,
     meta,
     rows,
-    grad_kvr,
-    grad_qog,
+    grad_proj,
     grad_up,
     grad_bias,
 ):
@@ -294,9 +374,9 @@
     last = run[SPAN - 1 :, :]
     valid, enter, carry = info[:, 1:2], info[:, 2:3], info[:, 3:4]
     grow, shrink, tail = jnp.exp(run), jnp.exp(-run), jnp.exp(last - run) * carry
-    query = qog[:, :KEY].astype(bf16).astype(f32)
-    keys = kvr[:, :KEY].astype(f32) * valid
-    values = kvr[:, KEY : KEY + VAL]
+    query = proj[:, :KEYS].astype(bf16).astype(f32)
+    keys = proj[:, KEYS:VALUES].astype(bf16).astype(f32) * valid
+    values = proj[:, VALUES:GATES].astype(bf16)
     q_decay = (query * QSCALE * grow).astype(bf16)
     k_decay = (keys * shrink).astype(bf16)
     k_final = (keys * tail).astype(bf16)
@@ -319,16 +399,16 @@
     grad_log = running_sum(grad_run, False) + grad_last
     grad_raw = grad_log * jax.nn.sigmoid(-raw[...]) * (1.0 / 16.0)
     high, low = two_parts(grad_raw)
-    rank = kvr[:, KEY + VAL :]
+    rank = proj[:, RANKS:].astype(bf16)
     grad_up[...] += dot_tn(rank, high) + dot_tn(rank, low)
     grad_bias[...] += jnp.sum(grad_raw, axis=0, keepdims=True)
     grad_rank = dot_nt(high, up[...]) + dot_nt(low, up[...])
     grad_k = (grad_kd * shrink + grad_kf * tail) * valid
-    grad_kvr[:, :KEY] = grad_k.astype(bf16)
-    grad_kvr[:, KEY : KEY + VAL] = grad_v.astype(bf16)
-    grad_kvr[:, KEY + VAL :] = grad_rank.astype(bf16)
-    grad_qog[:, :KEY] = (grad_qd * grow * QSCALE).astype(bf16)
-    grad_qog[:, KEY:] = grad_gate[...]
+    grad_proj[:, KEYS:VALUES] = grad_k.astype(bf16)
+    grad_proj[:, VALUES:GATES] = grad_v.astype(bf16)
+    grad_proj[:, RANKS:] = grad_rank.astype(bf16)
+    grad_proj[:, :KEYS] = (grad_qd * grow * QSCALE).astype(bf16)
+    grad_proj[:, GATES:RANKS] = grad_gate[...]
 
 
 class Mixer:
@@ -401,27 +481,12 @@
     return dot_tn(left, right).astype(out)
 
 
-def kvr_columns(weight, t):
-    wide = HEADS * KEY
-    return jnp.concatenate(
-        [
-            weight[:, wide + t * KEY : wide + (t + 1) * KEY],
-            weight[:, 2 * wide + t * VAL : 2 * wide + (t + 1) * VAL],
-            weight[:, 2 * wide + 2 * HEADS * VAL :],
-        ],
-        axis=1,
-    )
-
-
-def qog_columns(weight, t):
-    start = 2 * HEADS * KEY + HEADS * VAL
-    return jnp.concatenate(
-        [
-            weight[:, t * KEY : (t + 1) * KEY],
-            weight[:, start + t * VAL : start + (t + 1) * VAL],
-        ],
-        axis=1,
-    )
+def in_columns(weight, t):
+    wide, tall = HEADS * KEY, HEADS * VAL
+    starts = [(0, KEY), (wide, KEY), (2 * wide, VAL), (2 * wide + tall, VAL)]
+    heads = [weight[:, start + t * size : start + (t + 1) * size] for start, size in starts]
+    rank = weight[:, 2 * wide + 2 * tall :]
+    return jnp.concatenate(heads + [jnp.pad(rank, ((0, 0), (0, LANES - RANK)))], axis=1)
 
 
 def from_earlier(end, decay):
@@ -493,15 +558,54 @@
     packed = jnp.concatenate(small)
     padded = -(-packed.shape[0] // 1024) * 1024
     packed = jnp.pad(packed, (0, padded - packed.shape[0])).reshape(-1, 128)
-    everyone = gather_all(packed).reshape(sizes[0], sizes[1], -1, padded)
     offset = [sum(lengths[:i]) for i in range(len(lengths) + 1)]
+
+    def gateup_columns(weight, t):
+        return jnp.concatenate(
+            [
+                weight[:, t * quarter : (t + 1) * quarter],
+                weight[:, ff + t * quarter : ff + (t + 1) * quarter],
+            ],
+            axis=1,
+        )
+
+    moves = row_owner_moves()
+    back = [(b, a) for a, b in moves]
+
+    in_rows = share_columns(in_weight, place, in_columns)
+    for axis in ("q", "p", "c", "y", "h"):
+        packed = stack_axis(packed, axis)
+    packed = jnp.moveaxis(packed, 0, 2)
+    in_rows, packed, ffn_in, out_weight = together(in_rows, packed, ffn_in, out_weight)
+    in_h = half_swap(in_rows)
+    in_y, in_c = near_copies(in_rows)
+    gateup_rows = share_columns(ffn_in, place, gateup_columns)
+    out_rows = lax.ppermute(out_weight, AXES, moves)
+    in_h, in_y, in_c, gateup_rows, out_rows, x_send = together(
+        in_h, in_y, in_c, gateup_rows, out_rows, x_own
+    )
+    in_hy, in_hc = near_copies(in_h)
+    in_yc = core_swap(in_y)
+    x_group = gather_group(x_send)
+    out_h = half_swap(out_rows)
+    out_y, out_c = near_copies(out_rows)
+    in_hy, in_hc, in_yc, x_group, out_h, out_y, out_c, ffn_out, gateup_rows, dy_send = together(
+        in_hy, in_hc, in_yc, x_group, out_h, out_y, out_c, ffn_out, gateup_rows, dy_own
+    )
+    w_gateup = lax.all_gather(gateup_rows, COPIES, axis=0, tiled=True)
+    in_hyc = core_swap(in_hy)
+    down_rows = lax.ppermute(ffn_out, AXES, moves)
+    dy_group = gather_group(dy_send)
+    out_hy, out_hc = near_copies(out_h)
+    out_yc = core_swap(out_y)
+    everyone = packed.reshape(sizes[0], sizes[1], -1, padded)
 
     def small_part(i):
         return everyone[..., offset[i] : offset[i + 1]]
 
     up_cols = decay_up.shape[1]
     up_all = small_part(0).reshape(devices, RANK, up_cols).transpose(1, 0, 2).reshape(RANK, HEADS, KEY)
-    up_head = pick(up_all, place, 1)
+    up_head = jnp.pad(pick(up_all, place, 1), ((0, LANES - RANK), (0, 0)))
     bias_head = pick(small_part(1).reshape(HEADS, 1, KEY), place, 0).astype(f32)
     gain_one = small_part(2).reshape(-1).astype(f32)
     gain_head = small_part(3).reshape(1, -1).astype(f32)
@@ -533,34 +637,17 @@
     keep = jnp.broadcast_to((final == before).astype(f32), (count, SPAN))
     rows = jnp.stack([seg_blocks, keep] + [jnp.zeros((count, SPAN), f32)] * 6, axis=1)
 
-    kvr_rows = share_columns(in_weight, place, kvr_columns)
-    qog_rows = share_columns(in_weight, place, qog_columns)
-    w_kvr, chain = gather_copies(kvr_rows, None)
-    w_qog, chain = gather_copies(qog_rows, chain)
-    x_group = jnp.concatenate(gather_group(after(x_own, qog_rows)))
-    moves = row_owner_moves()
-    back = [(b, a) for a, b in moves]
-    w_out, chain = gather_copies(lax.ppermute(out_weight, AXES, moves), chain)
-    dy_group = jnp.concatenate(gather_group(after(dy_own, x_group)))
-    ffn_late = after(ffn_in, x_group)
-    gate_rows = share_columns(ffn_late, place, lambda w, t: w[:, t * quarter : (t + 1) * quarter])
-    up_rows = share_columns(
-        ffn_late, place, lambda w, t: w[:, ff + t * quarter : ff + (t + 1) * quarter]
-    )
-    down_rows = lax.ppermute(ffn_out, AXES, moves)
-    w_down, chain = gather_copies(down_rows, chain)
-    w_gate, chain = gather_copies(gate_rows, chain)
-    w_up, chain = gather_copies(up_rows, chain)
-
+    x_group = in_order(x_group)
+    w_in = all_copies(in_rows, (in_y, in_c, in_yc, in_h, in_hy, in_hc, in_hyc))
     n1 = normed(x_group.astype(f32), gain_one).astype(bf16)
-    kvr = mm(n1, w_kvr, bf16)
+    proj = mm(n1, w_in)
     mixer = Mixer(place, count, tokens // SPAN)
     state_shape = (VAL, KEY)
     scratch = [pltpu.VMEM(state_shape, f32), pltpu.VMEM((1, KEY), f32)]
     sums, raw, prior, through, end, decay = mixer.call(
         states_kernel,
         ["rows", "whole", "whole", "tokens", "blocks"],
-        [kvr, up_head, bias_head, meta, rows],
+        [proj, up_head, bias_head, meta, rows],
         [
             ("rows", (rows_all, KEY), f32),
             ("rows", (rows_all, KEY), f32),
@@ -572,49 +659,60 @@
         scratch,
         flops=2 * rows_all * KEY * VAL,
     )
+    end, down_rows, out_hy, out_hc, out_yc, dy_group = together(
+        end, down_rows, out_hy, out_hc, out_yc, dy_group
+    )
     entering = from_earlier(end, decay)
-    qog = mm(n1, w_qog)
+    out_hyc = core_swap(out_hy)
+    entering, out_hyc, down_rows = together(entering, out_hyc, down_rows)
+    w_out = all_copies(out_rows, (out_y, out_c, out_yc, out_h, out_hy, out_hc, out_hyc), True)
+    down_h = half_swap(down_rows)
+    down_y, down_c = near_copies(down_rows)
     gated, mixed = mixer.call(
         mixed_kernel,
-        ["rows", "rows", "rows", "blocks", "blocks", "whole", "whole", "tokens", "blocks"],
-        [kvr, qog, sums, prior, through, entering, gain_head, meta, rows],
+        ["rows", "rows", "blocks", "blocks", "whole", "whole", "tokens", "blocks"],
+        [proj, sums, prior, through, entering, gain_head, meta, rows],
         [("rows", (rows_all, VAL), bf16), ("rows", (rows_all, VAL), f32)],
         flops=2 * rows_all * (KEY * VAL + SPAN * (KEY + VAL)),
     )
     mix_parts = mm(gated, w_out).reshape(4, tokens, width)
     mix = scatter_group([mix_parts[m] for m in range(4)])
+    mix, down_h, down_y, down_c = together(mix, down_h, down_y, down_c)
     h1 = x_own.astype(f32) + mix
-
+    n2_group = gather_group(normed(h1, gain_two).astype(bf16))
+    down_hy, down_hc = near_copies(down_h)
+    down_yc = core_swap(down_y)
+    n2_group, down_hy, down_hc, down_yc = together(n2_group, down_hy, down_hc, down_yc)
+    down_hyc = core_swap(down_hy)
+    w_down = all_copies(
+        down_rows, (down_y, down_c, down_yc, down_h, down_hy, down_hc, down_hyc), True
+    )
+    n2_group = in_order(n2_group)
+    dy_group = in_order(dy_group)
     grad_hidden = mm_nt(dy_group, w_down)
-    n2 = normed(h1, gain_two).astype(bf16)
-    n2_group = jnp.concatenate(gather_group(n2))
-    gate = mm(n2_group, w_gate)
-    up = mm(n2_group, w_up)
+
+    gateup = mm(n2_group, w_gateup)
+    gate, up = gateup[:, :quarter], gateup[:, quarter:]
     sig = jax.nn.sigmoid(gate)
     hidden = (gate * sig * up).astype(bf16)
+    grad_gu = jnp.concatenate(
+        [grad_hidden * up * sig * (1.0 + gate * (1.0 - sig)), grad_hidden * gate * sig], axis=1
+    ).astype(bf16)
+    n2_grad_parts = mm_nt(grad_gu, w_gateup).reshape(4, tokens, width)
+    grad_gu, hidden, n2_grad_parts = together(grad_gu, hidden, n2_grad_parts)
+    n2_grad = scatter_group([n2_grad_parts[m] for m in range(4)])
     y_parts = mm(hidden, w_down).reshape(4, tokens, width)
-    grad_g = (grad_hidden * up * sig * (1.0 + gate * (1.0 - sig))).astype(bf16)
-    grad_u = (grad_hidden * gate * sig).astype(bf16)
-    n2_grad_parts = (mm_nt(grad_g, w_gate) + mm_nt(grad_u, w_up)).reshape(4, tokens, width)
-    n2_grad = scatter_group([n2_grad_parts[m] for m in range(4)])
+    gateup_sum = reduce_copies(mm_tn(n2_group, grad_gu, bf16))
+    down_sum = reduce_tall(mm_tn(hidden, dy_group, bf16))
+
     h1_grad_part, gain_two_grad = normed_grad(h1, gain_two, n2_grad)
     h1_grad = dy_own.astype(f32) + h1_grad_part
-    mix_grad = jnp.concatenate(gather_group(h1_grad.astype(bf16)))
-
-    down_grad = mm_tn(hidden, dy_group, bf16)
-    gate_w_grad = mm_tn(n2_group, grad_g, bf16)
-    up_w_grad = mm_tn(n2_group, grad_u, bf16)
-    down_sum = scatter_copies(down_grad)
-    gate_sum = scatter_copies(gate_w_grad)
-    up_sum = scatter_copies(up_w_grad, ("c", "h", "y"))
-    ffnout_grad = lax.ppermute(down_sum.astype(bf16), AXES, back).astype(f32)
-    ffnin_grad = jnp.concatenate(return_columns(gate_sum, place) + return_columns(up_sum, place), axis=1)
-
+    mix_grad = in_order(gather_group(h1_grad.astype(bf16)))
     grad_gated = mm_nt(mix_grad, w_out)
     grad_o, grad_gate, later, beyond, start, decay_b, head_grad = mixer.call(
         gate_grad_kernel,
         ["rows", "rows", "rows", "rows", "whole", "tokens", "blocks"],
-        [grad_gated, qog, mixed, sums, gain_head, meta, rows],
+        [grad_gated, proj, mixed, sums, gain_head, meta, rows],
         [
             ("rows", (rows_all, VAL), bf16),
             ("rows", (rows_all, VAL), bf16),
@@ -629,23 +727,15 @@
         flops=2 * rows_all * KEY * VAL,
     )
     leaving = from_later(start, decay_b)
-    out_w_grad = mm_tn(gated, mix_grad, bf16)
-    outproj_grad = lax.ppermute(scatter_copies(out_w_grad).astype(bf16), AXES, back).astype(f32)
-
     y = scatter_group([after(y_parts[m], mix_grad) for m in range(4)])
-    result = h1 + y
-    block_out = result.astype(bf16).reshape(1, tokens, width)
-    live = valid_mask.reshape(tokens, 1).astype(f32)
-    squares = jnp.stack(
-        [jnp.sum(live * result * result), jnp.sum(live * mix * mix), jnp.sum(live * y * y)]
-    )
-
-    grad_kvr, grad_qog, up_grad, bias_grad = mixer.call(
+    out_sum = Summing(mm_tn(gated, mix_grad, bf16), True)
+    leaving, out_sum.from_c = together(leaving, out_sum.from_c)
+    out_sum.send_y()
+    grad_proj, rank_grad, bias_grad = mixer.call(
         inputs_grad_kernel,
-        ["rows"] * 6 + ["blocks", "blocks", "whole", "blocks", "blocks", "whole", "whole", "tokens", "blocks"],
+        ["rows"] * 5 + ["blocks", "blocks", "whole", "blocks", "blocks", "whole", "whole", "tokens", "blocks"],
         [
-            kvr,
-            qog,
+            proj,
             sums,
             raw,
             grad_o,
@@ -661,39 +751,61 @@
             rows,
         ],
         [
-            ("rows", kvr.shape, bf16),
-            ("rows", qog.shape, bf16),
-            ("whole", (RANK, KEY), f32),
+            ("rows", proj.shape, bf16),
+            ("whole", (LANES, KEY), f32),
             ("whole", (1, KEY), f32),
         ],
         flops=2 * rows_all * (3 * KEY * VAL + SPAN * (3 * KEY + 2 * VAL)),
     )
-    n1_grad_parts = (mm_nt(grad_kvr, w_kvr) + mm_nt(grad_qog, w_qog)).reshape(4, tokens, width)
+    n1_grad_parts = mm_nt(grad_proj, w_in).reshape(4, tokens, width)
+    n1_grad_parts, out_sum.from_y, grad_proj, y = together(
+        n1_grad_parts, out_sum.from_y, grad_proj, y
+    )
     n1_grad = scatter_group([n1_grad_parts[m] for m in range(4)])
+    out_sum.send_h()
+    in_sum = Summing(mm_tn(n1, grad_proj, bf16))
+    n1_grad, in_sum.from_c, out_sum.from_h = together(n1_grad, in_sum.from_c, out_sum.from_h)
+    in_sum.send_y()
+    outproj_grad = lax.ppermute(out_sum.total().astype(bf16), AXES, back)
     input_part, gain_one_grad = normed_grad(x_own.astype(f32), gain_one, n1_grad)
     input_grad = (h1_grad + input_part).reshape(1, tokens, width)
-    kvr_sum = scatter_copies(mm_tn(n1, grad_kvr, bf16))
-    qog_sum = scatter_copies(mm_tn(n1, grad_qog, bf16), ("c", "h", "y"))
-    kvr_back = return_columns(kvr_sum, place)
-    qog_back = return_columns(qog_sum, place)
+    in_sum.from_y, outproj_grad, gateup_sum, down_sum = together(
+        in_sum.from_y, outproj_grad, gateup_sum, down_sum
+    )
+    in_sum.send_h()
+    gateup_back = return_columns(gateup_sum, place)
+    ffnout_grad = lax.ppermute(down_sum, AXES, back)
+    in_sum.from_h, gateup_back, ffnout_grad = together(in_sum.from_h, gateup_back, ffnout_grad)
+    in_back = return_columns(in_sum.total(), place)
+    ffnout_grad, outproj_grad = ffnout_grad.astype(f32), outproj_grad.astype(f32)
+    ffnin_grad = jnp.concatenate(
+        [part[:, :quarter] for part in gateup_back] + [part[:, quarter:] for part in gateup_back],
+        axis=1,
+    )
     inproj_grad = jnp.concatenate(
-        [part[:, :KEY] for part in qog_back]
-        + [part[:, :KEY] for part in kvr_back]
-        + [part[:, KEY : KEY + VAL] for part in kvr_back]
-        + [part[:, KEY:] for part in qog_back]
-        + [sum(part[:, KEY + VAL :] for part in kvr_back)],
+        [part[:, :KEYS] for part in in_back]
+        + [part[:, KEYS:VALUES] for part in in_back]
+        + [part[:, VALUES:GATES] for part in in_back]
+        + [part[:, GATES:RANKS] for part in in_back]
+        + [sum(part[:, RANKS : RANKS + RANK] for part in in_back)],
         axis=1,
     )
+    result = h1 + y
+    block_out = result.astype(bf16).reshape(1, tokens, width)
+    live = valid_mask.reshape(tokens, 1).astype(f32)
+    squares = jnp.stack(
+        [jnp.sum(live * result * result), jnp.sum(live * mix * mix), jnp.sum(live * y * y)]
+    )
 
     head_slot = (lax.broadcasted_iota(jnp.int32, (HEADS, 1, 1), 0) == place).astype(f32)
-    decay_part = head_slot * jnp.concatenate([up_grad, bias_grad], axis=0)[None]
-    early = [squares, head_grad.reshape(-1), gain_two_grad, decay_part.reshape(-1)]
-    total = jnp.concatenate(early)
+    decay_part = head_slot * jnp.concatenate([rank_grad[:RANK], bias_grad], axis=0)[None]
+    sums_of = [squares, head_grad.reshape(-1), gain_two_grad, decay_part.reshape(-1), gain_one_grad]
+    total = jnp.concatenate(sums_of)
     short = -total.shape[0] % 1024
-    total = sum_all(jnp.pad(total, (0, short)).reshape(-1, 128)).reshape(-1)
-    gain_one_sum = sum_all(gain_one_grad.reshape(-1, 128)).reshape(-1)
+    total = after(jnp.pad(total, (0, short)).reshape(-1, 128), in_sum.from_y)
+    total = sum_all(total).reshape(-1)
     ends = [0]
-    for part in early:
+    for part in sums_of:
         ends.append(ends[-1] + part.shape[0])
     squares = total[: ends[1]]
     root_means = jnp.sqrt(squares / (jnp.maximum(valid_count, 1.0) * width))
@@ -703,7 +815,7 @@
 
     headgain_grad = own(total[ends[1] : ends[2]], head_gain.shape[0])
     ffngain_grad = own(total[ends[2] : ends[3]], ffn_gain.shape[0])
-    mixgain_grad = own(gain_one_sum, mixer_gain.shape[0])
+    mixgain_grad = own(total[ends[4] : ends[5]], mixer_gain.shape[0])
     decay_all = total[ends[3] : ends[4]].reshape(HEADS, RANK + 1, KEY)
     decay_all = decay_all.transpose(1, 0, 2).reshape(RANK + 1, HEADS * KEY)
     decay_own = lax.dynamic_slice(decay_all, (0, me * up_cols), (RANK + 1, up_cols))

time: 950 us -> 774 us (0.81)
  waiting for transfers between devices: 480 us -> 401 us
  starting transfers between devices: 186 us -> 125 us
  other arithmetic: 82.5 us -> 50.9 us
  matrix products: 95.9 us -> 72.4 us
  Pallas kernels: 25.6 us -> 45.3 us
  local copies, waits for them, and re-layouts: 63.4 us -> 48.7 us
  between operations: 3.92 us -> 16.4 us
    ppermute x75 -> x37, waiting for transfers between devices: 276 us -> 101 us  [swap(): return lax.ppermute(value, axis, [(0, 1), (1, 0)])]
    ppermute x48 -> x36, waiting for transfers between devices: 164 us -> 232 us  [across(): return lax.ppermute(value, ('p', 'q'), [(i, i ^ mask) for i in range(4)])]
    select_n x36 -> x0, other arithmetic: 42.4 us -> none  [join(): jnp.where(first, jnp.concatenate([one, two]), jnp.concatenate([two, one]))]
    ppermute x75 -> x37, starting transfers between devices: 80.8 us -> 46.2 us  [swap(): return lax.ppermute(value, axis, [(0, 1), (1, 0)])]
    ppermute x1, waiting for transfers between devices: 0.01 us -> 29.2 us  [local(): down_rows = lax.ppermute(ffn_out, AXES, moves)]
    ppermute x48 -> x36, starting transfers between devices: 80.1 us -> 52.9 us  [across(): return lax.ppermute(value, ('p', 'q'), [(i, i ^ mask) for i in range(4)])]
    dot_general x6 -> x4, matrix products: 45.4 us -> 22 us  [dot_nt(): lax.dot_general(a, b, (((1,), (1,)), ((), ())), preferred_element_type=f32)]
    ppermute x1, waiting for transfers between devices: 32.4 us -> 10.2 us  [from_earlier(): return lax.ppermute(end, 'h', [(0, 1)])]
  transfers between devices with their start and end apart: 129 -> 82, of which waited for: 58 -> 40; matrix products, arithmetic and copies ran while one was open for 18% -> 14% of each run, Pallas kernels for 3% -> 6%
where the time goes in v2:
time: 774 us; the launch traced here: 760 us
  waiting for transfers between devices  401 us (52%)
  starting transfers between devices  125 us (16%)
  matrix products  72.4 us (9%)
  other arithmetic  50.9 us (7%)
  local copies, waits for them, and re-layouts  48.7 us (6%)
  Pallas kernels  45.3 us (6%)
  between operations  16.4 us (2%)
    ppermute x36, waiting for transfers between devices, across(): return lax.ppermute(value, ('p', 'q'), [(i, i ^ mask) for i in range(4)])  232 us
    ppermute x37, waiting for transfers between devices, swap(): return lax.ppermute(value, axis, [(0, 1), (1, 0)])  101 us
    ppermute x36, starting transfers between devices, across(): return lax.ppermute(value, ('p', 'q'), [(i, i ^ mask) for i in range(4)])  52.9 us
    ppermute x37, starting transfers between devices, swap(): return lax.ppermute(value, axis, [(0, 1), (1, 0)])  46.2 us
    pallas_call x4, Pallas kernels, call(): pl.pallas_call(kernel, grid_spec=pltpu.PrefetchScalarGridSpec(num_scalar_...  32.5 us
    unnamed x180, local copies, waits for them, and re-layouts  32.3 us
    ppermute x1, waiting for transfers between devices, local(): down_rows = lax.ppermute(ffn_out, AXES, moves)  29.2 us
    dot_general x4, matrix products, mm(): return jnp.dot(left, right, preferred_element_type=f32).astype(out)  25.3 us
  transfers between devices with their start and end apart: 82, of which 40 were waited for; matrix products, arithmetic and copies ran while one was open for 14% of the time, Pallas kernels for 6%

profile of v2, /device:TPU:8, one launch (start us, length us, event | category | flops | bytes accessed | tf_op | source)
XLA Modules:
  0.0 759.6 jit_solution(3049178687235725941)
XLA Ops:
  22.1 7.3 collective-permute-done.4
  46.3 12.3 %collective-permute-done.12 = bf16[64,2816]{1,0:T(8,128)(2,1)S(1)} collective-permute-done((bf16[64,2816]{1,0:T(8,128)(2,1)S(1)}, bf16[64,2816]{1,0:T(8,128)(2,1)S(1)}, u32[]{:S(2)}, u32[]{:S(2)}) %collective-permute-start.12) | collective-permute-done | bytes 360480 | tf_op jit(solution)/shard_map/ppermute | solution.py:39
  72.3 13.5 %collective-permute-done.14.refs_1_ = bf16[64,2048]{1,0:T(8,128)(2,1)S(1)} collective-permute-done((bf16[64,2048]{1,0:T(8,128)(2,1)}, bf16[64,2048]{1,0:T(8,128)(2,1)S(1)}, u32[]{:S(2)}, u32[]{:S(2)}) %collective-permute-start.14) | collective-permute-done | bytes 262176 | tf_op jit(solution)/shard_map/ppermute | solution.py:583
  100.7 9.9 %collective-permute-done.21.refs_5_ = bf16[64,2048]{1,0:T(8,128)(2,1)} collective-permute-done((bf16[64,2048]{1,0:T(8,128)(2,1)S(1)}, bf16[64,2048]{1,0:T(8,128)(2,1)}, u32[]{:S(2)}, u32[]{:S(2)}) %collective-permute-start.21) | collective-permute-done | bytes 262176 | tf_op jit(solution)/shard_map/ppermute | solution.py:35
  113.5 9.5 %collective-permute-done.19.refs_3_ = bf16[128,2048]{1,0:T(8,128)(2,1)S(1)} collective-permute-done((bf16[128,2048]{1,0:T(8,128)(2,1)S(1)}, bf16[128,2048]{1,0:T(8,128)(2,1)S(1)}, u32[]{:S(2)}, u32[]{:S(2)}) %collective-permute-start.19) | collective-permute-done | bytes 524320 | tf_op jit(solution)/shard_map/ppermute | solution.py:39
  151.8 7.8 %shard_map.222 = (f32[512,256]{1,0:T(8,128)S(1)}, f32[512,256]{1,0:T(8,128)S(1)}, bf16[8,512,256]{2,1,0:T(8,128)(2,1)S(1)}, f32[8,1,256]{2,1,0:T(1,128)S(1)}, bf...) custom-call(s32[1]{0:T(128)} %bitcast.1.place, f32[512,1664]{1,0:T(8,128)} %fusion.55.proj, bf16[128,256]{1,0:T(8,128)(2,1)S(1)} %pad.21.up, ...), custom_call_target="tpu_custom_call" | custom-call | flops 134217728 | bytes 7014400 | tf_op jit(solution)/shard_map/pallas_call | solution.py:443
  162.6 13.1 %collective-permute-done.30.refs_3_ = bf16[128,2048]{1,0:T(8,128)(2,1)} collective-permute-done((bf16[128,2048]{1,0:T(8,128)(2,1)S(1)}, bf16[128,2048]{1,0:T(8,128)(2,1)}, u32[]{:S(2)}, u32[]{:S(2)}) %collective-permute-start.30) | collective-permute-done | bytes 524320 | tf_op jit(solution)/shard_map/ppermute | solution.py:39
  176.5 29.2 %collective-permute-done.25.refs_1_ = bf16[176,2048]{1,0:T(8,128)(2,1)} collective-permute-done((bf16[176,2048]{1,0:T(8,128)(2,1)}, bf16[176,2048]{1,0:T(8,128)(2,1)}, u32[]{:S(2)}, u32[]{:S(2)}) %collective-permute-start.25) | collective-permute-done | bytes 720928 | tf_op jit(solution)/shard_map/ppermute | solution.py:597
  213.6 10.2 %collective-permute-done.32.entering = bf16[512,256]{1,0:T(8,128)(2,1)} collective-permute-done((bf16[512,256]{1,0:T(8,128)(2,1)}, bf16[512,256]{1,0:T(8,128)(2,1)}, u32[]{:S(2)}, u32[]{:S(2)}) %collective-permute-start.32) | collective-permute-done | bytes 262176 | tf_op jit(solution)/shard_map/ppermute | solution.py:495
  229.4 7.1 shard_map.223
  248.9 17.4 %collective-permute-done.34 = bf16[128,2048]{1,0:T(8,128)(2,1)} collective-permute-done((bf16[128,2048]{1,0:T(8,128)(2,1)S(1)}, bf16[128,2048]{1,0:T(8,128)(2,1)}, u32[]{:S(2)}, u32[]{:S(2)}) %collective-permute-start.34) | collective-permute-done | bytes 524320 | tf_op jit(solution)/shard_map/ppermute | solution.py:39
  270.7 10.4 %collective-permute-done.35 = bf16[128,2048]{1,0:T(8,128)(2,1)} collective-permute-done((bf16[128,2048]{1,0:T(8,128)(2,1)}, bf16[128,2048]{1,0:T(8,128)(2,1)}, u32[]{:S(2)}, u32[]{:S(2)}) %collective-permute-start.35) | collective-permute-done | bytes 524320 | tf_op jit(solution)/shard_map/ppermute | solution.py:39
  283.2 14.4 %collective-permute-done.37.refs_5_ = bf16[176,2048]{1,0:T(8,128)(2,1)} collective-permute-done((bf16[176,2048]{1,0:T(8,128)(2,1)}, bf16[176,2048]{1,0:T(8,128)(2,1)}, u32[]{:S(2)}, u32[]{:S(2)}) %collective-permute-start.37) | collective-permute-done | bytes 720928 | tf_op jit(solution)/shard_map/ppermute | solution.py:35
  303.4 10.9 %collective-permute-done.42.refs_4_ = bf16[128,2048]{1,0:T(8,128)(2,1)S(1)} collective-permute-done((bf16[128,2048]{1,0:T(8,128)(2,1)S(1)}, bf16[128,2048]{1,0:T(8,128)(2,1)S(1)}, u32[]{:S(2)}, u32[]{:S(2)}) %collective-permute-start.42) | collective-permute-done | bytes 524320 | tf_op jit(solution)/shard_map/ppermute | solution.py:39
  316.1 8.8 %collective-permute-done.41.refs_3_ = bf16[128,2048]{1,0:T(8,128)(2,1)S(1)} collective-permute-done((bf16[128,2048]{1,0:T(8,128)(2,1)S(1)}, bf16[128,2048]{1,0:T(8,128)(2,1)S(1)}, u32[]{:S(2)}, u32[]{:S(2)}) %collective-permute-start.41) | collective-permute-done | bytes 524320 | tf_op jit(solution)/shard_map/ppermute | solution.py:39
  336.7 10.3 %fusion.56 = f32[512,2816]{1,0:T(8,128)S(1)} fusion(bf16[512,2048]{1,0:T(8,128)(2,1)} %bitcast.248, bf16[2048,2816]{1,0:T(8,128)(2,1)} %all-gather.2.cloned.1.call-done), kind=kOutput, calls=%fused_computation.239 | convolution fusion | flops 5905580032 | bytes 19398656 | tf_op jit(solution)/shard_map/dot_general | solution.py:477
  353.4 10.5 %fusion.45 = f32[512,2048]{1,0:T(8,128)} fusion(bf16[2048,2816]{1,0:T(8,128)(2,1)} %all-gather.2.cloned.1.call-done, bf16[512,1408]{1,0:T(8,128)(2,1)S(1)} %get-tuple-element.212, bf16[512,1408]{1,0:T(8,128)(2,1)S(1)} %get-tuple-element.211), kind=kOutput, calls=%fused_computation.229 | convolution fusion | flops 5911347200 | bytes 18612224 | tf_op jit(solution)/shard_map/dot_general | solution.py:226
  369.2 11.3 %convolution_convert_fusion = bf16[2048,2816]{1,0:T(8,128)(2,1)} fusion(bf16[512,2048]{1,0:T(8,128)(2,1)} %bitcast.249, bf16[512,2816]{1,0:T(8,128)(2,1)} %pad_maximum_fusion), kind=kOutput, calls=%fused_computation | convolution fusion | flops 5911347200 | bytes 16515072 | tf_op jit(solution)/shard_map/dot_general | solution.py:230
  387.3 22.2 %collective-permute-done.47 = bf16[128,2048]{1,0:T(8,128)(2,1)S(1)} collective-permute-done((bf16[128,2048]{1,0:T(8,128)(2,1)S(1)}, bf16[128,2048]{1,0:T(8,128)(2,1)S(1)}, u32[]{:S(2)}, u32[]{:S(2)}) %collective-permute-start.47) | collective-permute-done | bytes 524320 | tf_op jit(solution)/shard_map/ppermute | solution.py:39
  409.4 16.7 %collective-permute-done.48 = bf16[128,2048]{1,0:T(8,128)(2,1)S(1)} collective-permute-done((bf16[128,2048]{1,0:T(8,128)(2,1)S(1)}, bf16[128,2048]{1,0:T(8,128)(2,1)S(1)}, u32[]{:S(2)}, u32[]{:S(2)}) %collective-permute-start.48) | collective-permute-done | bytes 524320 | tf_op jit(solution)/shard_map/ppermute | solution.py:39
  433.0 20.4 %collective-permute-done.52.refs_4_ = bf16[128,2048]{1,0:T(8,128)(2,1)} collective-permute-done((bf16[128,2048]{1,0:T(8,128)(2,1)}, bf16[128,2048]{1,0:T(8,128)(2,1)}, u32[]{:S(2)}, u32[]{:S(2)}) %collective-permute-start.52) | collective-permute-done | bytes 524320 | tf_op jit(solution)/shard_map/ppermute | solution.py:39
  453.4 8.7 %collective-permute-done.51.refs_3_ = bf16[128,2048]{1,0:T(8,128)(2,1)} collective-permute-done((bf16[128,2048]{1,0:T(8,128)(2,1)}, bf16[128,2048]{1,0:T(8,128)(2,1)}, u32[]{:S(2)}, u32[]{:S(2)}) %collective-permute-start.51) | collective-permute-done | bytes 524320 | tf_op jit(solution)/shard_map/ppermute | solution.py:39
  482.0 7.8 %shard_map.229 = (bf16[512,512]{1,0:T(8,128)(2,1)S(1)}, bf16[512,512]{1,0:T(8,128)(2,1)S(1)}, bf16[8,512,256]{2,1,0:T(8,128)(2,1)}, f32[8,1,256]{2,1,0:T(1,128)S...) custom-call(s32[1]{0:T(128)} %bitcast.1.place, f32[512,512]{1,0:T(8,128)S(1)} %fusion.57.grad_gated, ...), custom_call_target="tpu_custom_call" | custom-call | flops 134217728 | bytes 12128256 | tf_op jit(solution)/shard_map/pallas_call | solution.py:443
  494.4 21.9 %collective-permute-done.58 = bf16[128,2048]{1,0:T(8,128)(2,1)} collective-permute-done((bf16[128,2048]{1,0:T(8,128)(2,1)S(1)}, bf16[128,2048]{1,0:T(8,128)(2,1)}, u32[]{:S(2)}, u32[]{:S(2)}) %collective-permute-start.58) | collective-permute-done | bytes 524320 | tf_op jit(solution)/shard_map/ppermute | solution.py:39
  519.1 9.6 %collective-permute-done.53.leaving = bf16[512,256]{1,0:T(8,128)(2,1)S(1)} collective-permute-done((bf16[512,256]{1,0:T(8,128)(2,1)S(1)}, bf16[512,256]{1,0:T(8,128)(2,1)S(1)}, u32[]{:S(2)}, u32[]{:S(2)}) %collective-permute-start.53) | collective-permute-done | bytes 262176 | tf_op jit(solution)/shard_map/ppermute | solution.py:507
  533.7 9.8 %shard_map.230 = (bf16[512,1664]{1,0:T(8,128)(2,1)S(1)}, f32[128,256]{1,0:T(8,128)S(1)}, f32[1,256]{1,0:T(1,128)S(1)}) custom-call(s32[1]{0:T(128)} %bitcast.1.place, f32[512,1664]{1,0:T(8,128)} %fusion.55.proj, f32[512,256]{1,0:T(8,128)S(1)} %get-tuple-element.118.sums, f32[512,256]{1,0:T(8,128)S(1)} %copy-done.39, ...), custom_call_target="tpu_custom_call" | custom-call | flops 520093696 | bytes 20676608 | tf_op jit(solution)/shard_map/pallas_call | solution.py:443
  560.0 12.2 %collective-permute-start.61 = (bf16[128,2048]{1,0:T(8,128)(2,1)S(1)}, bf16[128,2048]{1,0:T(8,128)(2,1)S(1)}, u32[]{:S(2)}, u32[]{:S(2)}) collective-permute-start(bf16[128,2048]{1,0:T(8,128)(2,1)S(1)} %get-tuple-element.227), channel_id=1, source_target_pairs={{0,3},{1,2},{2,1},{3,0},{4,7},{5,6},{6,5},{7,4},{8,11},{9,10},{10,... | collective-permute-start | bytes 1572872 | tf_op jit(solution)/shard_map/ppermute | solution.py:39
  575.2 20.9 %collective-permute-done.61 = bf16[128,2048]{1,0:T(8,128)(2,1)S(1)} collective-permute-done((bf16[128,2048]{1,0:T(8,128)(2,1)S(1)}, bf16[128,2048]{1,0:T(8,128)(2,1)S(1)}, u32[]{:S(2)}, u32[]{:S(2)}) %collective-permute-start.61) | collective-permute-done | bytes 524320 | tf_op jit(solution)/shard_map/ppermute | solution.py:39
  596.1 17.4 %collective-permute-done.60 = bf16[128,2048]{1,0:T(8,128)(2,1)S(1)} collective-permute-done((bf16[128,2048]{1,0:T(8,128)(2,1)S(1)}, bf16[128,2048]{1,0:T(8,128)(2,1)S(1)}, u32[]{:S(2)}, u32[]{:S(2)}) %collective-permute-start.60) | collective-permute-done | bytes 524320 | tf_op jit(solution)/shard_map/ppermute | solution.py:39
  639.2 27.8 %collective-permute-done.64 = bf16[2,256,1664]{2,1,0:T(8,128)(2,1)} collective-permute-done((bf16[2,256,1664]{2,1,0:T(8,128)(2,1)}, bf16[2,256,1664]{2,1,0:T(8,128)(2,1)}, u32[]{:S(2)}, u32[]{:S(2)}) %collective-permute-start.64) | collective-permute-done | bytes 1703968 | tf_op jit(solution)/shard_map/ppermute | solution.py:35
  694.3 6.4 collective-permute-done.68
  701.1 28.9 %collective-permute-done.78 = f32[176,128]{1,0:T(8,128)S(1)} collective-permute-done((f32[176,128]{1,0:T(8,128)S(1)}, f32[176,128]{1,0:T(8,128)S(1)}, u32[]{:S(2)}, u32[]{:S(2)}) %collective-permute-start.78) | collective-permute-done | bytes 90144 | tf_op jit(solution)/shard_map/ppermute | solution.py:35
  (479 shorter events, 298.7 us)
Async XLA Ops:
  7.2 329.5 %all-gather.2.cloned.1.call-start = ((), (), s32[]{:S(2)}) async-start(), calls=%async_computation.2 | async-start | bytes 12976128 | tf_op jit(solution)/shard_map/all_gather | solution.py:595
  44.8 41.1 %collective-permute-start.10 = (bf16[256,1664]{1,0:T(8,128)(2,1)S(1)}, bf16[256,1664]{1,0:T(8,128)(2,1)S(1)}, u32[]{:S(2)}, u32[]{:S(2)}) collective-permute-start(bf16[256,1664]{1,0:T(8,128)(2,1)S(1)} %pad_maximum_fusion.2.refs_1_), channel_id=1, source_target_pairs={{0,8},{8,0},{1,9},{9,1},{2,10},{10,2},{3,11},{11,3},{4,12},{12,4},... | collective-permute-start | bytes 2555912 | tf_op jit(solution)/shard_map/ppermute | solution.py:35
  44.8 41.1 %collective-permute-start.9 = (bf16[256,1664]{1,0:T(8,128)(2,1)S(1)}, bf16[256,1664]{1,0:T(8,128)(2,1)S(1)}, u32[]{:S(2)}, u32[]{:S(2)}) collective-permute-start(bf16[256,1664]{1,0:T(8,128)(2,1)S(1)} %pad_maximum_fusion.2.refs_1_), channel_id=1, source_target_pairs={{0,16},{16,0},{1,17},{17,1},{2,18},{18,2},{3,19},{19,3},{4,20},{20... | collective-permute-start | bytes 2555912 | tf_op jit(solution)/shard_map/ppermute | solution.py:35
  90.4 34.2 %collective-permute-start.17 = (bf16[256,1664]{1,0:T(8,128)(2,1)S(1)}, bf16[256,1664]{1,0:T(8,128)(2,1)S(1)}, u32[]{:S(2)}, u32[]{:S(2)}) collective-permute-start(bf16[256,1664]{1,0:T(8,128)(2,1)S(1)} %collective-permute-done.9.refs_2_), channel_id=1, source_target_pairs={{0,8},{8,0},{1,9},{9,1},{2,10},{10,2},{3,11},{11,3},{4,12},{12,4},... | collective-permute-start | bytes 2555912 | tf_op jit(solution)/shard_map/ppermute | solution.py:35
  90.4 35.1 %collective-permute-start.16 = (bf16[256,1664]{1,0:T(8,128)(2,1)}, bf16[256,1664]{1,0:T(8,128)(2,1)S(1)}, u32[]{:S(2)}, u32[]{:S(2)}) collective-permute-start(bf16[256,1664]{1,0:T(8,128)(2,1)} %collective-permute-done.8.refs_5_), channel_id=1, source_target_pairs={{0,8},{8,0},{1,9},{9,1},{2,10},{10,2},{3,11},{11,3},{4,12},{12,4},... | collective-permute-start | bytes 2555912 | tf_op jit(solution)/shard_map/ppermute | solution.py:35
  91.7 34.8 %collective-permute-start.15 = (bf16[256,1664]{1,0:T(8,128)(2,1)}, bf16[256,1664]{1,0:T(8,128)(2,1)}, u32[]{:S(2)}, u32[]{:S(2)}) collective-permute-start(bf16[256,1664]{1,0:T(8,128)(2,1)} %collective-permute-done.8.refs_5_), channel_id=1, source_target_pairs={{0,16},{16,0},{1,17},{17,1},{2,18},{18,2},{3,19},{19,3},{4,20},{20... | collective-permute-start | bytes 2555912 | tf_op jit(solution)/shard_map/ppermute | solution.py:35
  126.5 507.5 %reduce-scatter.5.cloned.1.call-start = ((), (), s32[]{:S(2)}) async-start(), calls=%async_computation.4 | async-start | bytes 6488064 | tf_op jit(solution)/shard_map/reduce_scatter | solution.py:204
  129.0 32.7 %collective-permute-start.26 = (bf16[64,2048]{1,0:T(8,128)(2,1)}, bf16[64,2048]{1,0:T(8,128)(2,1)}, u32[]{:S(2)}, u32[]{:S(2)}) collective-permute-start(bf16[64,2048]{1,0:T(8,128)(2,1)} %collective-permute-done.21.refs_5_), channel_id=1, source_target_pairs={{0,16},{16,0},{1,17},{17,1},{2,18},{18,2},{3,19},{19,3},{4,20},{20... | collective-permute-start | bytes 786440 | tf_op jit(solution)/shard_map/ppermute | solution.py:35
  137.9 37.8 %collective-permute-start.30 = (bf16[128,2048]{1,0:T(8,128)(2,1)S(1)}, bf16[128,2048]{1,0:T(8,128)(2,1)}, u32[]{:S(2)}, u32[]{:S(2)}) collective-permute-start(bf16[128,2048]{1,0:T(8,128)(2,1)S(1)} %bitcast.245), channel_id=1, source_target_pairs={{0,2},{1,3},{2,0},{3,1},{4,6},{5,7},{6,4},{7,5},{8,10},{9,11},{10,... | collective-permute-start | bytes 1572872 | tf_op jit(solution)/shard_map/ppermute | solution.py:39
  142.3 33.4 %collective-permute-start.29 = (bf16[128,2048]{1,0:T(8,128)(2,1)S(1)}, bf16[128,2048]{1,0:T(8,128)(2,1)S(1)}, u32[]{:S(2)}, u32[]{:S(2)}) collective-permute-start(bf16[128,2048]{1,0:T(8,128)(2,1)S(1)} %bitcast.246), channel_id=1, source_target_pairs={{0,1},{1,0},{2,3},{3,2},{4,5},{5,4},{6,7},{7,6},{8,9},{9,8},{10,11... | collective-permute-start | bytes 1572872 | tf_op jit(solution)/shard_map/ppermute | solution.py:39
  143.8 61.9 %collective-permute-start.25 = (bf16[176,2048]{1,0:T(8,128)(2,1)}, bf16[176,2048]{1,0:T(8,128)(2,1)}, u32[]{:S(2)}, u32[]{:S(2)}) collective-permute-start(bf16[176,2048]{1,0:T(8,128)(2,1)} %param.21), channel_id=1, source_target_pairs={{0,0},{1,8},{2,16},{3,24},{4,4},{5,12},{6,20},{7,28},{8,1},{9,9},{... | collective-permute-start | bytes 2162696 | tf_op jit(solution)/shard_map/ppermute | solution.py:597
  242.7 28.1 %collective-permute-start.36 = (bf16[128,2048]{1,0:T(8,128)(2,1)}, bf16[128,2048]{1,0:T(8,128)(2,1)}, u32[]{:S(2)}, u32[]{:S(2)}) collective-permute-start(bf16[128,2048]{1,0:T(8,128)(2,1)} %get-tuple-element.233), channel_id=1, source_target_pairs={{0,3},{1,2},{2,1},{3,0},{4,7},{5,6},{6,5},{7,4},{8,11},{9,10},{10,... | collective-permute-start | bytes 1572872 | tf_op jit(solution)/shard_map/ppermute | solution.py:39
  242.7 38.5 %collective-permute-start.35 = (bf16[128,2048]{1,0:T(8,128)(2,1)}, bf16[128,2048]{1,0:T(8,128)(2,1)}, u32[]{:S(2)}, u32[]{:S(2)}) collective-permute-start(bf16[128,2048]{1,0:T(8,128)(2,1)} %get-tuple-element.234), channel_id=1, source_target_pairs={{0,2},{1,3},{2,0},{3,1},{4,6},{5,7},{6,4},{7,5},{8,10},{9,11},{10,... | collective-permute-start | bytes 1572872 | tf_op jit(solution)/shard_map/ppermute | solution.py:39
  244.5 38.7 %collective-permute-start.39 = (bf16[176,2048]{1,0:T(8,128)(2,1)}, bf16[176,2048]{1,0:T(8,128)(2,1)}, u32[]{:S(2)}, u32[]{:S(2)}) collective-permute-start(bf16[176,2048]{1,0:T(8,128)(2,1)} %collective-permute-done.25.refs_1_), channel_id=1, source_target_pairs={{0,8},{8,0},{1,9},{9,1},{2,10},{10,2},{3,11},{11,3},{4,12},{12,4},... | collective-permute-start | bytes 2162696 | tf_op jit(solution)/shard_map/ppermute | solution.py:35
  244.5 38.7 %collective-permute-start.38 = (bf16[176,2048]{1,0:T(8,128)(2,1)}, bf16[176,2048]{1,0:T(8,128)(2,1)}, u32[]{:S(2)}, u32[]{:S(2)}) collective-permute-start(bf16[176,2048]{1,0:T(8,128)(2,1)} %collective-permute-done.25.refs_1_), channel_id=1, source_target_pairs={{0,16},{16,0},{1,17},{17,1},{2,18},{18,2},{3,19},{19,3},{4,20},{20... | collective-permute-start | bytes 2162696 | tf_op jit(solution)/shard_map/ppermute | solution.py:35
  266.3 31.3 %collective-permute-start.37 = (bf16[176,2048]{1,0:T(8,128)(2,1)}, bf16[176,2048]{1,0:T(8,128)(2,1)}, u32[]{:S(2)}, u32[]{:S(2)}) collective-permute-start(bf16[176,2048]{1,0:T(8,128)(2,1)} %collective-permute-done.25.refs_1_), channel_id=1, source_target_pairs={{0,4},{4,0},{1,5},{5,1},{2,6},{6,2},{3,7},{7,3},{8,12},{12,8},{9,1... | collective-permute-start | bytes 2162696 | tf_op jit(solution)/shard_map/ppermute | solution.py:35
  298.7 27.7 %collective-permute-start.45 = (bf16[176,2048]{1,0:T(8,128)(2,1)}, bf16[176,2048]{1,0:T(8,128)(2,1)S(1)}, u32[]{:S(2)}, u32[]{:S(2)}) collective-permute-start(bf16[176,2048]{1,0:T(8,128)(2,1)} %collective-permute-done.38.refs_2_), channel_id=1, source_target_pairs={{0,8},{8,0},{1,9},{9,1},{2,10},{10,2},{3,11},{11,3},{4,12},{12,4},... | collective-permute-start | bytes 2162696 | tf_op jit(solution)/shard_map/ppermute | solution.py:35
  369.1 297.9 %reduce-scatter.3.cloned.1.call-start = ((), (), s32[]{:S(2)}) async-start(), calls=%async_computation.3 | async-start | bytes 12976128 | tf_op jit(solution)/shard_map/reduce_scatter | solution.py:199
  386.3 39.9 %collective-permute-start.48 = (bf16[128,2048]{1,0:T(8,128)(2,1)S(1)}, bf16[128,2048]{1,0:T(8,128)(2,1)S(1)}, u32[]{:S(2)}, u32[]{:S(2)}) collective-permute-start(bf16[128,2048]{1,0:T(8,128)(2,1)S(1)} %get-tuple-element.231), channel_id=1, source_target_pairs={{0,2},{1,3},{2,0},{3,1},{4,6},{5,7},{6,4},{7,5},{8,10},{9,11},{10,... | collective-permute-start | bytes 1572872 | tf_op jit(solution)/shard_map/ppermute | solution.py:39
  430.2 31.9 %collective-permute-start.51 = (bf16[128,2048]{1,0:T(8,128)(2,1)}, bf16[128,2048]{1,0:T(8,128)(2,1)}, u32[]{:S(2)}, u32[]{:S(2)}) collective-permute-start(bf16[128,2048]{1,0:T(8,128)(2,1)} %get-tuple-element.200.refs_1_), channel_id=1, source_target_pairs={{0,2},{1,3},{2,0},{3,1},{4,6},{5,7},{6,4},{7,5},{8,10},{9,11},{10,... | collective-permute-start | bytes 1572872 | tf_op jit(solution)/shard_map/ppermute | solution.py:39
  432.6 29.4 %collective-permute-start.50 = (bf16[128,2048]{1,0:T(8,128)(2,1)}, bf16[128,2048]{1,0:T(8,128)(2,1)}, u32[]{:S(2)}, u32[]{:S(2)}) collective-permute-start(bf16[128,2048]{1,0:T(8,128)(2,1)} %get-tuple-element.200.refs_1_), channel_id=1, source_target_pairs={{0,1},{1,0},{2,3},{3,2},{4,5},{5,4},{6,7},{7,6},{8,9},{9,8},{10,11... | collective-permute-start | bytes 1572872 | tf_op jit(solution)/shard_map/ppermute | solution.py:39
  467.5 61.2 %collective-permute-start.54 = (bf16[512,2048]{1,0:T(8,128)(2,1)}, bf16[512,2048]{1,0:T(8,128)(2,1)}, u32[]{:S(2)}, u32[]{:S(2)}) collective-permute-start(bf16[512,2048]{1,0:T(8,128)(2,1)} %convolution_convert_fusion.3), channel_id=1, source_target_pairs={{0,8},{8,0},{1,9},{9,1},{2,10},{10,2},{3,11},{11,3},{4,12},{12,4},... | collective-permute-start | bytes 6291464 | tf_op jit(solution)/shard_map/ppermute | solution.py:35
  475.5 40.9 %collective-permute-start.58 = (bf16[128,2048]{1,0:T(8,128)(2,1)S(1)}, bf16[128,2048]{1,0:T(8,128)(2,1)}, u32[]{:S(2)}, u32[]{:S(2)}) collective-permute-start(bf16[128,2048]{1,0:T(8,128)(2,1)S(1)} %get-tuple-element.167), channel_id=1, source_target_pairs={{0,3},{1,2},{2,1},{3,0},{4,7},{5,6},{6,5},{7,4},{8,11},{9,10},{10,... | collective-permute-start | bytes 1572872 | tf_op jit(solution)/shard_map/ppermute | solution.py:39
  489.8 38.9 %collective-permute-start.53 = (bf16[512,256]{1,0:T(8,128)(2,1)S(1)}, bf16[512,256]{1,0:T(8,128)(2,1)S(1)}, u32[]{:S(2)}, u32[]{:S(2)}) collective-permute-start(bf16[512,256]{1,0:T(8,128)(2,1)S(1)} %get-tuple-element.159), channel_id=1, source_target_pairs={{4,0},{5,1},{6,2},{7,3},{12,8},{13,9},{14,10},{15,11},{20,16},{21,... | collective-permute-start | bytes 786440 | tf_op jit(solution)/shard_map/ppermute | solution.py:507
  555.2 60.8 %collective-permute-start.62 = (bf16[2048,1664]{1,0:T(8,128)(2,1)}, bf16[2048,1664]{1,0:T(8,128)(2,1)}, u32[]{:S(2)}, u32[]{:S(2)}) collective-permute-start(bf16[2048,1664]{1,0:T(8,128)(2,1)} %convolution_convert_fusion.2), channel_id=1, source_target_pairs={{0,8},{8,0},{1,9},{9,1},{2,10},{10,2},{3,11},{11,3},{4,12},{12,4},... | collective-permute-start | bytes 20447240 | tf_op jit(solution)/shard_map/ppermute | solution.py:35
  560.0 36.1 %collective-permute-start.61 = (bf16[128,2048]{1,0:T(8,128)(2,1)S(1)}, bf16[128,2048]{1,0:T(8,128)(2,1)S(1)}, u32[]{:S(2)}, u32[]{:S(2)}) collective-permute-start(bf16[128,2048]{1,0:T(8,128)(2,1)S(1)} %get-tuple-element.227), channel_id=1, source_target_pairs={{0,3},{1,2},{2,1},{3,0},{4,7},{5,6},{6,5},{7,4},{8,11},{9,10},{10,... | collective-permute-start | bytes 1572872 | tf_op jit(solution)/shard_map/ppermute | solution.py:39
  572.2 41.3 %collective-permute-start.60 = (bf16[128,2048]{1,0:T(8,128)(2,1)S(1)}, bf16[128,2048]{1,0:T(8,128)(2,1)S(1)}, u32[]{:S(2)}, u32[]{:S(2)}) collective-permute-start(bf16[128,2048]{1,0:T(8,128)(2,1)S(1)} %get-tuple-element.228), channel_id=1, source_target_pairs={{0,2},{1,3},{2,0},{3,1},{4,6},{5,7},{6,4},{7,5},{8,10},{9,11},{10,... | collective-permute-start | bytes 1572872 | tf_op jit(solution)/shard_map/ppermute | solution.py:39
  575.1 40.9 %collective-permute-start.63 = (bf16[64,2048]{1,0:T(8,128)(2,1)S(1)}, bf16[64,2048]{1,0:T(8,128)(2,1)S(1)}, u32[]{:S(2)}, u32[]{:S(2)}) collective-permute-start(bf16[64,2048]{1,0:T(8,128)(2,1)S(1)} %fusion.30), channel_id=1, source_target_pairs={{0,4},{4,0},{1,5},{5,1},{2,6},{6,2},{3,7},{7,3},{8,12},{12,8},{9,1... | collective-permute-start | bytes 786440 | tf_op jit(solution)/shard_map/ppermute | solution.py:35
  622.2 44.8 %collective-permute-start.64 = (bf16[2,256,1664]{2,1,0:T(8,128)(2,1)}, bf16[2,256,1664]{2,1,0:T(8,128)(2,1)}, u32[]{:S(2)}, u32[]{:S(2)}) collective-permute-start(bf16[2,256,1664]{2,1,0:T(8,128)(2,1)} %bitcast.75), channel_id=1, source_target_pairs={{0,16},{16,0},{1,17},{17,1},{2,18},{18,2},{3,19},{19,3},{4,20},{20... | collective-permute-start | bytes 5111816 | tf_op jit(solution)/shard_map/ppermute | solution.py:35
  679.8 54.1 %collective-permute-start.70 = (bf16[176,2048]{1,0:T(8,128)(2,1)}, bf16[176,2048]{1,0:T(8,128)(2,1)}, u32[]{:S(2)}, u32[]{:S(2)}) collective-permute-start(bf16[176,2048]{1,0:T(8,128)(2,1)} %reduce-scatter.5.cloned.1.call-done), channel_id=1, source_target_pairs={{0,0},{8,1},{16,2},{24,3},{4,4},{12,5},{20,6},{28,7},{1,8},{9,9},{... | collective-permute-start | bytes 2162696 | tf_op jit(solution)/shard_map/ppermute | solution.py:777
  691.3 42.6 %collective-permute-start.66 = (bf16[256,1664]{1,0:T(8,128)(2,1)}, bf16[256,1664]{1,0:T(8,128)(2,1)}, u32[]{:S(2)}, u32[]{:S(2)}) collective-permute-start(bf16[256,1664]{1,0:T(8,128)(2,1)} %fusion.19), channel_id=1, source_target_pairs={{0,4},{4,0},{1,5},{5,1},{2,6},{6,2},{3,7},{7,3},{8,12},{12,8},{9,1... | collective-permute-start | bytes 2555912 | tf_op jit(solution)/shard_map/ppermute | solution.py:35
  691.3 38.6 %collective-permute-start.78 = (f32[176,128]{1,0:T(8,128)S(1)}, f32[176,128]{1,0:T(8,128)S(1)}, u32[]{:S(2)}, u32[]{:S(2)}) collective-permute-start(f32[176,128]{1,0:T(8,128)S(1)} %add.472), channel_id=1, source_target_pairs={{0,4},{4,0},{1,5},{5,1},{2,6},{6,2},{3,7},{7,3},{8,12},{12,8},{9,1... | collective-permute-start | bytes 270344 | tf_op jit(solution)/shard_map/ppermute | solution.py:35
  (126 other events, 1630.8 us)
Sparse Core Ops, SparseCore 0:
  126.6 122.3 all-gather.1
  369.3 85.1 reduce-scatter.4
  458.4 145.4 reduce-scatter.2

commit v3 on v2

--- a/solution.py
+++ b/solution.py
@@ -19,6 +19,7 @@
 AXES = ("y", "c", "h", "p", "q")
 COPIES = ("y", "c", "h")
 
+
 bf16 = jnp.bfloat16
 f32 = jnp.float32
 
@@ -35,17 +36,28 @@
     return lax.ppermute(value, axis, [(0, 1), (1, 0)])
 
 
-def across(value, mask):
-    return lax.ppermute(value, ("p", "q"), [(i, i ^ mask) for i in range(4)])
-
-
-def gather_group(value):
-    return [value] + [across(value, mask) for mask in (1, 2, 3)]
-
-
-def scatter_group(parts):
-    received = [across(parts[mask].astype(bf16), mask) for mask in (1, 2, 3)]
-    return parts[0] + received[0].astype(f32) + received[1].astype(f32) + received[2].astype(f32)
+def across(value, mask, group=("p", "q")):
+    return lax.ppermute(value, group, [(i, i ^ mask) for i in range(4)])
+
+
+def two_of(value, group=("p", "q")):
+    return across(value, 1, group), across(value, 2, group)
+
+
+def last_of(value, group=("p", "q")):
+    return across(value, 3, group)
+
+
+def shares(parts):
+    return [parts[mask].astype(bf16) for mask in range(4)]
+
+
+def add_shares(own, received):
+    return own + received[0].astype(f32) + received[1].astype(f32) + received[2].astype(f32)
+
+
+def half_swap(block):
+    return swap(block, "h") if binary_copies() else block
 
 
 def stack_axis(value, axis):
@@ -56,166 +68,214 @@
     return jnp.where(first, jnp.stack([value, other]), jnp.stack([other, value]))
 
 
-def sum_all(value):
-    for axis in ("q", "p", "c", "y", "h"):
-        if lax.axis_size(axis) == 2:
-            value = value + swap(value, axis)
-        else:
-            value = lax.psum(value, axis)
-    return value
+def sum_over(value, axis):
+    if lax.axis_size(axis) == 2:
+        return value + swap(value, axis)
+    return lax.psum(value, axis)
+
+
+def sum_group(value, axes):
+    if any(lax.axis_size(axis) != 2 for axis in axes):
+        return lax.psum(value, axes)
+    return value + across(value, 1, axes) + across(value, 2, axes) + across(value, 3, axes)
 
 
 def binary_copies():
     return all(lax.axis_size(axis) == 2 for axis in COPIES)
 
 
-def half_swap(block):
-    return swap(block, "h") if binary_copies() else block
-
-
-def near_copies(block):
-    return (swap(block, "y"), swap(block, "c")) if binary_copies() else (block, block)
-
-
-def core_swap(block):
-    return swap(block, "c") if binary_copies() else block
-
-
-def lay_kernel(count, slots, *refs):
+def lay_kernel(offsets, pieces, count, *refs):
     blocks, whole, sems = refs[:count], refs[count], refs[count + 1]
-    copies = [
-        pltpu.make_async_copy(blocks[i], whole.at[slots[i]], sems.at[i]) for i in range(count)
-    ]
+    copies = []
+    for i, (block, first, rows) in enumerate(pieces):
+        place = pl.ds(pl.multiple_of(offsets[i], 16), rows)
+        copies.append(
+            pltpu.make_async_copy(
+                blocks[block].at[pl.ds(first, rows)], whole.at[place], sems.at[i]
+            )
+        )
     for copy in copies:
         copy.start()
     for copy in copies:
         copy.wait()
 
 
-def lay(blocks, slots):
-    count, (rows, cols), kind = len(blocks), blocks[0].shape, blocks[0].dtype
-    size = count * rows * cols * kind.itemsize
-    whole = pl.pallas_call(
-        lambda *refs: lay_kernel(count, *refs),
+def lay(blocks, pieces, offsets):
+    cols, kind = blocks[0].shape[1], blocks[0].dtype
+    total = sum(rows for _, _, rows in pieces)
+    return pl.pallas_call(
+        lambda offsets, *refs: lay_kernel(offsets, pieces, len(blocks), *refs),
         grid_spec=pltpu.PrefetchScalarGridSpec(
             num_scalar_prefetch=1,
             grid=(1,),
-            in_specs=[pl.BlockSpec(memory_space=pl.ANY)] * count,
+            in_specs=[pl.BlockSpec(memory_space=pl.ANY)] * len(blocks),
             out_specs=pl.BlockSpec(memory_space=pl.ANY),
-            scratch_shapes=[pltpu.SemaphoreType.DMA((count,))],
+            scratch_shapes=[pltpu.SemaphoreType.DMA((len(pieces),))],
         ),
-        out_shape=jax.ShapeDtypeStruct((count, rows, cols), kind),
+        out_shape=jax.ShapeDtypeStruct((total, cols), kind),
         compiler_params=pltpu.CompilerParams(vmem_limit_bytes=16 * 1024 * 1024),
-        cost_estimate=pl.CostEstimate(flops=0, bytes_accessed=2 * size, transcendentals=0),
-    )(jnp.stack(slots).astype(jnp.int32), *blocks)
-    return whole.reshape(count * rows, cols)
+        cost_estimate=pl.CostEstimate(
+            flops=0, bytes_accessed=2 * total * cols * kind.itemsize, transcendentals=0
+        ),
+    )(jnp.stack(offsets).astype(jnp.int32), *blocks)
 
 
 def in_order(blocks):
-    return lay(blocks, [jnp.int32(i) for i in range(len(blocks))])
-
-
-def all_copies(block, parts, tall=False):
-    if not binary_copies():
-        return lax.all_gather(block, COPIES, axis=0, tiled=True)
-    h, c, y = (lax.axis_index(axis) for axis in ("h", "c", "y"))
-    flips = [(0, 0, 0), (1, 0, 0), (0, 1, 0), (1, 1, 0), (0, 0, 1), (1, 0, 1), (0, 1, 1), (1, 1, 1)]
-    slots = []
-    for fy, fc, fh in flips:
-        ty, tc, th = y ^ fy, c ^ fc, h ^ fh
-        slots.append(th * 4 + ty * 2 + tc if tall else ty * 4 + tc * 2 + th)
-    return lay((block,) + tuple(parts), slots)
+    rows = blocks[0].shape[0]
+    pieces = [(i, 0, rows) for i in range(len(blocks))]
+    return lay(blocks, pieces, [jnp.int32(i * rows) for i in range(len(blocks))])
 
 
 def pick(value, index, axis):
     return lax.dynamic_index_in_dim(value, index, axis, keepdims=False)
 
 
-def copies_part(value, y, tall):
-    ys, hs = lax.axis_size("y"), lax.axis_size("h")
-    c = lax.axis_index("c")
-    rows, cols = value.shape
-    if tall and binary_copies():
-        return pick(pick(value.reshape(hs, ys, 2, -1, cols), y, 1), c, 1)
-    part = rows // (2 * ys)
-    return lax.dynamic_slice_in_dim(value, (y * 2 + c) * part, part, 0).reshape(hs, -1, cols)
-
-
-class Summing:
-    def __init__(self, grad, tall=False):
-        self.grad, self.tall = grad, tall
-        self.from_c = swap(grad, "c")
-
-    def of(self, y):
-        one = copies_part(self.grad, y, self.tall).astype(f32)
-        return one + copies_part(self.from_c, y, self.tall).astype(f32)
-
-    def send_y(self):
-        mine = lax.axis_index("y")
-        if lax.axis_size("y") == 2:
-            self.from_y = swap(self.of(1 - mine).astype(bf16), "y")
-        else:
-            parts = jnp.stack([self.of(y) for y in range(lax.axis_size("y"))])
-            self.from_y = lax.psum_scatter(parts.astype(bf16), "y", scatter_dimension=0)
-
-    def near(self):
-        if lax.axis_size("y") == 2:
-            return self.of(lax.axis_index("y")) + self.from_y.astype(f32)
-        return self.from_y.astype(f32)
-
-    def send_h(self):
-        mine = lax.axis_index("h")
-        if lax.axis_size("h") == 2:
-            self.from_h = swap(pick(self.near(), 1 - mine, 0).astype(bf16), "h")
-        else:
-            self.from_h = lax.psum_scatter(self.near().astype(bf16), "h", scatter_dimension=0)
-
-    def total(self):
-        if lax.axis_size("h") == 2:
-            return pick(self.near(), lax.axis_index("h"), 0) + self.from_h.astype(f32)
-        return self.from_h.astype(f32)
-
-
-def share_columns(weight, place, columns):
+class Names:
+    def __getattr__(self, name):
+        return name
+
+
+n = Names()
+
+
+class Live:
+    def __init__(self, **values):
+        self.v = dict(values)
+        self.binary = binary_copies()
+        self.at = {axis: lax.axis_index(axis) for axis in AXES}
+
+    def sync(self, *names):
+        self.v.update(zip(names, lax.optimization_barrier([self.v[name] for name in names])))
+
+    def swap(self, name, value, axis):
+        self.v[name] = swap(value(), axis) if self.binary else jnp.zeros((8, 128), bf16)
+
+    def send(self, *names):
+        for name in names:
+            weight, way = name.split("__")
+            source = weight if len(way) == 1 else weight + "__" + way[:-1]
+            axis = "h" if way[-1] == "f" else way[-1]
+            self.swap(name, lambda: self.v[source], axis)
+
+    def gathered(self, weight):
+        own = self.v[weight]
+        if not self.binary:
+            return lax.all_gather(own, COPIES, axis=0, tiled=True)
+        rows, blocks, pieces, offsets = own.shape[0], [], [], []
+        for way in ("", "y", "c", "yc", "f", "fy", "fc", "fyc"):
+            y, c = self.at["y"] ^ ("y" in way), self.at["c"] ^ ("c" in way)
+            f = self.at["h"] ^ ("f" in way)
+            place = f * 4 + y * 2 + c if weight == n.out else y * 4 + c * 2 + f
+            pieces.append((len(blocks), 0, rows))
+            offsets.append(place * rows)
+            blocks.append(self.v[weight + "__" + way] if way else own)
+        return lay(blocks, pieces, offsets)
+
+    def near(self, weight, y, f):
+        c, total = self.at["c"], 0.0
+        for value in (self.v[weight + "_g"], self.v[weight + "_g__c"]):
+            rows, cols = value.shape
+            place = f * 4 + y * 2 + c if weight == n.out else y * 4 + c * 2 + f
+            value = lax.dynamic_slice_in_dim(value, place * (rows // 8), rows // 8, 0)
+            total = total + value.astype(f32)
+        return total
+
+    def add(self, *names):
+        for name in names:
+            weight, way = name.split("_g__")
+            y, f = self.at["y"], self.at["h"]
+            if way == "c":
+                self.swap(name, lambda: self.v[weight + "_g"], "c")
+            elif way in ("y0", "y1"):
+                which = 1 - f if way == "y0" else f
+                self.swap(name, lambda: self.near(weight, 1 - y, which).astype(bf16), "y")
+            else:
+                first = weight + "_g__y0"
+                self.swap(
+                    name,
+                    lambda: (self.near(weight, y, 1 - f) + self.v[first].astype(f32)).astype(bf16),
+                    "h",
+                )
+
+    def summed(self, weight):
+        grad = weight + "_g"
+        if not self.binary:
+            return lax.psum_scatter(
+                self.v[grad], COPIES, scatter_dimension=0, tiled=True
+            ).astype(f32)
+        value = self.near(weight, self.at["y"], self.at["h"])
+        return value + self.v[grad + "__y1"].astype(f32) + self.v[grad + "__f"].astype(f32)
+
+
+def share_columns(weight, place, columns, group=("p", "q")):
     pieces = [columns(weight, t) for t in range(4)]
     got = []
     for mask in range(4):
         piece = lax.select_n(place, *[pieces[t ^ mask] for t in range(4)])
-        got.append(piece if mask == 0 else across(piece, mask))
+        got.append(piece if mask == 0 else across(piece, mask, group))
     return jnp.concatenate(
         [lax.select_n(place, *[got[t ^ spot] for t in range(4)]) for spot in range(4)]
     )
 
 
-def return_columns(grad, place):
+def return_columns(grad, place, group=("p", "q")):
     value = grad.reshape(4, grad.shape[0] // 4, grad.shape[1])
     got = [pick(value, place, 0).astype(f32)]
     for mask in (1, 2, 3):
-        got.append(across(pick(value, place ^ mask, 0).astype(bf16), mask).astype(f32))
+        got.append(across(pick(value, place ^ mask, 0).astype(bf16), mask, group).astype(f32))
     return [lax.select_n(place, *[got[t ^ spot] for t in range(4)]) for spot in range(4)]
 
 
-def reduce_copies(grad):
-    return lax.psum_scatter(grad, COPIES, scatter_dimension=0, tiled=True)
-
-
-def reduce_tall(grad):
-    axes = ("h", "y", "c") if binary_copies() else COPIES
-    return lax.psum_scatter(grad, axes, scatter_dimension=0, tiled=True)
+def both_halves(own, other):
+    first = lax.axis_index("h") == 0
+    return jnp.where(first, jnp.concatenate([own, other]), jnp.concatenate([other, own]))
+
+
+def gather_halves(own, other, tall):
+    if not binary_copies():
+        return lax.all_gather(own, COPIES, axis=0, tiled=True)
+    both = both_halves(own, other)
+    if not tall:
+        return lax.all_gather(both, ("y", "c"), axis=0, tiled=True)
+    both = both.reshape(2, -1, own.shape[1])
+    return lax.all_gather(both, ("y", "c"), axis=1, tiled=True).reshape(-1, own.shape[1])
+
+
+def sum_near(grad, tall):
+    if not binary_copies():
+        return lax.psum_scatter(grad, COPIES, scatter_dimension=0, tiled=True)
+    cols = grad.shape[1]
+    if tall:
+        grad = grad.reshape(2, -1, cols)
+        return lax.psum_scatter(grad, ("y", "c"), scatter_dimension=1, tiled=True)
+    return lax.psum_scatter(grad, ("y", "c"), scatter_dimension=0, tiled=True).reshape(2, -1, cols)
+
+
+def other_half(part):
+    if not binary_copies():
+        return jnp.zeros((8, 128), bf16)
+    return swap(pick(part, 1 - lax.axis_index("h"), 0), "h")
+
+
+def sum_halves(part, other):
+    if not binary_copies():
+        return part.astype(f32)
+    return pick(part, lax.axis_index("h"), 0).astype(f32) + other.astype(f32)
 
 
 def row_owner_moves():
     total = 1
     for axis in AXES:
         total *= lax.axis_size(axis)
-    if binary_copies():
-        pairs = []
-        for g in range(total):
-            yc, h, pq = g // 8, g // 4 % 2, g % 4
-            pairs.append((g, pq * 8 + h * 4 + yc))
-        return pairs
-    copies = total // 4
-    return [(g, (g % copies) * 4 + g // copies) for g in range(total)]
+    if not binary_copies():
+        copies = total // 4
+        return [(g, (g % copies) * 4 + g // copies) for g in range(total)]
+    pairs = []
+    for g in range(total):
+        y, c, h, p, q = (g >> bit & 1 for bit in (4, 3, 2, 1, 0))
+        to = (p, q, h, y, c)
+        pairs.append((g, sum(bit << (4 - i) for i, bit in enumerate(to))))
+    return pairs
 
 
 def dot_nn(a, b):
@@ -569,35 +629,34 @@
             axis=1,
         )
 
-    moves = row_owner_moves()
-    back = [(b, a) for a, b in moves]
-
-    in_rows = share_columns(in_weight, place, in_columns)
-    for axis in ("q", "p", "c", "y", "h"):
+    def inverse(pairs):
+        return [(b, a) for a, b in pairs]
+
+    out_moves, down_moves = row_owner_moves(), row_owner_moves()
+    live = Live(x=x_own, dy=dy_own, ffn_in=ffn_in, ffn_out=ffn_out, out_weight=out_weight)
+    v, sync, send, add = live.v, live.sync, live.send, live.add
+
+    v[n.inp] = share_columns(in_weight, place, in_columns)
+    for axis in ("q", "p", "c", "y"):
         packed = stack_axis(packed, axis)
-    packed = jnp.moveaxis(packed, 0, 2)
-    in_rows, packed, ffn_in, out_weight = together(in_rows, packed, ffn_in, out_weight)
-    in_h = half_swap(in_rows)
-    in_y, in_c = near_copies(in_rows)
-    gateup_rows = share_columns(ffn_in, place, gateup_columns)
-    out_rows = lax.ppermute(out_weight, AXES, moves)
-    in_h, in_y, in_c, gateup_rows, out_rows, x_send = together(
-        in_h, in_y, in_c, gateup_rows, out_rows, x_own
-    )
-    in_hy, in_hc = near_copies(in_h)
-    in_yc = core_swap(in_y)
-    x_group = gather_group(x_send)
-    out_h = half_swap(out_rows)
-    out_y, out_c = near_copies(out_rows)
-    in_hy, in_hc, in_yc, x_group, out_h, out_y, out_c, ffn_out, gateup_rows, dy_send = together(
-        in_hy, in_hc, in_yc, x_group, out_h, out_y, out_c, ffn_out, gateup_rows, dy_own
-    )
-    w_gateup = lax.all_gather(gateup_rows, COPIES, axis=0, tiled=True)
-    in_hyc = core_swap(in_hy)
-    down_rows = lax.ppermute(ffn_out, AXES, moves)
-    dy_group = gather_group(dy_send)
-    out_hy, out_hc = near_copies(out_h)
-    out_yc = core_swap(out_y)
+    sync(n.inp, n.out_weight, n.ffn_in)
+    send(n.inp__f, n.inp__y, n.inp__c)
+    v[n.gateup] = share_columns(v[n.ffn_in], place, gateup_columns)
+    v[n.out] = lax.ppermute(v[n.out_weight], AXES, out_moves)
+    v[n.packed] = packed
+    sync(n.inp__f, n.inp__y, n.inp__c, n.x, n.out, n.packed)
+    send(n.inp__fy, n.inp__fc, n.inp__yc)
+    v[n.x1], v[n.x2] = two_of(v[n.x])
+    v[n.x3] = last_of(v[n.x])
+    send(n.out__f, n.out__y, n.out__c)
+    v[n.packed] = jnp.moveaxis(stack_axis(v[n.packed], "h"), 0, 2)
+    sync(n.inp__fy, n.inp__fc, n.inp__yc, n.x1, n.x2, n.x3, n.out__f, n.out__y, n.out__c, n.gateup, n.packed)
+    send(n.inp__fyc, n.out__fy, n.out__fc, n.out__yc)
+    v[n.gate], v[n.up] = v[n.gateup][:, :quarter], v[n.gateup][:, quarter:]
+    v[n.gate__f] = half_swap(v[n.gate])
+    sync(n.inp__fyc, n.out__fy, n.out__fc, n.out__yc, n.gate, n.up, n.ffn_out, n.dy)
+    send(n.out__fyc)
+    packed = v[n.packed]
     everyone = packed.reshape(sizes[0], sizes[1], -1, padded)
 
     def small_part(i):
@@ -637,14 +696,14 @@
     keep = jnp.broadcast_to((final == before).astype(f32), (count, SPAN))
     rows = jnp.stack([seg_blocks, keep] + [jnp.zeros((count, SPAN), f32)] * 6, axis=1)
 
-    x_group = in_order(x_group)
-    w_in = all_copies(in_rows, (in_y, in_c, in_yc, in_h, in_hy, in_hc, in_hyc))
+    x_group = in_order([x_own, v[n.x1], v[n.x2], v[n.x3]])
+    w_in = live.gathered(n.inp)
     n1 = normed(x_group.astype(f32), gain_one).astype(bf16)
     proj = mm(n1, w_in)
     mixer = Mixer(place, count, tokens // SPAN)
     state_shape = (VAL, KEY)
     scratch = [pltpu.VMEM(state_shape, f32), pltpu.VMEM((1, KEY), f32)]
-    sums, raw, prior, through, end, decay = mixer.call(
+    sums, raw, prior, through, v[n.end], decay = mixer.call(
         states_kernel,
         ["rows", "whole", "whole", "tokens", "blocks"],
         [proj, up_head, bias_head, meta, rows],
@@ -659,15 +718,15 @@
         scratch,
         flops=2 * rows_all * KEY * VAL,
     )
-    end, down_rows, out_hy, out_hc, out_yc, dy_group = together(
-        end, down_rows, out_hy, out_hc, out_yc, dy_group
-    )
-    entering = from_earlier(end, decay)
-    out_hyc = core_swap(out_hy)
-    entering, out_hyc, down_rows = together(entering, out_hyc, down_rows)
-    w_out = all_copies(out_rows, (out_y, out_c, out_yc, out_h, out_hy, out_hc, out_hyc), True)
-    down_h = half_swap(down_rows)
-    down_y, down_c = near_copies(down_rows)
+    v[n.w_out] = live.gathered(n.out)
+    sync(n.end, n.ffn_out, n.w_out)
+    w_out = v[n.w_out]
+    v[n.entering] = from_earlier(v[n.end], decay)
+    v[n.down] = lax.ppermute(v[n.ffn_out], AXES, down_moves)
+    entering = v[n.entering]
+    sync(n.entering, n.gate, n.gate__f, n.up)
+    v[n.up__f] = half_swap(v[n.up])
+    w_gate = gather_halves(v[n.gate], v[n.gate__f], False)
     gated, mixed = mixer.call(
         mixed_kernel,
         ["rows", "rows", "blocks", "blocks", "whole", "whole", "tokens", "blocks"],
@@ -676,40 +735,62 @@
         flops=2 * rows_all * (KEY * VAL + SPAN * (KEY + VAL)),
     )
     mix_parts = mm(gated, w_out).reshape(4, tokens, width)
-    mix = scatter_group([mix_parts[m] for m in range(4)])
-    mix, down_h, down_y, down_c = together(mix, down_h, down_y, down_c)
+    mix_own = mix_parts[0]
+    v[n.mix_send] = shares(mix_parts)
+    sync(n.mix_send)
+    v[n.mix1], v[n.mix2] = across(v[n.mix_send][1], 1), across(v[n.mix_send][2], 2)
+    sync(n.mix1, n.mix2, n.mix_send, n.down, n.up, n.up__f)
+    v[n.down__f] = half_swap(v[n.down])
+    v[n.w_up] = gather_halves(v[n.up], v[n.up__f], False)
+    v[n.w_gate] = w_gate
+    v[n.mix3] = across(v[n.mix_send][3], 3)
+    sync(n.mix3)
+    mix = add_shares(mix_own, (v[n.mix1], v[n.mix2], v[n.mix3]))
     h1 = x_own.astype(f32) + mix
-    n2_group = gather_group(normed(h1, gain_two).astype(bf16))
-    down_hy, down_hc = near_copies(down_h)
-    down_yc = core_swap(down_y)
-    n2_group, down_hy, down_hc, down_yc = together(n2_group, down_hy, down_hc, down_yc)
-    down_hyc = core_swap(down_hy)
-    w_down = all_copies(
-        down_rows, (down_y, down_c, down_yc, down_h, down_hy, down_hc, down_hyc), True
-    )
-    n2_group = in_order(n2_group)
-    dy_group = in_order(dy_group)
+    v[n.n2] = normed(h1, gain_two).astype(bf16)
+    v[n.n21], v[n.n22] = two_of(v[n.n2])
+    sync(n.n21, n.n22, n.n2, n.dy, n.down, n.down__f, n.w_gate, n.w_up)
+    w_gate, w_up = v[n.w_gate], v[n.w_up]
+    w_down = gather_halves(v[n.down], v[n.down__f], True)
+    v[n.n23] = last_of(v[n.n2])
+    sync(n.n21, n.n22, n.n23, n.n2, n.dy)
+    v[n.dy1], v[n.dy2] = two_of(v[n.dy])
+    v[n.dy3] = last_of(v[n.dy])
+    n2_group = in_order([v[n.n2], v[n.n21], v[n.n22], v[n.n23]])
+    dy_group = in_order([dy_own, v[n.dy1], v[n.dy2], v[n.dy3]])
+    gate = mm(n2_group, w_gate)
+    up = mm(n2_group, w_up)
     grad_hidden = mm_nt(dy_group, w_down)
 
-    gateup = mm(n2_group, w_gateup)
-    gate, up = gateup[:, :quarter], gateup[:, quarter:]
     sig = jax.nn.sigmoid(gate)
     hidden = (gate * sig * up).astype(bf16)
-    grad_gu = jnp.concatenate(
-        [grad_hidden * up * sig * (1.0 + gate * (1.0 - sig)), grad_hidden * gate * sig], axis=1
-    ).astype(bf16)
-    n2_grad_parts = mm_nt(grad_gu, w_gateup).reshape(4, tokens, width)
-    grad_gu, hidden, n2_grad_parts = together(grad_gu, hidden, n2_grad_parts)
-    n2_grad = scatter_group([n2_grad_parts[m] for m in range(4)])
-    y_parts = mm(hidden, w_down).reshape(4, tokens, width)
-    gateup_sum = reduce_copies(mm_tn(n2_group, grad_gu, bf16))
-    down_sum = reduce_tall(mm_tn(hidden, dy_group, bf16))
-
+    grad_g = (grad_hidden * up * sig * (1.0 + gate * (1.0 - sig))).astype(bf16)
+    grad_u = (grad_hidden * gate * sig).astype(bf16)
+    n2_grad_parts = (mm_nt(grad_g, w_gate) + mm_nt(grad_u, w_up)).reshape(4, tokens, width)
+    v[n.n2_send] = shares(n2_grad_parts)
+    v[n.grad_g], v[n.grad_u], v[n.hidden] = grad_g, grad_u, hidden
+    sync(n.n2_send, n.grad_g, n.grad_u, n.hidden)
+    v[n.s1], v[n.s2] = across(v[n.n2_send][1], 1), across(v[n.n2_send][2], 2)
+    v[n.gate_g] = mm_tn(n2_group, v[n.grad_g], bf16)
+    sync(n.s1, n.s2, n.n2_send, n.hidden, n.grad_u, n.gate_g)
+    v[n.gate_part] = sum_near(v[n.gate_g], False)
+    v[n.up_g] = mm_tn(n2_group, v[n.grad_u], bf16)
+    v[n.s3] = across(v[n.n2_send][3], 3)
+    sync(n.s3, n.hidden, n.up_g)
+    v[n.up_part] = sum_near(v[n.up_g], False)
+    n2_grad = add_shares(n2_grad_parts[0], (v[n.s1], v[n.s2], v[n.s3]))
     h1_grad_part, gain_two_grad = normed_grad(h1, gain_two, n2_grad)
     h1_grad = dy_own.astype(f32) + h1_grad_part
-    mix_grad = in_order(gather_group(h1_grad.astype(bf16)))
+    v[n.dmix] = h1_grad.astype(bf16)
+    v[n.dmix1], v[n.dmix2] = two_of(v[n.dmix])
+    v[n.down_g] = mm_tn(v[n.hidden], dy_group, bf16)
+    sync(n.dmix, n.dmix1, n.dmix2, n.hidden, n.down_g)
+    v[n.down_part] = sum_near(v[n.down_g], True)
+    v[n.dmix3] = last_of(v[n.dmix])
+    sync(n.dmix, n.dmix1, n.dmix2, n.dmix3)
+    mix_grad = in_order([v[n.dmix], v[n.dmix1], v[n.dmix2], v[n.dmix3]])
     grad_gated = mm_nt(mix_grad, w_out)
-    grad_o, grad_gate, later, beyond, start, decay_b, head_grad = mixer.call(
+    grad_o, grad_gate, later, beyond, v[n.start], decay_b, head_grad = mixer.call(
         gate_grad_kernel,
         ["rows", "rows", "rows", "rows", "whole", "tokens", "blocks"],
         [grad_gated, proj, mixed, sums, gain_head, meta, rows],
@@ -726,12 +807,17 @@
         reverse=True,
         flops=2 * rows_all * KEY * VAL,
     )
-    leaving = from_later(start, decay_b)
-    y = scatter_group([after(y_parts[m], mix_grad) for m in range(4)])
-    out_sum = Summing(mm_tn(gated, mix_grad, bf16), True)
-    leaving, out_sum.from_c = together(leaving, out_sum.from_c)
-    out_sum.send_y()
-    grad_proj, rank_grad, bias_grad = mixer.call(
+    sync(n.start, n.hidden)
+    y_parts = mm(v[n.hidden], w_down).reshape(4, tokens, width)
+    v[n.y_send] = shares(y_parts)
+    v[n.leaving] = from_later(v[n.start], decay_b)
+    v[n.out_g] = mm_tn(gated, mix_grad, bf16)
+    sync(n.leaving, n.y_send, n.out_g, n.gate_part)
+    v[n.gate_other] = other_half(v[n.gate_part])
+    v[n.y1], v[n.y2] = across(v[n.y_send][1], 1), across(v[n.y_send][2], 2)
+    add(n.out_g__c)
+    leaving = v[n.leaving]
+    v[n.grad_proj], rank_grad, bias_grad = mixer.call(
         inputs_grad_kernel,
         ["rows"] * 5 + ["blocks", "blocks", "whole", "blocks", "blocks", "whole", "whole", "tokens", "blocks"],
         [
@@ -757,31 +843,68 @@
         ],
         flops=2 * rows_all * (3 * KEY * VAL + SPAN * (3 * KEY + 2 * VAL)),
     )
-    n1_grad_parts = mm_nt(grad_proj, w_in).reshape(4, tokens, width)
-    n1_grad_parts, out_sum.from_y, grad_proj, y = together(
-        n1_grad_parts, out_sum.from_y, grad_proj, y
-    )
-    n1_grad = scatter_group([n1_grad_parts[m] for m in range(4)])
-    out_sum.send_h()
-    in_sum = Summing(mm_tn(n1, grad_proj, bf16))
-    n1_grad, in_sum.from_c, out_sum.from_h = together(n1_grad, in_sum.from_c, out_sum.from_h)
-    in_sum.send_y()
-    outproj_grad = lax.ppermute(out_sum.total().astype(bf16), AXES, back)
-    input_part, gain_one_grad = normed_grad(x_own.astype(f32), gain_one, n1_grad)
+    n1_grad_all = mm_nt(v[n.grad_proj], w_in)
+    n1_grad_parts = n1_grad_all.reshape(4, tokens, width)
+    v[n.n1_send] = shares(n1_grad_parts)
+    sync(n.n1_send, n.grad_proj, n.y1, n.y2, n.y_send, n.out_g, n.out_g__c, n.gate_other, n.up_part)
+    v[n.up_other] = other_half(v[n.up_part])
+    v[n.t1], v[n.t2] = across(v[n.n1_send][1], 1), across(v[n.n1_send][2], 2)
+    v[n.y3] = across(v[n.y_send][3], 3)
+    add(n.out_g__y0, n.out_g__y1)
+    x_all = x_group.astype(f32)
+    x_scale = lax.rsqrt(jnp.mean(x_all * x_all, axis=-1, keepdims=True) + EPS)
+    gain_one_grad = jnp.sum(n1_grad_all * (x_all * x_scale), axis=0)
+    each = width // devices
+    decay_part = jnp.concatenate([rank_grad[:RANK], bias_grad], axis=0)
+    decay_part = decay_part.reshape(RANK + 1, KEY // up_cols, up_cols).transpose(1, 0, 2)
+    decay_part = decay_part.reshape(KEY // up_cols, -1)
+    spare = -(-decay_part.shape[1] // each)
+    decay_part = jnp.pad(decay_part, ((0, 0), (0, spare * each - decay_part.shape[1])))
+    decay_part = decay_part.reshape(KEY // up_cols * each, spare)
+    head_slot = lax.broadcasted_iota(jnp.int32, (HEADS, 1, 1), 0) == place
+    decay_part = jnp.where(head_slot, decay_part[None], 0.0).reshape(width, spare)
+    head_part = head_grad.reshape(devices, -1)
+    head_each = head_part.shape[1]
+    head_part = jnp.pad(head_part, ((0, 0), (0, each - head_each))).reshape(width)
+    singles = jnp.stack([gain_one_grad, gain_two_grad, head_part], axis=1)
+    extras = jnp.concatenate([singles, decay_part], axis=1)
+    first = RANKS + RANK
+    extras = jnp.pad(extras, ((0, 0), (first, RANKS + LANES - first - extras.shape[1])))
+    v[n.inp_g] = (mm_tn(n1, v[n.grad_proj]) + extras).astype(bf16)
+    sync(n.n1_send, n.t1, n.t2, n.inp_g, n.out_g__y0, n.out_g__y1, n.out_g, n.y3)
+    v[n.t3] = across(v[n.n1_send][3], 3)
+    add(n.inp_g__c)
+    sync(n.inp_g, n.inp_g__c)
+    add(n.inp_g__y0, n.inp_g__y1)
+    sync(n.t3, n.gate_other, n.gate_part, n.up_other, n.up_part, n.down_part, n.out_g, n.out_g__y0)
+    v[n.gate_back] = return_columns(sum_halves(v[n.gate_part], v[n.gate_other]), place)
+    v[n.up_back] = return_columns(sum_halves(v[n.up_part], v[n.up_other]), place)
+    v[n.down_other] = other_half(v[n.down_part])
+    add(n.out_g__f)
+    n1_grad = add_shares(n1_grad_parts[0], (v[n.t1], v[n.t2], v[n.t3]))
+    input_part, _ = normed_grad(x_own.astype(f32), gain_one, n1_grad)
     input_grad = (h1_grad + input_part).reshape(1, tokens, width)
-    in_sum.from_y, outproj_grad, gateup_sum, down_sum = together(
-        in_sum.from_y, outproj_grad, gateup_sum, down_sum
-    )
-    in_sum.send_h()
-    gateup_back = return_columns(gateup_sum, place)
-    ffnout_grad = lax.ppermute(down_sum, AXES, back)
-    in_sum.from_h, gateup_back, ffnout_grad = together(in_sum.from_h, gateup_back, ffnout_grad)
-    in_back = return_columns(in_sum.total(), place)
+    sync(n.inp_g, n.inp_g__y0, n.gate_back, n.up_back, n.y1, n.y2, n.y3)
+    add(n.inp_g__f)
+    y = add_shares(y_parts[0], (v[n.y1], v[n.y2], v[n.y3]))
+    result = h1 + y
+    block_out = result.astype(bf16).reshape(1, tokens, width)
+    kept = valid_mask.reshape(tokens, 1).astype(f32)
+    squares = jnp.stack(
+        [jnp.sum(kept * result * result), jnp.sum(kept * mix * mix), jnp.sum(kept * y * y)]
+    )
+    squares = sum_group(jnp.pad(squares, (0, 125)).reshape(1, 128), ("p", "q"))
+    v[n.squares] = sum_group(squares, ("y", "c"))
+    sync(n.inp_g__f, n.inp_g__y1, n.inp_g, n.out_g, n.out_g__f, n.squares, n.down_other)
+    v[n.squares] = sum_over(v[n.squares], "h")
+    gate_back, up_back = v[n.gate_back], v[n.up_back]
+    in_back = return_columns(live.summed(n.inp), place)
+    down_sum = sum_halves(v[n.down_part], v[n.down_other])
+    v[n.ffnout] = lax.ppermute(down_sum.astype(bf16), AXES, inverse(down_moves))
+    outproj_grad = lax.ppermute(live.summed(n.out).astype(bf16), AXES, inverse(out_moves))
+    ffnout_grad = v[n.ffnout]
     ffnout_grad, outproj_grad = ffnout_grad.astype(f32), outproj_grad.astype(f32)
-    ffnin_grad = jnp.concatenate(
-        [part[:, :quarter] for part in gateup_back] + [part[:, quarter:] for part in gateup_back],
-        axis=1,
-    )
+    ffnin_grad = jnp.concatenate(gate_back + up_back, axis=1)
     inproj_grad = jnp.concatenate(
         [part[:, :KEYS] for part in in_back]
         + [part[:, KEYS:VALUES] for part in in_back]
@@ -790,35 +913,13 @@
         + [sum(part[:, RANKS : RANKS + RANK] for part in in_back)],
         axis=1,
     )
-    result = h1 + y
-    block_out = result.astype(bf16).reshape(1, tokens, width)
-    live = valid_mask.reshape(tokens, 1).astype(f32)
-    squares = jnp.stack(
-        [jnp.sum(live * result * result), jnp.sum(live * mix * mix), jnp.sum(live * y * y)]
-    )
-
-    head_slot = (lax.broadcasted_iota(jnp.int32, (HEADS, 1, 1), 0) == place).astype(f32)
-    decay_part = head_slot * jnp.concatenate([rank_grad[:RANK], bias_grad], axis=0)[None]
-    sums_of = [squares, head_grad.reshape(-1), gain_two_grad, decay_part.reshape(-1), gain_one_grad]
-    total = jnp.concatenate(sums_of)
-    short = -total.shape[0] % 1024
-    total = after(jnp.pad(total, (0, short)).reshape(-1, 128), in_sum.from_y)
-    total = sum_all(total).reshape(-1)
-    ends = [0]
-    for part in sums_of:
-        ends.append(ends[-1] + part.shape[0])
-    squares = total[: ends[1]]
+    squares = v[n.squares].reshape(-1)[:3]
     root_means = jnp.sqrt(squares / (jnp.maximum(valid_count, 1.0) * width))
-
-    def own(value, length):
-        return lax.dynamic_slice(value, (me * length,), (length,))
-
-    headgain_grad = own(total[ends[1] : ends[2]], head_gain.shape[0])
-    ffngain_grad = own(total[ends[2] : ends[3]], ffn_gain.shape[0])
-    mixgain_grad = own(total[ends[4] : ends[5]], mixer_gain.shape[0])
-    decay_all = total[ends[3] : ends[4]].reshape(HEADS, RANK + 1, KEY)
-    decay_all = decay_all.transpose(1, 0, 2).reshape(RANK + 1, HEADS * KEY)
-    decay_own = lax.dynamic_slice(decay_all, (0, me * up_cols), (RANK + 1, up_cols))
+    spares = sum(part[:, first:] for part in in_back)
+    mixgain_grad, ffngain_grad = spares[:, 0], spares[:, 1]
+    headgain_grad = spares[:head_each, 2]
+    decay_own = spares[:, 3 : 3 + spare].reshape(-1)[: (RANK + 1) * up_cols]
+    decay_own = decay_own.reshape(RANK + 1, up_cols)
     return (
         block_out,
         input_grad,

time: 774 us -> 714 us (0.922)
  waiting for transfers between devices: 401 us -> 310 us
  local copies, waits for them, and re-layouts: 48.7 us -> 73.8 us
  matrix products: 72.4 us -> 89.6 us
  starting transfers between devices: 125 us -> 115 us
    ppermute x40 -> x49, waiting for transfers between devices: 280 us -> 175 us  [the longest x45 131 us: across(): return lax.ppermute(value, group, [(i, i ^ mask) for i in range(4)])]
    unnamed x180 -> x263, local copies, waits for them, and re-layouts: 32.3 us -> 48.4 us
    reduce_scatter x2 -> x3, waiting for transfers between devices: 0.02 us -> 11.8 us  [the longest x1 11.8 us: sum_near(): return lax.psum_scatter(grad, ('y', 'c'), scatter_dimension=1, tiled=True)]
    ppermute x40 -> x49, starting transfers between devices: 71.5 us -> 60.2 us  [the longest x45 47.8 us: across(): return lax.ppermute(value, group, [(i, i ^ mask) for i in range(4)])]
    ppermute x1, waiting for transfers between devices: 9.55 us -> 0.01 us  [from_later(): return lax.ppermute(start, 'h', [(1, 0)])]
    all_gather x1 -> x3, waiting for transfers between devices: 0.01 us -> 9.36 us  [the longest x2 8.89 us: gather_halves(): return lax.all_gather(both, ('y', 'c'), axis=0, tiled=True)]
    dot_general x4 -> x5, matrix products: 25.3 us -> 34.6 us  [mm(): return jnp.dot(left, right, preferred_element_type=f32).astype(out)]
    dot_general x4 -> x5, matrix products: 25.1 us -> 29.8 us  [dot_tn(): lax.dot_general(a, b, (((0,), (0,)), ((), ())), preferred_element_type=f32)]
  transfers between devices with their start and end apart: 82 -> 91, of which waited for: 40 -> 43; matrix products, arithmetic and copies ran while one was open for 14% -> 20% of each run, Pallas kernels for 6% -> 6%
where the time goes in v3:
time: 714 us; the launch traced here: 703 us
  waiting for transfers between devices  310 us (43%)
  starting transfers between devices  115 us (16%)
  matrix products  89.6 us (13%)
  local copies, waits for them, and re-layouts  73.8 us (10%)
  other arithmetic  57.9 us (8%)
  Pallas kernels  39.9 us (6%)
  between operations  16.9 us (2%)
    ppermute x45, waiting for transfers between devices, across(): return lax.ppermute(value, group, [(i, i ^ mask) for i in range(4)])  131 us
    ppermute x34, waiting for transfers between devices, swap(): return lax.ppermute(value, axis, [(0, 1), (1, 0)])  102 us
    ppermute x34, starting transfers between devices, swap(): return lax.ppermute(value, axis, [(0, 1), (1, 0)])  49.7 us
    unnamed x263, local copies, waits for them, and re-layouts  48.4 us
    ppermute x45, starting transfers between devices, across(): return lax.ppermute(value, group, [(i, i ^ mask) for i in range(4)])  47.8 us
    dot_general x5, matrix products, mm(): return jnp.dot(left, right, preferred_element_type=f32).astype(out)  34.6 us
    pallas_call x4, Pallas kernels, call(): pl.pallas_call(kernel, grid_spec=pltpu.PrefetchScalarGridSpec(num_scalar_...  31 us
    dot_general x5, matrix products, dot_tn(): lax.dot_general(a, b, (((0,), (0,)), ((), ())), preferred_element_type=f32)  29.8 us
  transfers between devices with their start and end apart: 91, of which 43 were waited for; matrix products, arithmetic and copies ran while one was open for 20% of the time, Pallas kernels for 6%

profile of v3, /device:TPU:8, one launch (start us, length us, event | category | flops | bytes accessed | tf_op | source)
XLA Modules:
  0.0 702.6 jit_solution(2128851653407881056)
XLA Ops:
  22.2 7.3 %collective-permute-done.8 = bf16[2,8,128]{2,1,0:T(8,128)(2,1)S(1)} collective-permute-done((bf16[2,8,128]{2,1,0:T(8,128)(2,1)S(1)}, bf16[2,8,128]{2,1,0:T(8,128)(2,1)S(1)}, u32[]{:S(2)}, u32[]{:S(2)}) %collective-permute-start.8) | collective-permute-done | bytes 4128 | tf_op jit(solution)/shard_map/ppermute | solution.py:36
  41.4 21.2 %collective-permute-done.6.refs_0_ = bf16[64,2048]{1,0:T(8,128)(2,1)S(1)} collective-permute-done((bf16[64,2048]{1,0:T(8,128)(2,1)S(1)}, bf16[64,2048]{1,0:T(8,128)(2,1)S(1)}, u32[]{:S(2)}, u32[]{:S(2)}) %collective-permute-start.6) | collective-permute-done | bytes 262176 | tf_op jit(solution)/shard_map/ppermute | solution.py:645
  65.2 7.4 %collective-permute-done.3.refs_4_ = bf16[256,1664]{1,0:T(8,128)(2,1)S(1)} collective-permute-done((bf16[256,1664]{1,0:T(8,128)(2,1)S(1)}, bf16[256,1664]{1,0:T(8,128)(2,1)S(1)}, u32[]{:S(2)}, u32[]{:S(2)}) %collective-permute-start.3) | collective-permute-done | bytes 852000 | tf_op jit(solution)/shard_map/ppermute | solution.py:36
  103.5 8.1 %collective-permute-done.15.refs_2_ = bf16[128,2048]{1,0:T(8,128)(2,1)S(1)} collective-permute-done((bf16[128,2048]{1,0:T(8,128)(2,1)S(1)}, bf16[128,2048]{1,0:T(8,128)(2,1)S(1)}, u32[]{:S(2)}, u32[]{:S(2)}) %collective-permute-start.15) | collective-permute-done | bytes 524320 | tf_op jit(solution)/shard_map/ppermute | solution.py:40
  142.4 7.5 %shard_map.222 = (f32[512,256]{1,0:T(8,128)S(1)}, f32[512,256]{1,0:T(8,128)S(1)}, bf16[8,512,256]{2,1,0:T(8,128)(2,1)S(1)}, f32[8,1,256]{2,1,0:T(1,128)S(1)}, bf...) custom-call(s32[1]{0:T(128)} %bitcast.1.place, f32[512,1664]{1,0:T(8,128)} %fusion.25.proj, bf16[128,256]{1,0:T(8,128)(2,1)S(1)} %pad.33.up, ...), custom_call_target="tpu_custom_call" | custom-call | flops 134217728 | bytes 7014400 | tf_op jit(solution)/shard_map/pallas_call | solution.py:503
  158.5 10.9 %collective-permute-done.29.entering = bf16[512,256]{1,0:T(8,128)(2,1)S(1)} collective-permute-done((bf16[512,256]{1,0:T(8,128)(2,1)S(1)}, bf16[512,256]{1,0:T(8,128)(2,1)S(1)}, u32[]{:S(2)}, u32[]{:S(2)}) %collective-permute-start.29) | collective-permute-done | bytes 262176 | tf_op jit(solution)/shard_map/ppermute | solution.py:555
  182.7 6.7 shard_map.224
  194.6 11.5 %collective-permute-done.32 = bf16[176,2048]{1,0:T(8,128)(2,1)} collective-permute-done((bf16[176,2048]{1,0:T(8,128)(2,1)}, bf16[176,2048]{1,0:T(8,128)(2,1)}, u32[]{:S(2)}, u32[]{:S(2)}) %collective-permute-start.32) | collective-permute-done | bytes 720928 | tf_op jit(solution)/shard_map/ppermute | solution.py:725
  207.2 9.9 %collective-permute-done.31 = bf16[128,2048]{1,0:T(8,128)(2,1)} collective-permute-done((bf16[128,2048]{1,0:T(8,128)(2,1)S(1)}, bf16[128,2048]{1,0:T(8,128)(2,1)}, u32[]{:S(2)}, u32[]{:S(2)}) %collective-permute-start.31) | collective-permute-done | bytes 524320 | tf_op jit(solution)/shard_map/ppermute | solution.py:40
  226.8 19.5 %collective-permute-done.35 = bf16[128,2048]{1,0:T(8,128)(2,1)} collective-permute-done((bf16[128,2048]{1,0:T(8,128)(2,1)}, bf16[128,2048]{1,0:T(8,128)(2,1)}, u32[]{:S(2)}, u32[]{:S(2)}) %collective-permute-start.35) | collective-permute-done | bytes 524320 | tf_op jit(solution)/shard_map/ppermute | solution.py:40
  257.4 7.0 collective-permute-done.37.refs_2_
  266.0 8.9 %all-gather.6.cloned.1.call-done = bf16[2048,1408]{1,0:T(8,128)(2,1)} async-done(((bf16[512,1408]{1,0:T(8,128)(2,1)}), bf16[2048,1408]{1,0:T(8,128)(2,1)}) %all-gather.6.cloned.1.call-update) | async-done | bytes 5767184 | tf_op jit(solution)/shard_map/all_gather | solution.py:239
  280.0 13.7 %collective-permute-done.39.refs_3_ = bf16[128,2048]{1,0:T(8,128)(2,1)S(1)} collective-permute-done((bf16[128,2048]{1,0:T(8,128)(2,1)}, bf16[128,2048]{1,0:T(8,128)(2,1)S(1)}, u32[]{:S(2)}, u32[]{:S(2)}) %collective-permute-start.39) | collective-permute-done | bytes 524320 | tf_op jit(solution)/shard_map/ppermute | solution.py:40
  301.1 8.4 %fusion.72 = f32[512,1408]{1,0:T(8,128)} fusion(bf16[512,2048]{1,0:T(8,128)(2,1)S(1)} %shard_map.226, bf16[2048,1408]{1,0:T(8,128)(2,1)} %all-gather.4.cloned.1.call-done), kind=kOutput, calls=%fused_computation.274 | convolution fusion | flops 2952790016 | bytes 10747904 | tf_op jit(solution)/shard_map/dot_general | solution.py:537
  309.8 9.6 %collective-permute-done.41.refs_2_ = bf16[128,2048]{1,0:T(8,128)(2,1)S(1)} collective-permute-done((bf16[128,2048]{1,0:T(8,128)(2,1)}, bf16[128,2048]{1,0:T(8,128)(2,1)S(1)}, u32[]{:S(2)}, u32[]{:S(2)}) %collective-permute-start.41) | collective-permute-done | bytes 524320 | tf_op jit(solution)/shard_map/ppermute | solution.py:40
  328.7 8.0 %multiply_convert_fusion = (bf16[512,1408]{1,0:T(8,128)(2,1)}, bf16[512,1408]{1,0:T(8,128)(2,1)S(1)}, bf16[512,1408]{1,0:T(8,128)(2,1)S(1)}) fusion(f32[512,1408]{1,0:T(8,128)S(1)} %copy-done.110, f32[512,1408]{1,0:T(8,128)S(1)} %fusion.71, bf16[512,2048]{1,0:T(8,128)(2,1)S(1)} %copy-done.18, bf16[2048,1408]{1,0:T(8,128)(2,1)} %all-gather.6.cloned.1.call-done), kind=kOutput, calls=%fused_computation.13 | convolution fusion | flops 2964324352 | bytes 17956864 | tf_op jit(solution)/shard_map/dot_general | solution.py:537
  353.7 7.1 %collective-permute-done.43 = bf16[128,2048]{1,0:T(8,128)(2,1)} collective-permute-done((bf16[128,2048]{1,0:T(8,128)(2,1)}, bf16[128,2048]{1,0:T(8,128)(2,1)}, u32[]{:S(2)}, u32[]{:S(2)}) %collective-permute-start.43) | collective-permute-done | bytes 524320 | tf_op jit(solution)/shard_map/ppermute | solution.py:40
  362.8 8.9 %convolution_convert_fusion.1 = bf16[2048,1408]{1,0:T(8,128)(2,1)} fusion(bf16[512,2048]{1,0:T(8,128)(2,1)} %copy-done.17, bf16[512,1408]{1,0:T(8,128)(2,1)} %copy-done.109), kind=kOutput, calls=%fused_computation.2 | convolution fusion | flops 2955673600 | bytes 9306112 | tf_op jit(solution)/shard_map/dot_general | solution.py:290
  396.7 10.6 %collective-permute-done.48.refs_3_ = bf16[128,2048]{1,0:T(8,128)(2,1)} collective-permute-done((bf16[128,2048]{1,0:T(8,128)(2,1)}, bf16[128,2048]{1,0:T(8,128)(2,1)}, u32[]{:S(2)}, u32[]{:S(2)}) %collective-permute-start.48) | collective-permute-done | bytes 524320 | tf_op jit(solution)/shard_map/ppermute | solution.py:40
  414.2 7.5 %shard_map.228 = (bf16[512,512]{1,0:T(8,128)(2,1)S(1)}, bf16[512,512]{1,0:T(8,128)(2,1)S(1)}, bf16[8,512,256]{2,1,0:T(8,128)(2,1)}, f32[8,1,256]{2,1,0:T(1,128)S...) custom-call(s32[1]{0:T(128)} %bitcast.1.place, f32[512,512]{1,0:T(8,128)S(1)} %fusion.74.grad_gated, ...), custom_call_target="tpu_custom_call" | custom-call | flops 134217728 | bytes 12128256 | tf_op jit(solution)/shard_map/pallas_call | solution.py:503
  428.2 9.2 %fusion.70 = (bf16[512,2048]{1,0:T(8,128)(2,1)S(1)}, f32[512,2048]{1,0:T(8,128)}) fusion(bf16[512,1408]{1,0:T(8,128)(2,1)} %get-tuple-element.249, bf16[1408,2048]{1,0:T(8,128)(2,1)} %bitcast.240), kind=kOutput, calls=%fused_computation.272 | convolution fusion | flops 2953838592 | bytes 13500416 | tf_op jit(solution)/shard_map/dot_general | solution.py:537
  448.3 9.3 %shard_map.229 = (bf16[512,1664]{1,0:T(8,128)(2,1)S(1)}, f32[128,256]{1,0:T(8,128)S(1)}, f32[1,256]{1,0:T(1,128)S(1)}) custom-call(s32[1]{0:T(128)} %bitcast.1.place, f32[512,1664]{1,0:T(8,128)} %fusion.25.proj, f32[512,256]{1,0:T(8,128)S(1)} %get-tuple-element.185.sums, f32[512,256]{1,0:T(8,128)S(1)} %copy-done.53, bf16[512,512]{1,0:T(8,128)(2,1)S(1)} %copy-done.55, ...), custom_call_target="tpu_custom_call" | custom-call | flops 520093696 | bytes 20676608 | tf_op jit(solution)/shard_map/pallas_call | solution.py:503
  466.7 8.9 %fusion.3 = (f32[2048]{0:T(1024)S(1)}, bf16[512,2048]{1,0:T(8,128)(2,1)}, f32[512,2048]{1,0:T(8,128)}) fusion(bf16[512,2048]{1,0:T(8,128)(2,1)S(1)} %shard_map.220, f32[512]{0:T(512)S(1)} %copy-done.104, bf16[512,1664]{1,0:T(8,128)(2,1)S(1)} %copy-done.68, bf16[2048,1664]{1,0:T(8,128)(2,1)} %copy-done.6), kind=kOutput, calls=%fused_computation.9 | convolution fusion | flops 3494901760 | bytes 16918528 | tf_op jit(solution)/shard_map/dot_general | solution.py:286
  479.6 14.0 %collective-permute-done.53 = bf16[256,1408]{1,0:T(8,128)(2,1)S(1)} collective-permute-done((bf16[256,1408]{1,0:T(8,128)(2,1)}, bf16[256,1408]{1,0:T(8,128)(2,1)S(1)}, u32[]{:S(2)}, u32[]{:S(2)}) %collective-permute-start.53) | collective-permute-done | bytes 720928 | tf_op jit(solution)/shard_map/ppermute | solution.py:36
  501.3 8.1 %add_convert_fusion = bf16[2048,1664]{1,0:T(8,128)(2,1)} fusion(f32[2048,12]{1,0:T(8,128)} %copy.49, bf16[512,1664]{1,0:T(8,128)(2,1)} %copy-done.67, bf16[512,2048]{1,0:T(8,128)(2,1)S(1)} %shard_map.220, f32[2048]{0:T(1024)S(1)} %reshape.628, f32[512]{0:T(512)S(1)} %copy-done.104), kind=kOutput, calls=%fused_computation | convolution fusion | flops 3500670976 | bytes 10725376 | tf_op jit(solution)/shard_map/dot_general | solution.py:290
  509.4 7.0 collective-permute-done.56
  525.8 11.8 %reduce-scatter.8.cloned.1.call-done = bf16[2,176,2048]{2,1,0:T(8,128)(2,1)} async-done(((bf16[2,704,2048]{2,1,0:T(8,128)(2,1)}), bf16[2,176,2048]{2,1,0:T(8,128)(2,1)}) %reduce-scatter.8.cloned.1.call-update) | async-done | bytes 1441808 | tf_op jit(solution)/shard_map/reduce_scatter | solution.py:250
  537.6 17.2 %collective-permute-done.62 = bf16[256,1408]{1,0:T(8,128)(2,1)} collective-permute-done((bf16[256,1408]{1,0:T(8,128)(2,1)}, bf16[256,1408]{1,0:T(8,128)(2,1)}, u32[]{:S(2)}, u32[]{:S(2)}) %collective-permute-start.62) | collective-permute-done | bytes 720928 | tf_op jit(solution)/shard_map/ppermute | solution.py:36
  577.8 9.4 %collective-permute-done.67 = bf16[64,1408]{1,0:T(8,128)(2,1)S(1)} collective-permute-done((bf16[64,1408]{1,0:T(8,128)(2,1)S(1)}, bf16[64,1408]{1,0:T(8,128)(2,1)S(1)}, u32[]{:S(2)}, u32[]{:S(2)}) %collective-permute-start.67) | collective-permute-done | bytes 180256 | tf_op jit(solution)/shard_map/ppermute | solution.py:40
  591.9 6.8 collective-permute-done.60
  620.1 32.8 %collective-permute-done.71 = bf16[64,2048]{1,0:T(8,128)(2,1)S(1)} collective-permute-done((bf16[64,2048]{1,0:T(8,128)(2,1)S(1)}, bf16[64,2048]{1,0:T(8,128)(2,1)S(1)}, u32[]{:S(2)}, u32[]{:S(2)}) %collective-permute-start.71) | collective-permute-done | bytes 262176 | tf_op jit(solution)/shard_map/ppermute | solution.py:36
  682.1 12.0 %collective-permute-done.83 = bf16[176,2048]{1,0:T(8,128)(2,1)S(1)} collective-permute-done((bf16[176,2048]{1,0:T(8,128)(2,1)S(1)}, bf16[176,2048]{1,0:T(8,128)(2,1)S(1)}, u32[]{:S(2)}, u32[]{:S(2)}) %collective-permute-start.83) | collective-permute-done | bytes 720928 | tf_op jit(solution)/shard_map/ppermute | solution.py:903
  (589 shorter events, 339.7 us)
Async XLA Ops:
  7.2 258.8 %all-gather.4.cloned.1.call-start = ((), (), s32[]{:S(2)}) async-start(), calls=%async_computation.3 | async-start | bytes 7208960 | tf_op jit(solution)/shard_map/all_gather | solution.py:239
  32.6 30.1 %collective-permute-start.5 = (bf16[256,1664]{1,0:T(8,128)(2,1)S(1)}, bf16[256,1664]{1,0:T(8,128)(2,1)S(1)}, u32[]{:S(2)}, u32[]{:S(2)}) collective-permute-start(bf16[256,1664]{1,0:T(8,128)(2,1)S(1)} %pad_maximum_fusion.1.refs_0_), channel_id=1, source_target_pairs={{0,8},{8,0},{1,9},{9,1},{2,10},{10,2},{3,11},{11,3},{4,12},{12,4},... | collective-permute-start | bytes 2555912 | tf_op jit(solution)/shard_map/ppermute | solution.py:36
  32.7 32.5 %collective-permute-start.4 = (bf16[256,1664]{1,0:T(8,128)(2,1)S(1)}, bf16[256,1664]{1,0:T(8,128)(2,1)S(1)}, u32[]{:S(2)}, u32[]{:S(2)}) collective-permute-start(bf16[256,1664]{1,0:T(8,128)(2,1)S(1)} %pad_maximum_fusion.1.refs_0_), channel_id=1, source_target_pairs={{0,16},{16,0},{1,17},{17,1},{2,18},{18,2},{3,19},{19,3},{4,20},{20... | collective-permute-start | bytes 2555912 | tf_op jit(solution)/shard_map/ppermute | solution.py:36
  33.2 39.3 %collective-permute-start.3 = (bf16[256,1664]{1,0:T(8,128)(2,1)S(1)}, bf16[256,1664]{1,0:T(8,128)(2,1)S(1)}, u32[]{:S(2)}, u32[]{:S(2)}) collective-permute-start(bf16[256,1664]{1,0:T(8,128)(2,1)S(1)} %pad_maximum_fusion.1.refs_0_), channel_id=1, source_target_pairs={{0,4},{4,0},{1,5},{5,1},{2,6},{6,2},{3,7},{7,3},{8,12},{12,8},{9,1... | collective-permute-start | bytes 2555912 | tf_op jit(solution)/shard_map/ppermute | solution.py:36
  35.8 26.8 %collective-permute-start.6 = (bf16[64,2048]{1,0:T(8,128)(2,1)S(1)}, bf16[64,2048]{1,0:T(8,128)(2,1)S(1)}, u32[]{:S(2)}, u32[]{:S(2)}) collective-permute-start(bf16[64,2048]{1,0:T(8,128)(2,1)S(1)} %copy-done.107), channel_id=1, source_target_pairs={{0,0},{1,8},{2,16},{3,24},{4,4},{5,12},{6,20},{7,28},{8,1},{9,9},{... | collective-permute-start | bytes 786440 | tf_op jit(solution)/shard_map/ppermute | solution.py:645
  41.4 32.7 %collective-permute-start.21 = (bf16[64,2816]{1,0:T(8,128)(2,1)}, bf16[64,2816]{1,0:T(8,128)(2,1)}, u32[]{:S(2)}, u32[]{:S(2)}) collective-permute-start(bf16[64,2816]{1,0:T(8,128)(2,1)} %select_select_fusion.5), channel_id=1, source_target_pairs={{0,2},{1,3},{2,0},{3,1},{4,6},{5,7},{6,4},{7,5},{8,10},{9,11},{10,... | collective-permute-start | bytes 1081352 | tf_op jit(solution)/shard_map/ppermute | solution.py:40
  88.2 23.3 %collective-permute-start.15 = (bf16[128,2048]{1,0:T(8,128)(2,1)S(1)}, bf16[128,2048]{1,0:T(8,128)(2,1)S(1)}, u32[]{:S(2)}, u32[]{:S(2)}) collective-permute-start(bf16[128,2048]{1,0:T(8,128)(2,1)S(1)} %bitcast.197), channel_id=1, source_target_pairs={{0,2},{1,3},{2,0},{3,1},{4,6},{5,7},{6,4},{7,5},{8,10},{9,11},{10,... | collective-permute-start | bytes 1572872 | tf_op jit(solution)/shard_map/ppermute | solution.py:40
  124.7 33.8 %collective-permute-start.33 = (bf16[256,1408]{1,0:T(8,128)(2,1)}, bf16[256,1408]{1,0:T(8,128)(2,1)S(1)}, u32[]{:S(2)}, u32[]{:S(2)}) collective-permute-start(bf16[256,1408]{1,0:T(8,128)(2,1)} %get-tuple-element.209), channel_id=1, source_target_pairs={{0,4},{4,0},{1,5},{5,1},{2,6},{6,2},{3,7},{7,3},{8,12},{12,8},{9,1... | collective-permute-start | bytes 2162696 | tf_op jit(solution)/shard_map/ppermute | solution.py:36
  126.7 24.0 %collective-permute-start.28 = (bf16[64,2048]{1,0:T(8,128)(2,1)}, bf16[64,2048]{1,0:T(8,128)(2,1)S(1)}, u32[]{:S(2)}, u32[]{:S(2)}) collective-permute-start(bf16[64,2048]{1,0:T(8,128)(2,1)} %collective-permute-done.25.refs_5_), channel_id=1, source_target_pairs={{0,8},{8,0},{1,9},{9,1},{2,10},{10,2},{3,11},{11,3},{4,12},{12,4},... | collective-permute-start | bytes 786440 | tf_op jit(solution)/shard_map/ppermute | solution.py:36
  171.8 103.1 %all-gather.6.cloned.1.call-start = ((), (), s32[]{:S(2)}) async-start(), calls=%async_computation.4 | async-start | bytes 7208960 | tf_op jit(solution)/shard_map/all_gather | solution.py:239
  174.0 32.0 %collective-permute-start.32 = (bf16[176,2048]{1,0:T(8,128)(2,1)}, bf16[176,2048]{1,0:T(8,128)(2,1)}, u32[]{:S(2)}, u32[]{:S(2)}) collective-permute-start(bf16[176,2048]{1,0:T(8,128)(2,1)} %param.21), channel_id=1, source_target_pairs={{0,0},{1,8},{2,16},{3,24},{4,4},{5,12},{6,20},{7,28},{8,1},{9,9},{... | collective-permute-start | bytes 2162696 | tf_op jit(solution)/shard_map/ppermute | solution.py:725
  176.4 40.7 %collective-permute-start.34 = (bf16[256,1408]{1,0:T(8,128)(2,1)}, bf16[256,1408]{1,0:T(8,128)(2,1)S(1)}, u32[]{:S(2)}, u32[]{:S(2)}) collective-permute-start(bf16[256,1408]{1,0:T(8,128)(2,1)} %get-tuple-element.211), channel_id=1, source_target_pairs={{0,4},{4,0},{1,5},{5,1},{2,6},{6,2},{3,7},{7,3},{8,12},{12,8},{9,1... | collective-permute-start | bytes 2162696 | tf_op jit(solution)/shard_map/ppermute | solution.py:36
  194.6 22.5 %collective-permute-start.31 = (bf16[128,2048]{1,0:T(8,128)(2,1)S(1)}, bf16[128,2048]{1,0:T(8,128)(2,1)}, u32[]{:S(2)}, u32[]{:S(2)}) collective-permute-start(bf16[128,2048]{1,0:T(8,128)(2,1)S(1)} %get-tuple-element.198), channel_id=1, source_target_pairs={{0,2},{1,3},{2,0},{3,1},{4,6},{5,7},{6,4},{7,5},{8,10},{9,11},{10,... | collective-permute-start | bytes 1572872 | tf_op jit(solution)/shard_map/ppermute | solution.py:40
  218.8 103.2 %all-gather.8.cloned.1.call-start = ((), (), s32[]{:S(2)}) async-start(), calls=%async_computation.5 | async-start | bytes 7208960 | tf_op jit(solution)/shard_map/all_gather | solution.py:241
  218.8 27.4 %collective-permute-start.35 = (bf16[128,2048]{1,0:T(8,128)(2,1)}, bf16[128,2048]{1,0:T(8,128)(2,1)}, u32[]{:S(2)}, u32[]{:S(2)}) collective-permute-start(bf16[128,2048]{1,0:T(8,128)(2,1)} %get-tuple-element.206), channel_id=1, source_target_pairs={{0,3},{1,2},{2,1},{3,0},{4,7},{5,6},{6,5},{7,4},{8,11},{9,10},{10,... | collective-permute-start | bytes 1572872 | tf_op jit(solution)/shard_map/ppermute | solution.py:40
  221.6 35.9 %collective-permute-start.38 = (bf16[176,2048]{1,0:T(8,128)(2,1)}, bf16[176,2048]{1,0:T(8,128)(2,1)S(1)}, u32[]{:S(2)}, u32[]{:S(2)}) collective-permute-start(bf16[176,2048]{1,0:T(8,128)(2,1)} %collective-permute-done.32), channel_id=1, source_target_pairs={{0,4},{4,0},{1,5},{5,1},{2,6},{6,2},{3,7},{7,3},{8,12},{12,8},{9,1... | collective-permute-start | bytes 2162696 | tf_op jit(solution)/shard_map/ppermute | solution.py:36
  278.4 164.8 %reduce-scatter.4.cloned.1.call-start = ((), (), s32[]{:S(2)}) async-start(), calls=%async_computation.6 | async-start | bytes 7208960 | tf_op jit(solution)/shard_map/reduce_scatter | solution.py:251
  295.2 24.2 %collective-permute-start.41 = (bf16[128,2048]{1,0:T(8,128)(2,1)}, bf16[128,2048]{1,0:T(8,128)(2,1)S(1)}, u32[]{:S(2)}, u32[]{:S(2)}) collective-permute-start(bf16[128,2048]{1,0:T(8,128)(2,1)} %bitcast.201), channel_id=1, source_target_pairs={{0,2},{1,3},{2,0},{3,1},{4,6},{5,7},{6,4},{7,5},{8,10},{9,11},{10,... | collective-permute-start | bytes 1572872 | tf_op jit(solution)/shard_map/ppermute | solution.py:40
  296.7 22.7 %collective-permute-start.40 = (bf16[128,2048]{1,0:T(8,128)(2,1)}, bf16[128,2048]{1,0:T(8,128)(2,1)S(1)}, u32[]{:S(2)}, u32[]{:S(2)}) collective-permute-start(bf16[128,2048]{1,0:T(8,128)(2,1)} %bitcast.202), channel_id=1, source_target_pairs={{0,1},{1,0},{2,3},{3,2},{4,5},{5,4},{6,7},{7,6},{8,9},{9,8},{10,11... | collective-permute-start | bytes 1572872 | tf_op jit(solution)/shard_map/ppermute | solution.py:40
  362.0 117.5 %reduce-scatter.6.cloned.1.call-start = ((), (), s32[]{:S(2)}) async-start(), calls=%async_computation.7 | async-start | bytes 7208960 | tf_op jit(solution)/shard_map/reduce_scatter | solution.py:251
  376.5 161.1 %reduce-scatter.8.cloned.1.call-start = ((), (), s32[]{:S(2)}) async-start(), calls=%async_computation.8 | async-start | bytes 7208960 | tf_op jit(solution)/shard_map/reduce_scatter | solution.py:250
  463.2 30.4 %collective-permute-start.53 = (bf16[256,1408]{1,0:T(8,128)(2,1)}, bf16[256,1408]{1,0:T(8,128)(2,1)S(1)}, u32[]{:S(2)}, u32[]{:S(2)}) collective-permute-start(bf16[256,1408]{1,0:T(8,128)(2,1)} %dynamic-slice_bitcast_fusion.2), channel_id=1, source_target_pairs={{0,4},{4,0},{1,5},{5,1},{2,6},{6,2},{3,7},{7,3},{8,12},{12,8},{9,1... | collective-permute-start | bytes 2162696 | tf_op jit(solution)/shard_map/ppermute | solution.py:36
  466.7 26.9 %collective-permute-start.52 = (bf16[512,2048]{1,0:T(8,128)(2,1)}, bf16[512,2048]{1,0:T(8,128)(2,1)}, u32[]{:S(2)}, u32[]{:S(2)}) collective-permute-start(bf16[512,2048]{1,0:T(8,128)(2,1)} %convolution_convert_fusion.3), channel_id=1, source_target_pairs={{0,8},{8,0},{1,9},{9,1},{2,10},{10,2},{3,11},{11,3},{4,12},{12,4},... | collective-permute-start | bytes 6291464 | tf_op jit(solution)/shard_map/ppermute | solution.py:36
  519.2 51.6 %collective-permute-start.59 = (bf16[2048,1664]{1,0:T(8,128)(2,1)}, bf16[2048,1664]{1,0:T(8,128)(2,1)}, u32[]{:S(2)}, u32[]{:S(2)}) collective-permute-start(bf16[2048,1664]{1,0:T(8,128)(2,1)} %add_convert_fusion), channel_id=1, source_target_pairs={{0,8},{8,0},{1,9},{9,1},{2,10},{10,2},{3,11},{11,3},{4,12},{12,4},... | collective-permute-start | bytes 20447240 | tf_op jit(solution)/shard_map/ppermute | solution.py:36
  520.2 34.7 %collective-permute-start.62 = (bf16[256,1408]{1,0:T(8,128)(2,1)}, bf16[256,1408]{1,0:T(8,128)(2,1)}, u32[]{:S(2)}, u32[]{:S(2)}) collective-permute-start(bf16[256,1408]{1,0:T(8,128)(2,1)} %dynamic-slice_bitcast_fusion.1), channel_id=1, source_target_pairs={{0,4},{4,0},{1,5},{5,1},{2,6},{6,2},{3,7},{7,3},{8,12},{12,8},{9,1... | collective-permute-start | bytes 2162696 | tf_op jit(solution)/shard_map/ppermute | solution.py:36
  523.4 31.4 %collective-permute-start.61 = (bf16[128,2048]{1,0:T(8,128)(2,1)}, bf16[128,2048]{1,0:T(8,128)(2,1)S(1)}, u32[]{:S(2)}, u32[]{:S(2)}) collective-permute-start(bf16[128,2048]{1,0:T(8,128)(2,1)} %get-tuple-element.278), channel_id=1, source_target_pairs={{0,3},{1,2},{2,1},{3,0},{4,7},{5,6},{6,5},{7,4},{8,11},{9,10},{10,... | collective-permute-start | bytes 1572872 | tf_op jit(solution)/shard_map/ppermute | solution.py:40
  560.2 92.7 %collective-permute-start.78 = (bf16[176,2048]{1,0:T(8,128)(2,1)S(1)}, bf16[176,2048]{1,0:T(8,128)(2,1)S(1)}, u32[]{:S(2)}, u32[]{:S(2)}) collective-permute-start(bf16[176,2048]{1,0:T(8,128)(2,1)S(1)} %dynamic-slice_bitcast_fusion), channel_id=1, source_target_pairs={{0,4},{4,0},{1,5},{5,1},{2,6},{6,2},{3,7},{7,3},{8,12},{12,8},{9,1... | collective-permute-start | bytes 2162696 | tf_op jit(solution)/shard_map/ppermute | solution.py:36
  590.7 62.2 %collective-permute-start.70 = (bf16[256,1664]{1,0:T(8,128)(2,1)S(1)}, bf16[256,1664]{1,0:T(8,128)(2,1)S(1)}, u32[]{:S(2)}, u32[]{:S(2)}) collective-permute-start(bf16[256,1664]{1,0:T(8,128)(2,1)S(1)} %get-tuple-element.340), channel_id=1, source_target_pairs={{0,16},{16,0},{1,17},{17,1},{2,18},{18,2},{3,19},{19,3},{4,20},{20... | collective-permute-start | bytes 2555912 | tf_op jit(solution)/shard_map/ppermute | solution.py:36
  611.0 41.9 %collective-permute-start.69 = (bf16[256,1664]{1,0:T(8,128)(2,1)S(1)}, bf16[256,1664]{1,0:T(8,128)(2,1)S(1)}, u32[]{:S(2)}, u32[]{:S(2)}) collective-permute-start(bf16[256,1664]{1,0:T(8,128)(2,1)S(1)} %add_convert_fusion.2), channel_id=1, source_target_pairs={{0,4},{4,0},{1,5},{5,1},{2,6},{6,2},{3,7},{7,3},{8,12},{12,8},{9,1... | collective-permute-start | bytes 2555912 | tf_op jit(solution)/shard_map/ppermute | solution.py:36
  616.0 36.8 %collective-permute-start.71 = (bf16[64,2048]{1,0:T(8,128)(2,1)S(1)}, bf16[64,2048]{1,0:T(8,128)(2,1)S(1)}, u32[]{:S(2)}, u32[]{:S(2)}) collective-permute-start(bf16[64,2048]{1,0:T(8,128)(2,1)S(1)} %add_convert_fusion.5), channel_id=1, source_target_pairs={{0,4},{4,0},{1,5},{5,1},{2,6},{6,2},{3,7},{7,3},{8,12},{12,8},{9,1... | collective-permute-start | bytes 786440 | tf_op jit(solution)/shard_map/ppermute | solution.py:36
  657.8 22.6 %collective-permute-start.82 = (bf16[64,2048]{1,0:T(8,128)(2,1)S(1)}, bf16[64,2048]{1,0:T(8,128)(2,1)}, u32[]{:S(2)}, u32[]{:S(2)}) collective-permute-start(bf16[64,2048]{1,0:T(8,128)(2,1)S(1)} %add_convert_fusion.4), channel_id=1, source_target_pairs={{0,0},{8,1},{16,2},{24,3},{4,4},{12,5},{20,6},{28,7},{1,8},{9,9},{... | collective-permute-start | bytes 786440 | tf_op jit(solution)/shard_map/ppermute | solution.py:904
  665.5 28.6 %collective-permute-start.83 = (bf16[176,2048]{1,0:T(8,128)(2,1)S(1)}, bf16[176,2048]{1,0:T(8,128)(2,1)S(1)}, u32[]{:S(2)}, u32[]{:S(2)}) collective-permute-start(bf16[176,2048]{1,0:T(8,128)(2,1)S(1)} %fusion.5), channel_id=1, source_target_pairs={{0,0},{8,1},{16,2},{24,3},{4,4},{12,5},{20,6},{28,7},{1,8},{9,9},{... | collective-permute-start | bytes 2162696 | tf_op jit(solution)/shard_map/ppermute | solution.py:903
  (174 other events, 1755.2 us)
Sparse Core Ops, SparseCore 0:
  171.9 56.8 all-gather.3
  230.9 43.9 all-gather.5
  278.6 43.3 all-gather.7
  362.1 53.9 reduce-scatter.3
  418.7 54.8 reduce-scatter.5
  476.0 61.5 reduce-scatter.7

commit v4 on v3

--- a/solution.py
+++ b/solution.py
@@ -846,7 +846,7 @@
     n1_grad_all = mm_nt(v[n.grad_proj], w_in)
     n1_grad_parts = n1_grad_all.reshape(4, tokens, width)
     v[n.n1_send] = shares(n1_grad_parts)
-    sync(n.n1_send, n.grad_proj, n.y1, n.y2, n.y_send, n.out_g, n.out_g__c, n.gate_other, n.up_part)
+    sync(n.n1_send, n.grad_proj, n.y1, n.y2, n.y_send, n.out_g, n.out_g__c, n.up_part)
     v[n.up_other] = other_half(v[n.up_part])
     v[n.t1], v[n.t2] = across(v[n.n1_send][1], 1), across(v[n.n1_send][2], 2)
     v[n.y3] = across(v[n.y_send][3], 3)
@@ -871,21 +871,21 @@
     first = RANKS + RANK
     extras = jnp.pad(extras, ((0, 0), (first, RANKS + LANES - first - extras.shape[1])))
     v[n.inp_g] = (mm_tn(n1, v[n.grad_proj]) + extras).astype(bf16)
-    sync(n.n1_send, n.t1, n.t2, n.inp_g, n.out_g__y0, n.out_g__y1, n.out_g, n.y3)
+    sync(n.n1_send, n.t1, n.t2, n.inp_g, n.out_g__y0, n.out_g__y1, n.out_g, n.y3, n.gate_other)
     v[n.t3] = across(v[n.n1_send][3], 3)
     add(n.inp_g__c)
     sync(n.inp_g, n.inp_g__c)
     add(n.inp_g__y0, n.inp_g__y1)
-    sync(n.t3, n.gate_other, n.gate_part, n.up_other, n.up_part, n.down_part, n.out_g, n.out_g__y0)
+    sync(n.t3, n.gate_other, n.gate_part, n.down_part, n.out_g, n.out_g__y0)
     v[n.gate_back] = return_columns(sum_halves(v[n.gate_part], v[n.gate_other]), place)
-    v[n.up_back] = return_columns(sum_halves(v[n.up_part], v[n.up_other]), place)
     v[n.down_other] = other_half(v[n.down_part])
     add(n.out_g__f)
     n1_grad = add_shares(n1_grad_parts[0], (v[n.t1], v[n.t2], v[n.t3]))
     input_part, _ = normed_grad(x_own.astype(f32), gain_one, n1_grad)
     input_grad = (h1_grad + input_part).reshape(1, tokens, width)
-    sync(n.inp_g, n.inp_g__y0, n.gate_back, n.up_back, n.y1, n.y2, n.y3)
+    sync(n.inp_g, n.inp_g__y0, n.gate_back, n.up_other, n.up_part, n.y1, n.y2, n.y3)
     add(n.inp_g__f)
+    v[n.up_back] = return_columns(sum_halves(v[n.up_part], v[n.up_other]), place)
     y = add_shares(y_parts[0], (v[n.y1], v[n.y2], v[n.y3]))
     result = h1 + y
     block_out = result.astype(bf16).reshape(1, tokens, width)

time: 714 us -> 708 us (level)
  waiting for transfers between devices: 310 us -> 295 us
    ppermute x34, waiting for transfers between devices: 102 us -> 75.1 us  [swap(): return lax.ppermute(value, axis, [(0, 1), (1, 0)])]
    ppermute x45, waiting for transfers between devices: 131 us -> 140 us  [across(): return lax.ppermute(value, group, [(i, i ^ mask) for i in range(4)])]
    unnamed x263 -> x254, local copies, waits for them, and re-layouts: 48.4 us -> 48.6 us
  transfers between devices with their start and end apart: 91 -> 91, of which waited for: 43 -> 39; matrix products, arithmetic and copies ran while one was open for 20% -> 20% of each run, Pallas kernels for 6% -> 6%
where the time goes in v4:
time: 708 us; the launch traced here: 696 us
  waiting for transfers between devices  295 us (42%)
  starting transfers between devices  122 us (17%)
  matrix products  89.3 us (13%)
  local copies, waits for them, and re-layouts  76.2 us (11%)
  other arithmetic  56.7 us (8%)
  Pallas kernels  40 us (6%)
  between operations  17 us (2%)
    ppermute x45, waiting for transfers between devices, across(): return lax.ppermute(value, group, [(i, i ^ mask) for i in range(4)])  140 us
    ppermute x34, waiting for transfers between devices, swap(): return lax.ppermute(value, axis, [(0, 1), (1, 0)])  75.1 us
    ppermute x45, starting transfers between devices, across(): return lax.ppermute(value, group, [(i, i ^ mask) for i in range(4)])  54.1 us
    ppermute x34, starting transfers between devices, swap(): return lax.ppermute(value, axis, [(0, 1), (1, 0)])  51.6 us
    unnamed x254, local copies, waits for them, and re-layouts  48.6 us
    dot_general x5, matrix products, mm(): return jnp.dot(left, right, preferred_element_type=f32).astype(out)  34.3 us
    pallas_call x4, Pallas kernels, call(): pl.pallas_call(kernel, grid_spec=pltpu.PrefetchScalarGridSpec(num_scalar_...  31.2 us
    dot_general x5, matrix products, dot_tn(): lax.dot_general(a, b, (((0,), (0,)), ((), ())), preferred_element_type=f32)  29.8 us
  transfers between devices with their start and end apart: 91, of which 39 were waited for; matrix products, arithmetic and copies ran while one was open for 20% of the time, Pallas kernels for 6%

profile of v4, /device:TPU:8, one launch (start us, length us, event | category | flops | bytes accessed | tf_op | source)
XLA Modules:
  0.0 696.4 jit_solution(13119788514760068758)
XLA Ops:
  22.1 7.3 %collective-permute-done.8 = bf16[2,8,128]{2,1,0:T(8,128)(2,1)S(1)} collective-permute-done((bf16[2,8,128]{2,1,0:T(8,128)(2,1)S(1)}, bf16[2,8,128]{2,1,0:T(8,128)(2,1)S(1)}, u32[]{:S(2)}, u32[]{:S(2)}) %collective-permute-start.8) | collective-permute-done | bytes 4128 | tf_op jit(solution)/shard_map/ppermute | solution.py:36
  41.4 21.2 %collective-permute-done.6.refs_0_ = bf16[64,2048]{1,0:T(8,128)(2,1)S(1)} collective-permute-done((bf16[64,2048]{1,0:T(8,128)(2,1)S(1)}, bf16[64,2048]{1,0:T(8,128)(2,1)S(1)}, u32[]{:S(2)}, u32[]{:S(2)}) %collective-permute-start.6) | collective-permute-done | bytes 262176 | tf_op jit(solution)/shard_map/ppermute | solution.py:645
  65.2 7.3 %collective-permute-done.3.refs_4_ = bf16[256,1664]{1,0:T(8,128)(2,1)S(1)} collective-permute-done((bf16[256,1664]{1,0:T(8,128)(2,1)S(1)}, bf16[256,1664]{1,0:T(8,128)(2,1)S(1)}, u32[]{:S(2)}, u32[]{:S(2)}) %collective-permute-start.3) | collective-permute-done | bytes 852000 | tf_op jit(solution)/shard_map/ppermute | solution.py:36
  93.9 6.7 collective-permute-done.16.refs_3_
  103.4 8.1 %collective-permute-done.15.refs_2_ = bf16[128,2048]{1,0:T(8,128)(2,1)S(1)} collective-permute-done((bf16[128,2048]{1,0:T(8,128)(2,1)S(1)}, bf16[128,2048]{1,0:T(8,128)(2,1)S(1)}, u32[]{:S(2)}, u32[]{:S(2)}) %collective-permute-start.15) | collective-permute-done | bytes 524320 | tf_op jit(solution)/shard_map/ppermute | solution.py:40
  144.5 7.5 %shard_map.222 = (f32[512,256]{1,0:T(8,128)S(1)}, f32[512,256]{1,0:T(8,128)S(1)}, bf16[8,512,256]{2,1,0:T(8,128)(2,1)S(1)}, f32[8,1,256]{2,1,0:T(1,128)S(1)}, bf...) custom-call(s32[1]{0:T(128)} %bitcast.1.place, f32[512,1664]{1,0:T(8,128)} %fusion.25.proj, bf16[128,256]{1,0:T(8,128)(2,1)S(1)} %pad.33.up, ...), custom_call_target="tpu_custom_call" | custom-call | flops 134217728 | bytes 7014400 | tf_op jit(solution)/shard_map/pallas_call | solution.py:503
  158.6 11.4 %collective-permute-done.29.entering = bf16[512,256]{1,0:T(8,128)(2,1)S(1)} collective-permute-done((bf16[512,256]{1,0:T(8,128)(2,1)S(1)}, bf16[512,256]{1,0:T(8,128)(2,1)S(1)}, u32[]{:S(2)}, u32[]{:S(2)}) %collective-permute-start.29) | collective-permute-done | bytes 262176 | tf_op jit(solution)/shard_map/ppermute | solution.py:555
  181.7 6.8 shard_map.224
  194.4 12.5 %collective-permute-done.32 = bf16[176,2048]{1,0:T(8,128)(2,1)} collective-permute-done((bf16[176,2048]{1,0:T(8,128)(2,1)}, bf16[176,2048]{1,0:T(8,128)(2,1)}, u32[]{:S(2)}, u32[]{:S(2)}) %collective-permute-start.32) | collective-permute-done | bytes 720928 | tf_op jit(solution)/shard_map/ppermute | solution.py:725
  206.9 10.2 %collective-permute-done.31 = bf16[128,2048]{1,0:T(8,128)(2,1)} collective-permute-done((bf16[128,2048]{1,0:T(8,128)(2,1)S(1)}, bf16[128,2048]{1,0:T(8,128)(2,1)}, u32[]{:S(2)}, u32[]{:S(2)}) %collective-permute-start.31) | collective-permute-done | bytes 524320 | tf_op jit(solution)/shard_map/ppermute | solution.py:40
  227.4 18.0 %collective-permute-done.35 = bf16[128,2048]{1,0:T(8,128)(2,1)} collective-permute-done((bf16[128,2048]{1,0:T(8,128)(2,1)}, bf16[128,2048]{1,0:T(8,128)(2,1)}, u32[]{:S(2)}, u32[]{:S(2)}) %collective-permute-start.35) | collective-permute-done | bytes 524320 | tf_op jit(solution)/shard_map/ppermute | solution.py:40
  264.2 11.8 %all-gather.6.cloned.1.call-done = bf16[2048,1408]{1,0:T(8,128)(2,1)} async-done(((bf16[512,1408]{1,0:T(8,128)(2,1)}), bf16[2048,1408]{1,0:T(8,128)(2,1)}) %all-gather.6.cloned.1.call-update) | async-done | bytes 5767184 | tf_op jit(solution)/shard_map/all_gather | solution.py:239
  281.1 13.7 %collective-permute-done.39.refs_3_ = bf16[128,2048]{1,0:T(8,128)(2,1)S(1)} collective-permute-done((bf16[128,2048]{1,0:T(8,128)(2,1)}, bf16[128,2048]{1,0:T(8,128)(2,1)S(1)}, u32[]{:S(2)}, u32[]{:S(2)}) %collective-permute-start.39) | collective-permute-done | bytes 524320 | tf_op jit(solution)/shard_map/ppermute | solution.py:40
  302.3 8.4 %fusion.76 = f32[512,1408]{1,0:T(8,128)} fusion(bf16[512,2048]{1,0:T(8,128)(2,1)S(1)} %shard_map.226, bf16[2048,1408]{1,0:T(8,128)(2,1)} %all-gather.4.cloned.1.call-done), kind=kOutput, calls=%fused_computation.274 | convolution fusion | flops 2952790016 | bytes 10747904 | tf_op jit(solution)/shard_map/dot_general | solution.py:537
  310.9 9.6 %collective-permute-done.41.refs_2_ = bf16[128,2048]{1,0:T(8,128)(2,1)S(1)} collective-permute-done((bf16[128,2048]{1,0:T(8,128)(2,1)}, bf16[128,2048]{1,0:T(8,128)(2,1)S(1)}, u32[]{:S(2)}, u32[]{:S(2)}) %collective-permute-start.41) | collective-permute-done | bytes 524320 | tf_op jit(solution)/shard_map/ppermute | solution.py:40
  329.8 8.0 %multiply_convert_fusion = (bf16[512,1408]{1,0:T(8,128)(2,1)}, bf16[512,1408]{1,0:T(8,128)(2,1)S(1)}, bf16[512,1408]{1,0:T(8,128)(2,1)S(1)}) fusion(f32[512,1408]{1,0:T(8,128)S(1)} %copy-done.107, f32[512,1408]{1,0:T(8,128)S(1)} %fusion.75, bf16[512,2048]{1,0:T(8,128)(2,1)S(1)} %copy-done.18, bf16[2048,1408]{1,0:T(8,128)(2,1)} %all-gather.6.cloned.1.call-done), kind=kOutput, calls=%fused_computation.13 | convolution fusion | flops 2964324352 | bytes 17956864 | tf_op jit(solution)/shard_map/dot_general | solution.py:537
  354.8 7.1 %collective-permute-done.43 = bf16[128,2048]{1,0:T(8,128)(2,1)} collective-permute-done((bf16[128,2048]{1,0:T(8,128)(2,1)}, bf16[128,2048]{1,0:T(8,128)(2,1)}, u32[]{:S(2)}, u32[]{:S(2)}) %collective-permute-start.43) | collective-permute-done | bytes 524320 | tf_op jit(solution)/shard_map/ppermute | solution.py:40
  363.9 8.9 %convolution_convert_fusion.1 = bf16[2048,1408]{1,0:T(8,128)(2,1)} fusion(bf16[512,2048]{1,0:T(8,128)(2,1)} %copy-done.17, bf16[512,1408]{1,0:T(8,128)(2,1)} %copy-done.106), kind=kOutput, calls=%fused_computation.2 | convolution fusion | flops 2955673600 | bytes 9306112 | tf_op jit(solution)/shard_map/dot_general | solution.py:290
  396.7 11.2 %collective-permute-done.48.refs_3_ = bf16[128,2048]{1,0:T(8,128)(2,1)} collective-permute-done((bf16[128,2048]{1,0:T(8,128)(2,1)}, bf16[128,2048]{1,0:T(8,128)(2,1)}, u32[]{:S(2)}, u32[]{:S(2)}) %collective-permute-start.48) | collective-permute-done | bytes 524320 | tf_op jit(solution)/shard_map/ppermute | solution.py:40
  414.8 7.5 %shard_map.228 = (bf16[512,512]{1,0:T(8,128)(2,1)S(1)}, bf16[512,512]{1,0:T(8,128)(2,1)S(1)}, bf16[8,512,256]{2,1,0:T(8,128)(2,1)}, f32[8,1,256]{2,1,0:T(1,128)S...) custom-call(s32[1]{0:T(128)} %bitcast.1.place, f32[512,512]{1,0:T(8,128)S(1)} %fusion.78.grad_gated, ...), custom_call_target="tpu_custom_call" | custom-call | flops 134217728 | bytes 12128256 | tf_op jit(solution)/shard_map/pallas_call | solution.py:503
  430.7 8.9 %fusion.74 = (bf16[512,2048]{1,0:T(8,128)(2,1)S(1)}, f32[512,2048]{1,0:T(8,128)}) fusion(bf16[512,1408]{1,0:T(8,128)(2,1)} %get-tuple-element.245, bf16[1408,2048]{1,0:T(8,128)(2,1)} %bitcast.243), kind=kOutput, calls=%fused_computation.272 | convolution fusion | flops 2953838592 | bytes 13500416 | tf_op jit(solution)/shard_map/dot_general | solution.py:537
  450.6 9.3 %shard_map.229 = (bf16[512,1664]{1,0:T(8,128)(2,1)S(1)}, f32[128,256]{1,0:T(8,128)S(1)}, f32[1,256]{1,0:T(1,128)S(1)}) custom-call(s32[1]{0:T(128)} %bitcast.1.place, f32[512,1664]{1,0:T(8,128)} %fusion.25.proj, f32[512,256]{1,0:T(8,128)S(1)} %get-tuple-element.181.sums, f32[512,256]{1,0:T(8,128)S(1)} %copy-done.53, bf16[512,512]{1,0:T(8,128)(2,1)S(1)} %copy-done.55, ...), custom_call_target="tpu_custom_call" | custom-call | flops 520093696 | bytes 20676608 | tf_op jit(solution)/shard_map/pallas_call | solution.py:503
  468.8 8.9 %fusion.3 = (f32[2048]{0:T(1024)S(1)}, bf16[512,2048]{1,0:T(8,128)(2,1)}, f32[512,2048]{1,0:T(8,128)}) fusion(bf16[512,2048]{1,0:T(8,128)(2,1)S(1)} %shard_map.220, f32[512]{0:T(512)S(1)} %copy-done.102, bf16[512,1664]{1,0:T(8,128)(2,1)S(1)} %copy-done.69, bf16[2048,1664]{1,0:T(8,128)(2,1)} %copy-done.6), kind=kOutput, calls=%fused_computation.9 | convolution fusion | flops 3494901760 | bytes 16918528 | tf_op jit(solution)/shard_map/dot_general | solution.py:286
  488.4 8.2 %collective-permute-done.58 = bf16[256,1408]{1,0:T(8,128)(2,1)} collective-permute-done((bf16[256,1408]{1,0:T(8,128)(2,1)}, bf16[256,1408]{1,0:T(8,128)(2,1)}, u32[]{:S(2)}, u32[]{:S(2)}) %collective-permute-start.58) | collective-permute-done | bytes 720928 | tf_op jit(solution)/shard_map/ppermute | solution.py:36
  499.0 8.0 %add_convert_fusion = bf16[2048,1664]{1,0:T(8,128)(2,1)} fusion(f32[2048,12]{1,0:T(8,128)} %copy.49, bf16[512,1664]{1,0:T(8,128)(2,1)} %copy-done.68, bf16[512,2048]{1,0:T(8,128)(2,1)S(1)} %shard_map.220, f32[2048]{0:T(1024)S(1)} %reshape.628, f32[512]{0:T(512)S(1)} %copy-done.103), kind=kOutput, calls=%fused_computation | convolution fusion | flops 3500670976 | bytes 10725376 | tf_op jit(solution)/shard_map/dot_general | solution.py:290
  522.7 9.3 %reduce-scatter.8.cloned.1.call-done = bf16[2,176,2048]{2,1,0:T(8,128)(2,1)} async-done(((bf16[2,704,2048]{2,1,0:T(8,128)(2,1)}), bf16[2,176,2048]{2,1,0:T(8,128)(2,1)}) %reduce-scatter.8.cloned.1.call-update) | async-done | bytes 1441808 | tf_op jit(solution)/shard_map/reduce_scatter | solution.py:250
  532.0 6.8 collective-permute-done.61
  563.7 8.0 %collective-permute-done.60 = bf16[256,1664]{1,0:T(8,128)(2,1)S(1)} collective-permute-done((bf16[256,1664]{1,0:T(8,128)(2,1)S(1)}, bf16[256,1664]{1,0:T(8,128)(2,1)S(1)}, u32[]{:S(2)}, u32[]{:S(2)}) %collective-permute-start.60) | collective-permute-done | bytes 852000 | tf_op jit(solution)/shard_map/ppermute | solution.py:36
  592.9 9.1 %collective-permute-done.81 = bf16[64,1408]{1,0:T(8,128)(2,1)S(1)} collective-permute-done((bf16[64,1408]{1,0:T(8,128)(2,1)S(1)}, bf16[64,1408]{1,0:T(8,128)(2,1)S(1)}, u32[]{:S(2)}, u32[]{:S(2)}) %collective-permute-start.81) | collective-permute-done | bytes 180256 | tf_op jit(solution)/shard_map/ppermute | solution.py:40
  609.3 13.6 %collective-permute-done.67 = bf16[256,1664]{1,0:T(8,128)(2,1)S(1)} collective-permute-done((bf16[256,1664]{1,0:T(8,128)(2,1)S(1)}, bf16[256,1664]{1,0:T(8,128)(2,1)S(1)}, u32[]{:S(2)}, u32[]{:S(2)}) %collective-permute-start.67) | collective-permute-done | bytes 852000 | tf_op jit(solution)/shard_map/ppermute | solution.py:36
  622.8 22.7 %collective-permute-done.66 = bf16[256,1664]{1,0:T(8,128)(2,1)S(1)} collective-permute-done((bf16[256,1664]{1,0:T(8,128)(2,1)S(1)}, bf16[256,1664]{1,0:T(8,128)(2,1)S(1)}, u32[]{:S(2)}, u32[]{:S(2)}) %collective-permute-start.66) | collective-permute-done | bytes 852000 | tf_op jit(solution)/shard_map/ppermute | solution.py:36
  674.3 13.5 %collective-permute-done.83 = bf16[176,2048]{1,0:T(8,128)(2,1)S(1)} collective-permute-done((bf16[176,2048]{1,0:T(8,128)(2,1)S(1)}, bf16[176,2048]{1,0:T(8,128)(2,1)S(1)}, u32[]{:S(2)}, u32[]{:S(2)}) %collective-permute-start.83) | collective-permute-done | bytes 720928 | tf_op jit(solution)/shard_map/ppermute | solution.py:903
  (582 shorter events, 349.7 us)
Async XLA Ops:
  7.2 257.0 %all-gather.4.cloned.1.call-start = ((), (), s32[]{:S(2)}) async-start(), calls=%async_computation.3 | async-start | bytes 7208960 | tf_op jit(solution)/shard_map/all_gather | solution.py:239
  32.5 30.1 %collective-permute-start.5 = (bf16[256,1664]{1,0:T(8,128)(2,1)S(1)}, bf16[256,1664]{1,0:T(8,128)(2,1)S(1)}, u32[]{:S(2)}, u32[]{:S(2)}) collective-permute-start(bf16[256,1664]{1,0:T(8,128)(2,1)S(1)} %pad_maximum_fusion.1.refs_0_), channel_id=1, source_target_pairs={{0,8},{8,0},{1,9},{9,1},{2,10},{10,2},{3,11},{11,3},{4,12},{12,4},... | collective-permute-start | bytes 2555912 | tf_op jit(solution)/shard_map/ppermute | solution.py:36
  32.6 32.5 %collective-permute-start.4 = (bf16[256,1664]{1,0:T(8,128)(2,1)S(1)}, bf16[256,1664]{1,0:T(8,128)(2,1)S(1)}, u32[]{:S(2)}, u32[]{:S(2)}) collective-permute-start(bf16[256,1664]{1,0:T(8,128)(2,1)S(1)} %pad_maximum_fusion.1.refs_0_), channel_id=1, source_target_pairs={{0,16},{16,0},{1,17},{17,1},{2,18},{18,2},{3,19},{19,3},{4,20},{20... | collective-permute-start | bytes 2555912 | tf_op jit(solution)/shard_map/ppermute | solution.py:36
  33.2 39.3 %collective-permute-start.3 = (bf16[256,1664]{1,0:T(8,128)(2,1)S(1)}, bf16[256,1664]{1,0:T(8,128)(2,1)S(1)}, u32[]{:S(2)}, u32[]{:S(2)}) collective-permute-start(bf16[256,1664]{1,0:T(8,128)(2,1)S(1)} %pad_maximum_fusion.1.refs_0_), channel_id=1, source_target_pairs={{0,4},{4,0},{1,5},{5,1},{2,6},{6,2},{3,7},{7,3},{8,12},{12,8},{9,1... | collective-permute-start | bytes 2555912 | tf_op jit(solution)/shard_map/ppermute | solution.py:36
  35.8 26.8 %collective-permute-start.6 = (bf16[64,2048]{1,0:T(8,128)(2,1)S(1)}, bf16[64,2048]{1,0:T(8,128)(2,1)S(1)}, u32[]{:S(2)}, u32[]{:S(2)}) collective-permute-start(bf16[64,2048]{1,0:T(8,128)(2,1)S(1)} %copy-done.104), channel_id=1, source_target_pairs={{0,0},{1,8},{2,16},{3,24},{4,4},{5,12},{6,20},{7,28},{8,1},{9,9},{... | collective-permute-start | bytes 786440 | tf_op jit(solution)/shard_map/ppermute | solution.py:645
  41.4 32.7 %collective-permute-start.21 = (bf16[64,2816]{1,0:T(8,128)(2,1)}, bf16[64,2816]{1,0:T(8,128)(2,1)}, u32[]{:S(2)}, u32[]{:S(2)}) collective-permute-start(bf16[64,2816]{1,0:T(8,128)(2,1)} %select_select_fusion.5), channel_id=1, source_target_pairs={{0,2},{1,3},{2,0},{3,1},{4,6},{5,7},{6,4},{7,5},{8,10},{9,11},{10,... | collective-permute-start | bytes 1081352 | tf_op jit(solution)/shard_map/ppermute | solution.py:40
  88.2 23.3 %collective-permute-start.15 = (bf16[128,2048]{1,0:T(8,128)(2,1)S(1)}, bf16[128,2048]{1,0:T(8,128)(2,1)S(1)}, u32[]{:S(2)}, u32[]{:S(2)}) collective-permute-start(bf16[128,2048]{1,0:T(8,128)(2,1)S(1)} %bitcast.197), channel_id=1, source_target_pairs={{0,2},{1,3},{2,0},{3,1},{4,6},{5,7},{6,4},{7,5},{8,10},{9,11},{10,... | collective-permute-start | bytes 1572872 | tf_op jit(solution)/shard_map/ppermute | solution.py:40
  124.5 34.1 %collective-permute-start.33 = (bf16[256,1408]{1,0:T(8,128)(2,1)}, bf16[256,1408]{1,0:T(8,128)(2,1)S(1)}, u32[]{:S(2)}, u32[]{:S(2)}) collective-permute-start(bf16[256,1408]{1,0:T(8,128)(2,1)} %get-tuple-element.205), channel_id=1, source_target_pairs={{0,4},{4,0},{1,5},{5,1},{2,6},{6,2},{3,7},{7,3},{8,12},{12,8},{9,1... | collective-permute-start | bytes 2162696 | tf_op jit(solution)/shard_map/ppermute | solution.py:36
  128.8 24.0 %collective-permute-start.28 = (bf16[64,2048]{1,0:T(8,128)(2,1)}, bf16[64,2048]{1,0:T(8,128)(2,1)S(1)}, u32[]{:S(2)}, u32[]{:S(2)}) collective-permute-start(bf16[64,2048]{1,0:T(8,128)(2,1)} %collective-permute-done.25.refs_5_), channel_id=1, source_target_pairs={{0,8},{8,0},{1,9},{9,1},{2,10},{10,2},{3,11},{11,3},{4,12},{12,4},... | collective-permute-start | bytes 786440 | tf_op jit(solution)/shard_map/ppermute | solution.py:36
  172.3 103.7 %all-gather.6.cloned.1.call-start = ((), (), s32[]{:S(2)}) async-start(), calls=%async_computation.4 | async-start | bytes 7208960 | tf_op jit(solution)/shard_map/all_gather | solution.py:239
  173.2 33.6 %collective-permute-start.32 = (bf16[176,2048]{1,0:T(8,128)(2,1)}, bf16[176,2048]{1,0:T(8,128)(2,1)}, u32[]{:S(2)}, u32[]{:S(2)}) collective-permute-start(bf16[176,2048]{1,0:T(8,128)(2,1)} %param.21), channel_id=1, source_target_pairs={{0,0},{1,8},{2,16},{3,24},{4,4},{5,12},{6,20},{7,28},{8,1},{9,9},{... | collective-permute-start | bytes 2162696 | tf_op jit(solution)/shard_map/ppermute | solution.py:725
  175.6 41.5 %collective-permute-start.34 = (bf16[256,1408]{1,0:T(8,128)(2,1)}, bf16[256,1408]{1,0:T(8,128)(2,1)S(1)}, u32[]{:S(2)}, u32[]{:S(2)}) collective-permute-start(bf16[256,1408]{1,0:T(8,128)(2,1)} %get-tuple-element.207), channel_id=1, source_target_pairs={{0,4},{4,0},{1,5},{5,1},{2,6},{6,2},{3,7},{7,3},{8,12},{12,8},{9,1... | collective-permute-start | bytes 2162696 | tf_op jit(solution)/shard_map/ppermute | solution.py:36
  194.3 22.8 %collective-permute-start.31 = (bf16[128,2048]{1,0:T(8,128)(2,1)S(1)}, bf16[128,2048]{1,0:T(8,128)(2,1)}, u32[]{:S(2)}, u32[]{:S(2)}) collective-permute-start(bf16[128,2048]{1,0:T(8,128)(2,1)S(1)} %get-tuple-element.194), channel_id=1, source_target_pairs={{0,2},{1,3},{2,0},{3,1},{4,6},{5,7},{6,4},{7,5},{8,10},{9,11},{10,... | collective-permute-start | bytes 1572872 | tf_op jit(solution)/shard_map/ppermute | solution.py:40
  218.8 104.4 %all-gather.8.cloned.1.call-start = ((), (), s32[]{:S(2)}) async-start(), calls=%async_computation.5 | async-start | bytes 7208960 | tf_op jit(solution)/shard_map/all_gather | solution.py:241
  218.8 26.5 %collective-permute-start.35 = (bf16[128,2048]{1,0:T(8,128)(2,1)}, bf16[128,2048]{1,0:T(8,128)(2,1)}, u32[]{:S(2)}, u32[]{:S(2)}) collective-permute-start(bf16[128,2048]{1,0:T(8,128)(2,1)} %get-tuple-element.202), channel_id=1, source_target_pairs={{0,3},{1,2},{2,1},{3,0},{4,7},{5,6},{6,5},{7,4},{8,11},{9,10},{10,... | collective-permute-start | bytes 1572872 | tf_op jit(solution)/shard_map/ppermute | solution.py:40
  223.0 34.4 %collective-permute-start.38 = (bf16[176,2048]{1,0:T(8,128)(2,1)}, bf16[176,2048]{1,0:T(8,128)(2,1)S(1)}, u32[]{:S(2)}, u32[]{:S(2)}) collective-permute-start(bf16[176,2048]{1,0:T(8,128)(2,1)} %collective-permute-done.32), channel_id=1, source_target_pairs={{0,4},{4,0},{1,5},{5,1},{2,6},{6,2},{3,7},{7,3},{8,12},{12,8},{9,1... | collective-permute-start | bytes 2162696 | tf_op jit(solution)/shard_map/ppermute | solution.py:36
  279.6 166.0 %reduce-scatter.4.cloned.1.call-start = ((), (), s32[]{:S(2)}) async-start(), calls=%async_computation.6 | async-start | bytes 7208960 | tf_op jit(solution)/shard_map/reduce_scatter | solution.py:251
  296.3 24.2 %collective-permute-start.41 = (bf16[128,2048]{1,0:T(8,128)(2,1)}, bf16[128,2048]{1,0:T(8,128)(2,1)S(1)}, u32[]{:S(2)}, u32[]{:S(2)}) collective-permute-start(bf16[128,2048]{1,0:T(8,128)(2,1)} %bitcast.201), channel_id=1, source_target_pairs={{0,2},{1,3},{2,0},{3,1},{4,6},{5,7},{6,4},{7,5},{8,10},{9,11},{10,... | collective-permute-start | bytes 1572872 | tf_op jit(solution)/shard_map/ppermute | solution.py:40
  297.8 22.7 %collective-permute-start.40 = (bf16[128,2048]{1,0:T(8,128)(2,1)}, bf16[128,2048]{1,0:T(8,128)(2,1)S(1)}, u32[]{:S(2)}, u32[]{:S(2)}) collective-permute-start(bf16[128,2048]{1,0:T(8,128)(2,1)} %bitcast.202), channel_id=1, source_target_pairs={{0,1},{1,0},{2,3},{3,2},{4,5},{5,4},{6,7},{7,6},{8,9},{9,8},{10,11... | collective-permute-start | bytes 1572872 | tf_op jit(solution)/shard_map/ppermute | solution.py:40
  363.1 118.5 %reduce-scatter.6.cloned.1.call-start = ((), (), s32[]{:S(2)}) async-start(), calls=%async_computation.7 | async-start | bytes 7208960 | tf_op jit(solution)/shard_map/reduce_scatter | solution.py:251
  377.6 154.4 %reduce-scatter.8.cloned.1.call-start = ((), (), s32[]{:S(2)}) async-start(), calls=%async_computation.8 | async-start | bytes 7208960 | tf_op jit(solution)/shard_map/reduce_scatter | solution.py:250
  465.5 31.1 %collective-permute-start.58 = (bf16[256,1408]{1,0:T(8,128)(2,1)}, bf16[256,1408]{1,0:T(8,128)(2,1)}, u32[]{:S(2)}, u32[]{:S(2)}) collective-permute-start(bf16[256,1408]{1,0:T(8,128)(2,1)} %dynamic-slice_bitcast_fusion.2), channel_id=1, source_target_pairs={{0,4},{4,0},{1,5},{5,1},{2,6},{6,2},{3,7},{7,3},{8,12},{12,8},{9,1... | collective-permute-start | bytes 2162696 | tf_op jit(solution)/shard_map/ppermute | solution.py:36
  483.4 23.7 %collective-permute-start.56 = (bf16[64,2048]{1,0:T(8,128)(2,1)S(1)}, bf16[64,2048]{1,0:T(8,128)(2,1)S(1)}, u32[]{:S(2)}, u32[]{:S(2)}) collective-permute-start(bf16[64,2048]{1,0:T(8,128)(2,1)S(1)} %get-tuple-element.337), channel_id=1, source_target_pairs={{0,16},{16,0},{1,17},{17,1},{2,18},{18,2},{3,19},{19,3},{4,20},{20... | collective-permute-start | bytes 786440 | tf_op jit(solution)/shard_map/ppermute | solution.py:36
  484.5 22.5 %collective-permute-start.55 = (bf16[64,2048]{1,0:T(8,128)(2,1)S(1)}, bf16[64,2048]{1,0:T(8,128)(2,1)S(1)}, u32[]{:S(2)}, u32[]{:S(2)}) collective-permute-start(bf16[64,2048]{1,0:T(8,128)(2,1)S(1)} %get-tuple-element.338), channel_id=1, source_target_pairs={{0,16},{16,0},{1,17},{17,1},{2,18},{18,2},{3,19},{19,3},{4,20},{20... | collective-permute-start | bytes 786440 | tf_op jit(solution)/shard_map/ppermute | solution.py:36
  487.6 24.3 %collective-permute-start.53 = (bf16[128,2048]{1,0:T(8,128)(2,1)}, bf16[128,2048]{1,0:T(8,128)(2,1)S(1)}, u32[]{:S(2)}, u32[]{:S(2)}) collective-permute-start(bf16[128,2048]{1,0:T(8,128)(2,1)} %get-tuple-element.260), channel_id=1, source_target_pairs={{0,1},{1,0},{2,3},{3,2},{4,5},{5,4},{6,7},{7,6},{8,9},{9,8},{10,11... | collective-permute-start | bytes 1572872 | tf_op jit(solution)/shard_map/ppermute | solution.py:40
  516.1 33.2 %collective-permute-start.59 = (bf16[2048,1664]{1,0:T(8,128)(2,1)}, bf16[2048,1664]{1,0:T(8,128)(2,1)}, u32[]{:S(2)}, u32[]{:S(2)}) collective-permute-start(bf16[2048,1664]{1,0:T(8,128)(2,1)} %add_convert_fusion), channel_id=1, source_target_pairs={{0,8},{8,0},{1,9},{9,1},{2,10},{10,2},{3,11},{11,3},{4,12},{12,4},... | collective-permute-start | bytes 20447240 | tf_op jit(solution)/shard_map/ppermute | solution.py:36
  516.1 22.7 %collective-permute-start.61 = (bf16[128,2048]{1,0:T(8,128)(2,1)}, bf16[128,2048]{1,0:T(8,128)(2,1)S(1)}, u32[]{:S(2)}, u32[]{:S(2)}) collective-permute-start(bf16[128,2048]{1,0:T(8,128)(2,1)} %get-tuple-element.274), channel_id=1, source_target_pairs={{0,3},{1,2},{2,1},{3,0},{4,7},{5,6},{6,5},{7,4},{8,11},{9,10},{10,... | collective-permute-start | bytes 1572872 | tf_op jit(solution)/shard_map/ppermute | solution.py:40
  522.3 41.4 %collective-permute-start.65 = (bf16[256,1408]{1,0:T(8,128)(2,1)S(1)}, bf16[256,1408]{1,0:T(8,128)(2,1)S(1)}, u32[]{:S(2)}, u32[]{:S(2)}) collective-permute-start(bf16[256,1408]{1,0:T(8,128)(2,1)S(1)} %dynamic-slice_bitcast_fusion.1), channel_id=1, source_target_pairs={{0,4},{4,0},{1,5},{5,1},{2,6},{6,2},{3,7},{7,3},{8,12},{12,8},{9,1... | collective-permute-start | bytes 2162696 | tf_op jit(solution)/shard_map/ppermute | solution.py:36
  555.8 53.5 %collective-permute-start.68 = (bf16[64,2048]{1,0:T(8,128)(2,1)S(1)}, bf16[64,2048]{1,0:T(8,128)(2,1)S(1)}, u32[]{:S(2)}, u32[]{:S(2)}) collective-permute-start(bf16[64,2048]{1,0:T(8,128)(2,1)S(1)} %add_convert_fusion.5), channel_id=1, source_target_pairs={{0,4},{4,0},{1,5},{5,1},{2,6},{6,2},{3,7},{7,3},{8,12},{12,8},{9,1... | collective-permute-start | bytes 786440 | tf_op jit(solution)/shard_map/ppermute | solution.py:36
  559.5 49.8 %collective-permute-start.75 = (bf16[176,2048]{1,0:T(8,128)(2,1)S(1)}, bf16[176,2048]{1,0:T(8,128)(2,1)S(1)}, u32[]{:S(2)}, u32[]{:S(2)}) collective-permute-start(bf16[176,2048]{1,0:T(8,128)(2,1)S(1)} %dynamic-slice_bitcast_fusion), channel_id=1, source_target_pairs={{0,4},{4,0},{1,5},{5,1},{2,6},{6,2},{3,7},{7,3},{8,12},{12,8},{9,1... | collective-permute-start | bytes 2162696 | tf_op jit(solution)/shard_map/ppermute | solution.py:36
  605.8 39.7 %collective-permute-start.66 = (bf16[256,1664]{1,0:T(8,128)(2,1)S(1)}, bf16[256,1664]{1,0:T(8,128)(2,1)S(1)}, u32[]{:S(2)}, u32[]{:S(2)}) collective-permute-start(bf16[256,1664]{1,0:T(8,128)(2,1)S(1)} %add_convert_fusion.2), channel_id=1, source_target_pairs={{0,4},{4,0},{1,5},{5,1},{2,6},{6,2},{3,7},{7,3},{8,12},{12,8},{9,1... | collective-permute-start | bytes 2555912 | tf_op jit(solution)/shard_map/ppermute | solution.py:36
  658.4 29.4 %collective-permute-start.83 = (bf16[176,2048]{1,0:T(8,128)(2,1)S(1)}, bf16[176,2048]{1,0:T(8,128)(2,1)S(1)}, u32[]{:S(2)}, u32[]{:S(2)}) collective-permute-start(bf16[176,2048]{1,0:T(8,128)(2,1)S(1)} %fusion.5), channel_id=1, source_target_pairs={{0,0},{8,1},{16,2},{24,3},{4,4},{12,5},{20,6},{28,7},{1,8},{9,9},{... | collective-permute-start | bytes 2162696 | tf_op jit(solution)/shard_map/ppermute | solution.py:903
  (171 other events, 1702.2 us)
Sparse Core Ops, SparseCore 0:
  172.4 55.1 all-gather.3
  229.8 46.2 all-gather.5
  279.7 43.3 all-gather.7
  363.2 53.9 reduce-scatter.3
  419.8 54.8 reduce-scatter.5
  477.1 54.8 reduce-scatter.7

commit v5 on v4

--- a/solution.py
+++ b/solution.py
@@ -749,11 +749,11 @@
     h1 = x_own.astype(f32) + mix
     v[n.n2] = normed(h1, gain_two).astype(bf16)
     v[n.n21], v[n.n22] = two_of(v[n.n2])
-    sync(n.n21, n.n22, n.n2, n.dy, n.down, n.down__f, n.w_gate, n.w_up)
-    w_gate, w_up = v[n.w_gate], v[n.w_up]
+    sync(n.n21, n.n22, n.n2, n.dy, n.down, n.down__f)
     w_down = gather_halves(v[n.down], v[n.down__f], True)
     v[n.n23] = last_of(v[n.n2])
-    sync(n.n21, n.n22, n.n23, n.n2, n.dy)
+    sync(n.n21, n.n22, n.n23, n.n2, n.dy, n.w_gate, n.w_up)
+    w_gate, w_up = v[n.w_gate], v[n.w_up]
     v[n.dy1], v[n.dy2] = two_of(v[n.dy])
     v[n.dy3] = last_of(v[n.dy])
     n2_group = in_order([v[n.n2], v[n.n21], v[n.n22], v[n.n23]])

time: 708 us -> 706 us (level)
  waiting for transfers between devices: 295 us -> 287 us
    all_gather x2, waiting for transfers between devices: 11.8 us -> 0.01 us  [gather_halves(): return lax.all_gather(both, ('y', 'c'), axis=0, tiled=True)]
    all_gather x1, waiting for transfers between devices: 0.47 us -> 8.15 us  [gather_halves(): lax.all_gather(both, ('y', 'c'), axis=1, tiled=True)]
    unnamed x254 -> x256, local copies, waits for them, and re-layouts: 48.6 us -> 50.4 us
  transfers between devices with their start and end apart: 91 -> 91, of which waited for: 39 -> 38; matrix products, arithmetic and copies ran while one was open for 20% -> 21% of each run, Pallas kernels for 6% -> 6%
where the time goes in v5:
time: 706 us; the launch traced here: 695 us
  waiting for transfers between devices  287 us (41%)
  starting transfers between devices  128 us (18%)
  matrix products  89.3 us (13%)
  local copies, waits for them, and re-layouts  78 us (11%)
  other arithmetic  56.2 us (8%)
  Pallas kernels  40 us (6%)
  between operations  17 us (2%)
    ppermute x45, waiting for transfers between devices, across(): return lax.ppermute(value, group, [(i, i ^ mask) for i in range(4)])  135 us
    ppermute x34, waiting for transfers between devices, swap(): return lax.ppermute(value, axis, [(0, 1), (1, 0)])  75.2 us
    ppermute x45, starting transfers between devices, across(): return lax.ppermute(value, group, [(i, i ^ mask) for i in range(4)])  59.6 us
    ppermute x34, starting transfers between devices, swap(): return lax.ppermute(value, axis, [(0, 1), (1, 0)])  51.5 us
    unnamed x256, local copies, waits for them, and re-layouts  50.4 us
    dot_general x5, matrix products, mm(): return jnp.dot(left, right, preferred_element_type=f32).astype(out)  34.3 us
    pallas_call x4, Pallas kernels, call(): pl.pallas_call(kernel, grid_spec=pltpu.PrefetchScalarGridSpec(num_scalar_...  31.2 us
    dot_general x5, matrix products, dot_tn(): lax.dot_general(a, b, (((0,), (0,)), ((), ())), preferred_element_type=f32)  29.8 us
  transfers between devices with their start and end apart: 91, of which 38 were waited for; matrix products, arithmetic and copies ran while one was open for 21% of the time, Pallas kernels for 6%

profile of v5, /device:TPU:8, one launch (start us, length us, event | category | flops | bytes accessed | tf_op | source)
XLA Modules:
  0.0 694.8 jit_solution(10498458625870130540)
XLA Ops:
  22.1 7.3 %collective-permute-done.8 = bf16[2,8,128]{2,1,0:T(8,128)(2,1)S(1)} collective-permute-done((bf16[2,8,128]{2,1,0:T(8,128)(2,1)S(1)}, bf16[2,8,128]{2,1,0:T(8,128)(2,1)S(1)}, u32[]{:S(2)}, u32[]{:S(2)}) %collective-permute-start.8) | collective-permute-done | bytes 4128 | tf_op jit(solution)/shard_map/ppermute | solution.py:36
  41.4 21.2 %collective-permute-done.6.refs_0_ = bf16[64,2048]{1,0:T(8,128)(2,1)S(1)} collective-permute-done((bf16[64,2048]{1,0:T(8,128)(2,1)S(1)}, bf16[64,2048]{1,0:T(8,128)(2,1)S(1)}, u32[]{:S(2)}, u32[]{:S(2)}) %collective-permute-start.6) | collective-permute-done | bytes 262176 | tf_op jit(solution)/shard_map/ppermute | solution.py:645
  65.2 7.3 %collective-permute-done.3.refs_4_ = bf16[256,1664]{1,0:T(8,128)(2,1)S(1)} collective-permute-done((bf16[256,1664]{1,0:T(8,128)(2,1)S(1)}, bf16[256,1664]{1,0:T(8,128)(2,1)S(1)}, u32[]{:S(2)}, u32[]{:S(2)}) %collective-permute-start.3) | collective-permute-done | bytes 852000 | tf_op jit(solution)/shard_map/ppermute | solution.py:36
  103.4 8.1 %collective-permute-done.15.refs_2_ = bf16[128,2048]{1,0:T(8,128)(2,1)S(1)} collective-permute-done((bf16[128,2048]{1,0:T(8,128)(2,1)S(1)}, bf16[128,2048]{1,0:T(8,128)(2,1)S(1)}, u32[]{:S(2)}, u32[]{:S(2)}) %collective-permute-start.15) | collective-permute-done | bytes 524320 | tf_op jit(solution)/shard_map/ppermute | solution.py:40
  144.5 7.5 %shard_map.222 = (f32[512,256]{1,0:T(8,128)S(1)}, f32[512,256]{1,0:T(8,128)S(1)}, bf16[8,512,256]{2,1,0:T(8,128)(2,1)S(1)}, f32[8,1,256]{2,1,0:T(1,128)S(1)}, bf...) custom-call(s32[1]{0:T(128)} %bitcast.1.place, f32[512,1664]{1,0:T(8,128)} %fusion.25.proj, bf16[128,256]{1,0:T(8,128)(2,1)S(1)} %pad.33.up, ...), custom_call_target="tpu_custom_call" | custom-call | flops 134217728 | bytes 7014400 | tf_op jit(solution)/shard_map/pallas_call | solution.py:503
  158.6 11.4 %collective-permute-done.29.entering = bf16[512,256]{1,0:T(8,128)(2,1)S(1)} collective-permute-done((bf16[512,256]{1,0:T(8,128)(2,1)S(1)}, bf16[512,256]{1,0:T(8,128)(2,1)S(1)}, u32[]{:S(2)}, u32[]{:S(2)}) %collective-permute-start.29) | collective-permute-done | bytes 262176 | tf_op jit(solution)/shard_map/ppermute | solution.py:555
  181.8 6.8 shard_map.224
  194.4 12.5 %collective-permute-done.32 = bf16[176,2048]{1,0:T(8,128)(2,1)} collective-permute-done((bf16[176,2048]{1,0:T(8,128)(2,1)}, bf16[176,2048]{1,0:T(8,128)(2,1)}, u32[]{:S(2)}, u32[]{:S(2)}) %collective-permute-start.32) | collective-permute-done | bytes 720928 | tf_op jit(solution)/shard_map/ppermute | solution.py:725
  206.9 10.2 %collective-permute-done.31 = bf16[128,2048]{1,0:T(8,128)(2,1)} collective-permute-done((bf16[128,2048]{1,0:T(8,128)(2,1)S(1)}, bf16[128,2048]{1,0:T(8,128)(2,1)}, u32[]{:S(2)}, u32[]{:S(2)}) %collective-permute-start.31) | collective-permute-done | bytes 524320 | tf_op jit(solution)/shard_map/ppermute | solution.py:40
  227.4 18.0 %collective-permute-done.35 = bf16[128,2048]{1,0:T(8,128)(2,1)} collective-permute-done((bf16[128,2048]{1,0:T(8,128)(2,1)}, bf16[128,2048]{1,0:T(8,128)(2,1)}, u32[]{:S(2)}, u32[]{:S(2)}) %collective-permute-start.35) | collective-permute-done | bytes 524320 | tf_op jit(solution)/shard_map/ppermute | solution.py:40
  267.3 7.0 %collective-permute-start.39 = (bf16[128,2048]{1,0:T(8,128)(2,1)}, bf16[128,2048]{1,0:T(8,128)(2,1)S(1)}, u32[]{:S(2)}, u32[]{:S(2)}) collective-permute-start(bf16[128,2048]{1,0:T(8,128)(2,1)} %copy-done.13), channel_id=1, source_target_pairs={{0,3},{1,2},{2,1},{3,0},{4,7},{5,6},{6,5},{7,4},{8,11},{9,10},{10,... | collective-permute-start | bytes 1572872 | tf_op jit(solution)/shard_map/ppermute | solution.py:40
  274.3 11.5 %collective-permute-done.39.refs_3_ = bf16[128,2048]{1,0:T(8,128)(2,1)S(1)} collective-permute-done((bf16[128,2048]{1,0:T(8,128)(2,1)}, bf16[128,2048]{1,0:T(8,128)(2,1)S(1)}, u32[]{:S(2)}, u32[]{:S(2)}) %collective-permute-start.39) | collective-permute-done | bytes 524320 | tf_op jit(solution)/shard_map/ppermute | solution.py:40
  295.0 8.4 %fusion.76 = f32[512,1408]{1,0:T(8,128)} fusion(bf16[512,2048]{1,0:T(8,128)(2,1)S(1)} %shard_map.226, bf16[2048,1408]{1,0:T(8,128)(2,1)} %all-gather.4.cloned.1.call-done), kind=kOutput, calls=%fused_computation.274 | convolution fusion | flops 2952790016 | bytes 10747904 | tf_op jit(solution)/shard_map/dot_general | solution.py:537
  303.5 7.0 %collective-permute-done.41.refs_2_ = bf16[128,2048]{1,0:T(8,128)(2,1)S(1)} collective-permute-done((bf16[128,2048]{1,0:T(8,128)(2,1)}, bf16[128,2048]{1,0:T(8,128)(2,1)S(1)}, u32[]{:S(2)}, u32[]{:S(2)}) %collective-permute-start.41) | collective-permute-done | bytes 524320 | tf_op jit(solution)/shard_map/ppermute | solution.py:40
  313.5 8.2 %all-gather.8.cloned.1.call-done = bf16[2,704,2048]{2,1,0:T(8,128)(2,1)} async-done(((bf16[2,176,2048]{2,1,0:T(8,128)(2,1)}), bf16[2,704,2048]{2,1,0:T(8,128)(2,1)}) %all-gather.8.cloned.1.call-update) | async-done | bytes 5767184 | tf_op jit(solution)/shard_map/all_gather | solution.py:241
  328.3 8.0 %multiply_convert_fusion = (bf16[512,1408]{1,0:T(8,128)(2,1)}, bf16[512,1408]{1,0:T(8,128)(2,1)S(1)}, bf16[512,1408]{1,0:T(8,128)(2,1)S(1)}) fusion(f32[512,1408]{1,0:T(8,128)S(1)} %copy-done.108, f32[512,1408]{1,0:T(8,128)S(1)} %fusion.75, bf16[512,2048]{1,0:T(8,128)(2,1)S(1)} %copy-done.18, bf16[2048,1408]{1,0:T(8,128)(2,1)} %all-gather.6.cloned.1.call-done), kind=kOutput, calls=%fused_computation.13 | convolution fusion | flops 2964324352 | bytes 17956864 | tf_op jit(solution)/shard_map/dot_general | solution.py:537
  353.2 7.1 %collective-permute-done.43 = bf16[128,2048]{1,0:T(8,128)(2,1)} collective-permute-done((bf16[128,2048]{1,0:T(8,128)(2,1)}, bf16[128,2048]{1,0:T(8,128)(2,1)}, u32[]{:S(2)}, u32[]{:S(2)}) %collective-permute-start.43) | collective-permute-done | bytes 524320 | tf_op jit(solution)/shard_map/ppermute | solution.py:40
  362.4 8.9 %convolution_convert_fusion.1 = bf16[2048,1408]{1,0:T(8,128)(2,1)} fusion(bf16[512,2048]{1,0:T(8,128)(2,1)} %copy-done.17, bf16[512,1408]{1,0:T(8,128)(2,1)} %copy-done.107), kind=kOutput, calls=%fused_computation.2 | convolution fusion | flops 2955673600 | bytes 9306112 | tf_op jit(solution)/shard_map/dot_general | solution.py:290
  395.1 11.2 %collective-permute-done.48.refs_3_ = bf16[128,2048]{1,0:T(8,128)(2,1)} collective-permute-done((bf16[128,2048]{1,0:T(8,128)(2,1)}, bf16[128,2048]{1,0:T(8,128)(2,1)}, u32[]{:S(2)}, u32[]{:S(2)}) %collective-permute-start.48) | collective-permute-done | bytes 524320 | tf_op jit(solution)/shard_map/ppermute | solution.py:40
  413.2 7.5 %shard_map.228 = (bf16[512,512]{1,0:T(8,128)(2,1)S(1)}, bf16[512,512]{1,0:T(8,128)(2,1)S(1)}, bf16[8,512,256]{2,1,0:T(8,128)(2,1)}, f32[8,1,256]{2,1,0:T(1,128)S...) custom-call(s32[1]{0:T(128)} %bitcast.1.place, f32[512,512]{1,0:T(8,128)S(1)} %fusion.78.grad_gated, ...), custom_call_target="tpu_custom_call" | custom-call | flops 134217728 | bytes 12128256 | tf_op jit(solution)/shard_map/pallas_call | solution.py:503
  429.1 8.9 %fusion.74 = (bf16[512,2048]{1,0:T(8,128)(2,1)S(1)}, f32[512,2048]{1,0:T(8,128)}) fusion(bf16[512,1408]{1,0:T(8,128)(2,1)} %get-tuple-element.245, bf16[1408,2048]{1,0:T(8,128)(2,1)} %bitcast.243), kind=kOutput, calls=%fused_computation.272 | convolution fusion | flops 2953838592 | bytes 13500416 | tf_op jit(solution)/shard_map/dot_general | solution.py:537
  449.0 9.3 %shard_map.229 = (bf16[512,1664]{1,0:T(8,128)(2,1)S(1)}, f32[128,256]{1,0:T(8,128)S(1)}, f32[1,256]{1,0:T(1,128)S(1)}) custom-call(s32[1]{0:T(128)} %bitcast.1.place, f32[512,1664]{1,0:T(8,128)} %fusion.25.proj, f32[512,256]{1,0:T(8,128)S(1)} %get-tuple-element.181.sums, f32[512,256]{1,0:T(8,128)S(1)} %copy-done.55, bf16[512,512]{1,0:T(8,128)(2,1)S(1)} %copy-done.57, ...), custom_call_target="tpu_custom_call" | custom-call | flops 520093696 | bytes 20676608 | tf_op jit(solution)/shard_map/pallas_call | solution.py:503
  467.2 8.9 %fusion.3 = (f32[2048]{0:T(1024)S(1)}, bf16[512,2048]{1,0:T(8,128)(2,1)}, f32[512,2048]{1,0:T(8,128)}) fusion(bf16[512,2048]{1,0:T(8,128)(2,1)S(1)} %shard_map.220, f32[512]{0:T(512)S(1)} %copy-done.103, bf16[512,1664]{1,0:T(8,128)(2,1)S(1)} %copy-done.71, bf16[2048,1664]{1,0:T(8,128)(2,1)} %copy-done.6), kind=kOutput, calls=%fused_computation.9 | convolution fusion | flops 3494901760 | bytes 16918528 | tf_op jit(solution)/shard_map/dot_general | solution.py:286
  486.8 8.2 %collective-permute-done.58 = bf16[256,1408]{1,0:T(8,128)(2,1)} collective-permute-done((bf16[256,1408]{1,0:T(8,128)(2,1)}, bf16[256,1408]{1,0:T(8,128)(2,1)}, u32[]{:S(2)}, u32[]{:S(2)}) %collective-permute-start.58) | collective-permute-done | bytes 720928 | tf_op jit(solution)/shard_map/ppermute | solution.py:36
  497.4 8.1 %add_convert_fusion = bf16[2048,1664]{1,0:T(8,128)(2,1)} fusion(f32[2048,12]{1,0:T(8,128)} %copy.49, bf16[512,1664]{1,0:T(8,128)(2,1)} %copy-done.70, bf16[512,2048]{1,0:T(8,128)(2,1)S(1)} %shard_map.220, f32[2048]{0:T(1024)S(1)} %reshape.628, f32[512]{0:T(512)S(1)} %copy-done.104), kind=kOutput, calls=%fused_computation | convolution fusion | flops 3500670976 | bytes 10725376 | tf_op jit(solution)/shard_map/dot_general | solution.py:290
  521.2 9.3 %reduce-scatter.8.cloned.1.call-done = bf16[2,176,2048]{2,1,0:T(8,128)(2,1)} async-done(((bf16[2,704,2048]{2,1,0:T(8,128)(2,1)}), bf16[2,176,2048]{2,1,0:T(8,128)(2,1)}) %reduce-scatter.8.cloned.1.call-update) | async-done | bytes 1441808 | tf_op jit(solution)/shard_map/reduce_scatter | solution.py:250
  530.5 6.8 collective-permute-done.61
  562.1 8.1 %collective-permute-done.60 = bf16[256,1664]{1,0:T(8,128)(2,1)S(1)} collective-permute-done((bf16[256,1664]{1,0:T(8,128)(2,1)S(1)}, bf16[256,1664]{1,0:T(8,128)(2,1)S(1)}, u32[]{:S(2)}, u32[]{:S(2)}) %collective-permute-start.60) | collective-permute-done | bytes 852000 | tf_op jit(solution)/shard_map/ppermute | solution.py:36
  591.3 9.2 %collective-permute-done.81 = bf16[64,1408]{1,0:T(8,128)(2,1)S(1)} collective-permute-done((bf16[64,1408]{1,0:T(8,128)(2,1)S(1)}, bf16[64,1408]{1,0:T(8,128)(2,1)S(1)}, u32[]{:S(2)}, u32[]{:S(2)}) %collective-permute-start.81) | collective-permute-done | bytes 180256 | tf_op jit(solution)/shard_map/ppermute | solution.py:40
  607.7 13.6 %collective-permute-done.67 = bf16[256,1664]{1,0:T(8,128)(2,1)S(1)} collective-permute-done((bf16[256,1664]{1,0:T(8,128)(2,1)S(1)}, bf16[256,1664]{1,0:T(8,128)(2,1)S(1)}, u32[]{:S(2)}, u32[]{:S(2)}) %collective-permute-start.67) | collective-permute-done | bytes 852000 | tf_op jit(solution)/shard_map/ppermute | solution.py:36
  621.3 22.6 %collective-permute-done.66 = bf16[256,1664]{1,0:T(8,128)(2,1)S(1)} collective-permute-done((bf16[256,1664]{1,0:T(8,128)(2,1)S(1)}, bf16[256,1664]{1,0:T(8,128)(2,1)S(1)}, u32[]{:S(2)}, u32[]{:S(2)}) %collective-permute-start.66) | collective-permute-done | bytes 852000 | tf_op jit(solution)/shard_map/ppermute | solution.py:36
  672.7 13.5 %collective-permute-done.83 = bf16[176,2048]{1,0:T(8,128)(2,1)S(1)} collective-permute-done((bf16[176,2048]{1,0:T(8,128)(2,1)S(1)}, bf16[176,2048]{1,0:T(8,128)(2,1)S(1)}, u32[]{:S(2)}, u32[]{:S(2)}) %collective-permute-start.83) | collective-permute-done | bytes 720928 | tf_op jit(solution)/shard_map/ppermute | solution.py:903
  (584 shorter events, 356.2 us)
Async XLA Ops:
  7.2 279.4 %all-gather.4.cloned.1.call-start = ((), (), s32[]{:S(2)}) async-start(), calls=%async_computation.3 | async-start | bytes 7208960 | tf_op jit(solution)/shard_map/all_gather | solution.py:239
  32.5 30.1 %collective-permute-start.5 = (bf16[256,1664]{1,0:T(8,128)(2,1)S(1)}, bf16[256,1664]{1,0:T(8,128)(2,1)S(1)}, u32[]{:S(2)}, u32[]{:S(2)}) collective-permute-start(bf16[256,1664]{1,0:T(8,128)(2,1)S(1)} %pad_maximum_fusion.1.refs_0_), channel_id=1, source_target_pairs={{0,8},{8,0},{1,9},{9,1},{2,10},{10,2},{3,11},{11,3},{4,12},{12,4},... | collective-permute-start | bytes 2555912 | tf_op jit(solution)/shard_map/ppermute | solution.py:36
  32.6 32.5 %collective-permute-start.4 = (bf16[256,1664]{1,0:T(8,128)(2,1)S(1)}, bf16[256,1664]{1,0:T(8,128)(2,1)S(1)}, u32[]{:S(2)}, u32[]{:S(2)}) collective-permute-start(bf16[256,1664]{1,0:T(8,128)(2,1)S(1)} %pad_maximum_fusion.1.refs_0_), channel_id=1, source_target_pairs={{0,16},{16,0},{1,17},{17,1},{2,18},{18,2},{3,19},{19,3},{4,20},{20... | collective-permute-start | bytes 2555912 | tf_op jit(solution)/shard_map/ppermute | solution.py:36
  33.2 39.3 %collective-permute-start.3 = (bf16[256,1664]{1,0:T(8,128)(2,1)S(1)}, bf16[256,1664]{1,0:T(8,128)(2,1)S(1)}, u32[]{:S(2)}, u32[]{:S(2)}) collective-permute-start(bf16[256,1664]{1,0:T(8,128)(2,1)S(1)} %pad_maximum_fusion.1.refs_0_), channel_id=1, source_target_pairs={{0,4},{4,0},{1,5},{5,1},{2,6},{6,2},{3,7},{7,3},{8,12},{12,8},{9,1... | collective-permute-start | bytes 2555912 | tf_op jit(solution)/shard_map/ppermute | solution.py:36
  35.8 26.8 %collective-permute-start.6 = (bf16[64,2048]{1,0:T(8,128)(2,1)S(1)}, bf16[64,2048]{1,0:T(8,128)(2,1)S(1)}, u32[]{:S(2)}, u32[]{:S(2)}) collective-permute-start(bf16[64,2048]{1,0:T(8,128)(2,1)S(1)} %copy-done.105), channel_id=1, source_target_pairs={{0,0},{1,8},{2,16},{3,24},{4,4},{5,12},{6,20},{7,28},{8,1},{9,9},{... | collective-permute-start | bytes 786440 | tf_op jit(solution)/shard_map/ppermute | solution.py:645
  41.3 32.7 %collective-permute-start.21 = (bf16[64,2816]{1,0:T(8,128)(2,1)}, bf16[64,2816]{1,0:T(8,128)(2,1)}, u32[]{:S(2)}, u32[]{:S(2)}) collective-permute-start(bf16[64,2816]{1,0:T(8,128)(2,1)} %select_select_fusion.5), channel_id=1, source_target_pairs={{0,2},{1,3},{2,0},{3,1},{4,6},{5,7},{6,4},{7,5},{8,10},{9,11},{10,... | collective-permute-start | bytes 1081352 | tf_op jit(solution)/shard_map/ppermute | solution.py:40
  88.1 23.3 %collective-permute-start.15 = (bf16[128,2048]{1,0:T(8,128)(2,1)S(1)}, bf16[128,2048]{1,0:T(8,128)(2,1)S(1)}, u32[]{:S(2)}, u32[]{:S(2)}) collective-permute-start(bf16[128,2048]{1,0:T(8,128)(2,1)S(1)} %bitcast.197), channel_id=1, source_target_pairs={{0,2},{1,3},{2,0},{3,1},{4,6},{5,7},{6,4},{7,5},{8,10},{9,11},{10,... | collective-permute-start | bytes 1572872 | tf_op jit(solution)/shard_map/ppermute | solution.py:40
  124.5 34.1 %collective-permute-start.33 = (bf16[256,1408]{1,0:T(8,128)(2,1)}, bf16[256,1408]{1,0:T(8,128)(2,1)S(1)}, u32[]{:S(2)}, u32[]{:S(2)}) collective-permute-start(bf16[256,1408]{1,0:T(8,128)(2,1)} %get-tuple-element.209), channel_id=1, source_target_pairs={{0,4},{4,0},{1,5},{5,1},{2,6},{6,2},{3,7},{7,3},{8,12},{12,8},{9,1... | collective-permute-start | bytes 2162696 | tf_op jit(solution)/shard_map/ppermute | solution.py:36
  128.8 24.0 %collective-permute-start.28 = (bf16[64,2048]{1,0:T(8,128)(2,1)}, bf16[64,2048]{1,0:T(8,128)(2,1)S(1)}, u32[]{:S(2)}, u32[]{:S(2)}) collective-permute-start(bf16[64,2048]{1,0:T(8,128)(2,1)} %collective-permute-done.25.refs_5_), channel_id=1, source_target_pairs={{0,8},{8,0},{1,9},{9,1},{2,10},{10,2},{3,11},{11,3},{4,12},{12,4},... | collective-permute-start | bytes 786440 | tf_op jit(solution)/shard_map/ppermute | solution.py:36
  172.3 114.3 %all-gather.6.cloned.1.call-start = ((), (), s32[]{:S(2)}) async-start(), calls=%async_computation.4 | async-start | bytes 7208960 | tf_op jit(solution)/shard_map/all_gather | solution.py:239
  173.2 33.6 %collective-permute-start.32 = (bf16[176,2048]{1,0:T(8,128)(2,1)}, bf16[176,2048]{1,0:T(8,128)(2,1)}, u32[]{:S(2)}, u32[]{:S(2)}) collective-permute-start(bf16[176,2048]{1,0:T(8,128)(2,1)} %param.21), channel_id=1, source_target_pairs={{0,0},{1,8},{2,16},{3,24},{4,4},{5,12},{6,20},{7,28},{8,1},{9,9},{... | collective-permute-start | bytes 2162696 | tf_op jit(solution)/shard_map/ppermute | solution.py:725
  175.6 41.5 %collective-permute-start.34 = (bf16[256,1408]{1,0:T(8,128)(2,1)}, bf16[256,1408]{1,0:T(8,128)(2,1)S(1)}, u32[]{:S(2)}, u32[]{:S(2)}) collective-permute-start(bf16[256,1408]{1,0:T(8,128)(2,1)} %get-tuple-element.211), channel_id=1, source_target_pairs={{0,4},{4,0},{1,5},{5,1},{2,6},{6,2},{3,7},{7,3},{8,12},{12,8},{9,1... | collective-permute-start | bytes 2162696 | tf_op jit(solution)/shard_map/ppermute | solution.py:36
  194.3 22.8 %collective-permute-start.31 = (bf16[128,2048]{1,0:T(8,128)(2,1)S(1)}, bf16[128,2048]{1,0:T(8,128)(2,1)}, u32[]{:S(2)}, u32[]{:S(2)}) collective-permute-start(bf16[128,2048]{1,0:T(8,128)(2,1)S(1)} %get-tuple-element.194), channel_id=1, source_target_pairs={{0,2},{1,3},{2,0},{3,1},{4,6},{5,7},{6,4},{7,5},{8,10},{9,11},{10,... | collective-permute-start | bytes 1572872 | tf_op jit(solution)/shard_map/ppermute | solution.py:40
  218.8 102.8 %all-gather.8.cloned.1.call-start = ((), (), s32[]{:S(2)}) async-start(), calls=%async_computation.5 | async-start | bytes 7208960 | tf_op jit(solution)/shard_map/all_gather | solution.py:241
  218.8 26.5 %collective-permute-start.35 = (bf16[128,2048]{1,0:T(8,128)(2,1)}, bf16[128,2048]{1,0:T(8,128)(2,1)}, u32[]{:S(2)}, u32[]{:S(2)}) collective-permute-start(bf16[128,2048]{1,0:T(8,128)(2,1)} %get-tuple-element.202), channel_id=1, source_target_pairs={{0,3},{1,2},{2,1},{3,0},{4,7},{5,6},{6,5},{7,4},{8,11},{9,10},{10,... | collective-permute-start | bytes 1572872 | tf_op jit(solution)/shard_map/ppermute | solution.py:40
  223.0 34.4 %collective-permute-start.38 = (bf16[176,2048]{1,0:T(8,128)(2,1)}, bf16[176,2048]{1,0:T(8,128)(2,1)S(1)}, u32[]{:S(2)}, u32[]{:S(2)}) collective-permute-start(bf16[176,2048]{1,0:T(8,128)(2,1)} %collective-permute-done.32), channel_id=1, source_target_pairs={{0,4},{4,0},{1,5},{5,1},{2,6},{6,2},{3,7},{7,3},{8,12},{12,8},{9,1... | collective-permute-start | bytes 2162696 | tf_op jit(solution)/shard_map/ppermute | solution.py:36
  267.2 176.8 %reduce-scatter.4.cloned.1.call-start = ((), (), s32[]{:S(2)}) async-start(), calls=%async_computation.6 | async-start | bytes 7208960 | tf_op jit(solution)/shard_map/reduce_scatter | solution.py:251
  289.2 22.1 %collective-permute-start.40 = (bf16[128,2048]{1,0:T(8,128)(2,1)}, bf16[128,2048]{1,0:T(8,128)(2,1)S(1)}, u32[]{:S(2)}, u32[]{:S(2)}) collective-permute-start(bf16[128,2048]{1,0:T(8,128)(2,1)} %bitcast.202), channel_id=1, source_target_pairs={{0,1},{1,0},{2,3},{3,2},{4,5},{5,4},{6,7},{7,6},{8,9},{9,8},{10,11... | collective-permute-start | bytes 1572872 | tf_op jit(solution)/shard_map/ppermute | solution.py:40
  361.6 118.4 %reduce-scatter.6.cloned.1.call-start = ((), (), s32[]{:S(2)}) async-start(), calls=%async_computation.7 | async-start | bytes 7208960 | tf_op jit(solution)/shard_map/reduce_scatter | solution.py:251
  376.0 154.4 %reduce-scatter.8.cloned.1.call-start = ((), (), s32[]{:S(2)}) async-start(), calls=%async_computation.8 | async-start | bytes 7208960 | tf_op jit(solution)/shard_map/reduce_scatter | solution.py:250
  463.9 31.1 %collective-permute-start.58 = (bf16[256,1408]{1,0:T(8,128)(2,1)}, bf16[256,1408]{1,0:T(8,128)(2,1)}, u32[]{:S(2)}, u32[]{:S(2)}) collective-permute-start(bf16[256,1408]{1,0:T(8,128)(2,1)} %dynamic-slice_bitcast_fusion.2), channel_id=1, source_target_pairs={{0,4},{4,0},{1,5},{5,1},{2,6},{6,2},{3,7},{7,3},{8,12},{12,8},{9,1... | collective-permute-start | bytes 2162696 | tf_op jit(solution)/shard_map/ppermute | solution.py:36
  481.8 23.7 %collective-permute-start.56 = (bf16[64,2048]{1,0:T(8,128)(2,1)S(1)}, bf16[64,2048]{1,0:T(8,128)(2,1)S(1)}, u32[]{:S(2)}, u32[]{:S(2)}) collective-permute-start(bf16[64,2048]{1,0:T(8,128)(2,1)S(1)} %get-tuple-element.337), channel_id=1, source_target_pairs={{0,16},{16,0},{1,17},{17,1},{2,18},{18,2},{3,19},{19,3},{4,20},{20... | collective-permute-start | bytes 786440 | tf_op jit(solution)/shard_map/ppermute | solution.py:36
  482.9 22.5 %collective-permute-start.55 = (bf16[64,2048]{1,0:T(8,128)(2,1)S(1)}, bf16[64,2048]{1,0:T(8,128)(2,1)S(1)}, u32[]{:S(2)}, u32[]{:S(2)}) collective-permute-start(bf16[64,2048]{1,0:T(8,128)(2,1)S(1)} %get-tuple-element.338), channel_id=1, source_target_pairs={{0,16},{16,0},{1,17},{17,1},{2,18},{18,2},{3,19},{19,3},{4,20},{20... | collective-permute-start | bytes 786440 | tf_op jit(solution)/shard_map/ppermute | solution.py:36
  486.0 24.4 %collective-permute-start.53 = (bf16[128,2048]{1,0:T(8,128)(2,1)}, bf16[128,2048]{1,0:T(8,128)(2,1)S(1)}, u32[]{:S(2)}, u32[]{:S(2)}) collective-permute-start(bf16[128,2048]{1,0:T(8,128)(2,1)} %get-tuple-element.260), channel_id=1, source_target_pairs={{0,1},{1,0},{2,3},{3,2},{4,5},{5,4},{6,7},{7,6},{8,9},{9,8},{10,11... | collective-permute-start | bytes 1572872 | tf_op jit(solution)/shard_map/ppermute | solution.py:40
  514.5 33.2 %collective-permute-start.59 = (bf16[2048,1664]{1,0:T(8,128)(2,1)}, bf16[2048,1664]{1,0:T(8,128)(2,1)}, u32[]{:S(2)}, u32[]{:S(2)}) collective-permute-start(bf16[2048,1664]{1,0:T(8,128)(2,1)} %add_convert_fusion), channel_id=1, source_target_pairs={{0,8},{8,0},{1,9},{9,1},{2,10},{10,2},{3,11},{11,3},{4,12},{12,4},... | collective-permute-start | bytes 20447240 | tf_op jit(solution)/shard_map/ppermute | solution.py:36
  514.5 22.8 %collective-permute-start.61 = (bf16[128,2048]{1,0:T(8,128)(2,1)}, bf16[128,2048]{1,0:T(8,128)(2,1)S(1)}, u32[]{:S(2)}, u32[]{:S(2)}) collective-permute-start(bf16[128,2048]{1,0:T(8,128)(2,1)} %get-tuple-element.274), channel_id=1, source_target_pairs={{0,3},{1,2},{2,1},{3,0},{4,7},{5,6},{6,5},{7,4},{8,11},{9,10},{10,... | collective-permute-start | bytes 1572872 | tf_op jit(solution)/shard_map/ppermute | solution.py:40
  520.8 41.3 %collective-permute-start.65 = (bf16[256,1408]{1,0:T(8,128)(2,1)S(1)}, bf16[256,1408]{1,0:T(8,128)(2,1)S(1)}, u32[]{:S(2)}, u32[]{:S(2)}) collective-permute-start(bf16[256,1408]{1,0:T(8,128)(2,1)S(1)} %dynamic-slice_bitcast_fusion.1), channel_id=1, source_target_pairs={{0,4},{4,0},{1,5},{5,1},{2,6},{6,2},{3,7},{7,3},{8,12},{12,8},{9,1... | collective-permute-start | bytes 2162696 | tf_op jit(solution)/shard_map/ppermute | solution.py:36
  554.2 53.4 %collective-permute-start.68 = (bf16[64,2048]{1,0:T(8,128)(2,1)S(1)}, bf16[64,2048]{1,0:T(8,128)(2,1)S(1)}, u32[]{:S(2)}, u32[]{:S(2)}) collective-permute-start(bf16[64,2048]{1,0:T(8,128)(2,1)S(1)} %add_convert_fusion.5), channel_id=1, source_target_pairs={{0,4},{4,0},{1,5},{5,1},{2,6},{6,2},{3,7},{7,3},{8,12},{12,8},{9,1... | collective-permute-start | bytes 786440 | tf_op jit(solution)/shard_map/ppermute | solution.py:36
  557.9 49.8 %collective-permute-start.75 = (bf16[176,2048]{1,0:T(8,128)(2,1)S(1)}, bf16[176,2048]{1,0:T(8,128)(2,1)S(1)}, u32[]{:S(2)}, u32[]{:S(2)}) collective-permute-start(bf16[176,2048]{1,0:T(8,128)(2,1)S(1)} %dynamic-slice_bitcast_fusion), channel_id=1, source_target_pairs={{0,4},{4,0},{1,5},{5,1},{2,6},{6,2},{3,7},{7,3},{8,12},{12,8},{9,1... | collective-permute-start | bytes 2162696 | tf_op jit(solution)/shard_map/ppermute | solution.py:36
  604.3 39.6 %collective-permute-start.66 = (bf16[256,1664]{1,0:T(8,128)(2,1)S(1)}, bf16[256,1664]{1,0:T(8,128)(2,1)S(1)}, u32[]{:S(2)}, u32[]{:S(2)}) collective-permute-start(bf16[256,1664]{1,0:T(8,128)(2,1)S(1)} %add_convert_fusion.2), channel_id=1, source_target_pairs={{0,4},{4,0},{1,5},{5,1},{2,6},{6,2},{3,7},{7,3},{8,12},{12,8},{9,1... | collective-permute-start | bytes 2555912 | tf_op jit(solution)/shard_map/ppermute | solution.py:36
  649.5 22.4 %collective-permute-start.79 = (bf16[64,2048]{1,0:T(8,128)(2,1)}, bf16[64,2048]{1,0:T(8,128)(2,1)S(1)}, u32[]{:S(2)}, u32[]{:S(2)}) collective-permute-start(bf16[64,2048]{1,0:T(8,128)(2,1)} %add_convert_fusion.4), channel_id=1, source_target_pairs={{0,0},{8,1},{16,2},{24,3},{4,4},{12,5},{20,6},{28,7},{1,8},{9,9},{... | collective-permute-start | bytes 786440 | tf_op jit(solution)/shard_map/ppermute | solution.py:904
  656.8 29.4 %collective-permute-start.83 = (bf16[176,2048]{1,0:T(8,128)(2,1)S(1)}, bf16[176,2048]{1,0:T(8,128)(2,1)S(1)}, u32[]{:S(2)}, u32[]{:S(2)}) collective-permute-start(bf16[176,2048]{1,0:T(8,128)(2,1)S(1)} %fusion.5), channel_id=1, source_target_pairs={{0,0},{8,1},{16,2},{24,3},{4,4},{12,5},{20,6},{28,7},{1,8},{9,9},{... | collective-permute-start | bytes 2162696 | tf_op jit(solution)/shard_map/ppermute | solution.py:903
  (172 other events, 1700.0 us)
Sparse Core Ops, SparseCore 0:
  172.4 55.1 all-gather.3
  229.8 46.1 all-gather.5
  278.2 43.3 all-gather.7
  361.7 53.9 reduce-scatter.3
  418.3 54.8 reduce-scatter.5
  475.6 54.8 reduce-scatter.7
